TPU v7x, 32 devices: a whole 2x2x4 slice. The times are simulated.
32 devices in a mesh: seg: 8 (over z, x), lag: 4 (over y, core).
Axes of the slice: x: 2, y: 2, z: 4, core: 2. Of those that a mesh axis runs over, the one named last changes fastest.
Arguments:
- actuator_input: bfloat16 [24576, 256], P('seg'), may hold values from -6 to 6
- sensor_output: bfloat16 [24576, 2048], P('seg', 'lag'), may hold values from -6 to 6
- run_lengths: int32 [4], replicated, may hold values from 1 to 12288, 24576 in all
- lag_offsets: int32 [2], replicated, may hold values from 0 to 1022, as said below
Outputs:
- markov: float32 [256, 4, 2048], P('seg', 'lag')
Inputs may be any that keep to these rules, and one draw needn't show every extreme that they name: `run_lengths`: the 4 lengths add up to 24576; at least one equals 12288. `lag_offsets`: at least one block starts at 1022.
All inputs are finite; a program needn't handle non-finite values.
Results may differ from a plain program's by a relative error of at most 0.0003.
Values may be sent and summed in bfloat16 or wider, within the bound.
No kernel may reach another device: no remote copies, remote signals or barrier semaphores. Data moves between devices by JAX's collectives and lax.ppermute only.
A program may use at most 64 MiB of HBM per device.

v0:
```python
import math

import jax
import jax.numpy as jnp
from jax import lax
from jax.sharding import PartitionSpec as P

LMAX = 1024
LBW = 2
NBLK = 2


def shifted_2(value, axis, steps):
    count = lax.axis_size(axis)
    initial, last = (max(0, -steps), min(count, count - steps))
    return lax.ppermute(value, axis, [(source, source + steps) for source in range(initial, last)])


def segment_ids(run_lengths, start_row, row_count):
    run_ends = jnp.cumsum(run_lengths)
    places = start_row + jnp.arange(row_count, dtype=jnp.int32)
    return jnp.sum((run_ends[None, :] <= places[:, None]).astype(jnp.int32), axis=1)


def product_over_time(masked, shifted):
    return lax.dot_general(
        masked, shifted, (((0,), (0,)), ((), ())), preferred_element_type=jnp.float32
    )


def per_device(actuator_input, sensor_output, run_lengths, lag_offsets):
    samples = actuator_input.shape[0]
    devices_seg = lax.axis_size("seg")
    scaling = 1.0 / math.sqrt(samples * devices_seg)
    start_row = lax.axis_index("seg") * samples
    halo_rows = shifted_2(sensor_output[:LMAX], "seg", -1)
    idents = segment_ids(run_lengths, start_row, samples + LMAX)
    own_ids = idents[:samples]
    shifts = [lag_offsets[blk_num] + lag_step for blk_num in range(NBLK) for lag_step in range(LBW)]
    joined = jnp.concatenate([sensor_output, halo_rows], axis=0)

    def lag_term(columns, lag_value):
        shifted = lax.dynamic_slice_in_dim(joined, lag_value, samples, 0)
        shifted_ids = lax.dynamic_slice_in_dim(idents, lag_value, samples, 0)
        masked = jnp.where((own_ids == shifted_ids)[:, None], columns, jnp.zeros_like(columns))
        return product_over_time(masked, shifted)

    columns = actuator_input
    shares = lax.psum_scatter(
        jnp.stack([lag_term(columns, lag_value) for lag_value in shifts], axis=1),
        "seg",
        scatter_dimension=0,
        tiled=True,
    )
    result_rows = lax.all_to_all(shares, "lag", split_axis=1, concat_axis=2, tiled=True)
    return result_rows * scaling


def solution(mesh):
    return jax.shard_map(
        per_device,
        mesh=mesh,
        in_specs=(P("seg", None), P("seg", "lag"), P(), P()),
        out_specs=P("seg", "lag", None),
        check_vma=False,
    )
```

profile of v0, /device:TPU:0, one launch (start us, length us, event | category | flops | bytes accessed | tf_op | source)
XLA Modules:
  0.0 133.4 jit_solution(10965768090712506814)
XLA Ops:
  6.5 0.0 copy-start
  6.5 0.0 copy-start.2
  6.5 0.0 reduce-scatter.2.cloned.1.call-start
  6.5 1.3 slice.16
  7.9 1.3 collective-permute-start
  9.2 0.0 copy-done
  9.2 0.6 fusion.48
  14.6 0.0 copy-done.2
  14.6 0.2 reduce-window.8
  16.0 0.1 convert_reduce_fusion
  16.1 0.1 dynamic-slice_compare_fusion.3
  16.2 2.1 %constant_dynamic-update-slice_fusion.1 = bf16[4096,512]{1,0:T(8,128)(2,1)S(1)} fusion(bf16[3072,512]{1,0:T(8,128)(2,1)} %param.5), kind=kLoop, calls=%fused_computation.33 | loop fusion | bytes 6291456
  18.3 0.0 copy-start.1
  18.3 17.5 %collective-permute-done = bf16[1024,512]{1,0:T(8,128)(2,1)S(1)} collective-permute-done((bf16[1024,512]{1,0:T(8,128)(2,1)S(1)}, bf16[1024,512]{1,0:T(8,128)(2,1)S(1)}, u32[]{:S(2)}, u32[]{:S(2)}) %collective-permute-start) | collective-permute-done | bytes 1048608 | tf_op jit(solution)/shard_map/ppermute | solution.py:16
  35.9 0.1 constant_dynamic-update-slice_fusion
  36.0 0.0 copy-done.1
  36.0 2.0 %fusion.31 = f32[256,1,512]{2,0,1:T(8,128)S(1)} fusion(bf16[4096,512]{1,0:T(8,128)(2,1)S(1)} %constant_dynamic-update-slice_fusion, s32[]{:T(128)S(6)} %select_n.35, bf16[3072,256]{1,0:T(8,128)(2,1)S(1)} %copy-done.1, pred[3072]{0:T(1024)(128)(4,1)S(1)} %get-tuple-element.8), kind=kOutput, calls=%fused_computation.20 | convolution fusion | flops 806092800 | bytes 5245956 | tf_op jit(solution)/shard_map/dot_general | solution.py:26
  38.0 2.0 %fusion.26 = f32[256,1,512]{2,0,1:T(8,128)S(1)} fusion(bf16[4096,512]{1,0:T(8,128)(2,1)S(1)} %constant_dynamic-update-slice_fusion, s32[]{:T(128)S(6)} %select_n.33, bf16[3072,256]{1,0:T(8,128)(2,1)S(1)} %copy-done.1, pred[3072]{0:T(1024)(128)(4,1)S(1)} %get-tuple-element.6), kind=kOutput, calls=%fused_computation.19 | convolution fusion | flops 806092800 | bytes 5245956 | tf_op jit(solution)/shard_map/dot_general | solution.py:26
  39.9 2.0 %fusion.21 = f32[256,1,512]{2,0,1:T(8,128)S(1)} fusion(bf16[4096,512]{1,0:T(8,128)(2,1)S(1)} %constant_dynamic-update-slice_fusion, s32[]{:T(128)S(6)} %select_n.31, bf16[3072,256]{1,0:T(8,128)(2,1)S(1)} %copy-done.1, pred[3072]{0:T(1024)(128)(4,1)S(1)} %get-tuple-element.7), kind=kOutput, calls=%fused_computation.18 | convolution fusion | flops 806092800 | bytes 5245956 | tf_op jit(solution)/shard_map/dot_general | solution.py:26
  41.9 2.0 %fusion.16 = f32[256,1,512]{2,0,1:T(8,128)S(1)} fusion(bf16[4096,512]{1,0:T(8,128)(2,1)S(1)} %constant_dynamic-update-slice_fusion, s32[]{:T(128)S(6)} %select_n.29, bf16[3072,256]{1,0:T(8,128)(2,1)S(1)} %copy-done.1, pred[3072]{0:T(1024)(128)(4,1)S(1)} %get-tuple-element.5), kind=kOutput, calls=%fused_computation.17 | convolution fusion | flops 806092800 | bytes 5245956 | tf_op jit(solution)/shard_map/dot_general | solution.py:26
  43.9 1.5 %pad_maximum_fusion = f32[256,4,512]{2,0,1:T(8,128)} fusion(f32[256,1,512]{2,0,1:T(8,128)S(1)} %fusion.31, f32[256,1,512]{2,0,1:T(8,128)S(1)} %fusion.26, f32[256,1,512]{2,0,1:T(8,128)S(1)} %fusion.21, f32[256,1,512]{2,0,1:T(8,128)S(1)} %fusion.16), kind=kLoop, calls=%fused_computation.8 | loop fusion | flops 1572864 | bytes 4194304 | tf_op jit(solution)/shard_map/stack | solution.py:50
  45.5 0.0 reduce-scatter.2.cloned.1.call-update
  45.5 70.4 %reduce-scatter.2.cloned.1.call-done = f32[32,4,512]{2,0,1:T(8,128)} async-done(((f32[256,4,512]{2,0,1:T(8,128)}), f32[32,4,512]{2,0,1:T(8,128)}) %reduce-scatter.2.cloned.1.call-update) | async-done | bytes 262160 | tf_op jit(solution)/shard_map/reduce_scatter | solution.py:49
  115.9 9.4 %all_to_all.4 = f32[32,4,512]{2,0,1:T(8,128)S(1)} all-to-all(f32[32,4,512]{2,0,1:T(8,128)} %reduce-scatter.2.cloned.1.call-done), channel_id=1, replica_groups=mesh['seg'=8,'lag'=4] {'lag'}, dimensions={1} | all-to-all | bytes 524288 | tf_op jit(solution)/shard_map/all_to_all | solution.py:55
  125.3 0.2 copy.7
  125.5 1.1 mul.24
  (2 shorter events, 0.0 us)
Async XLA Ops:
  6.5 2.6 %copy-start = (s32[2]{0:T(128)S(1)}, s32[2]{0:T(128)}, u32[]{:S(2)}) copy-start(s32[2]{0:T(128)} %param.7) | copy-start | bytes 28
  6.5 8.1 %copy-start.2 = (s32[4]{0:T(128)S(1)}, s32[4]{0:T(128)}, u32[]{:S(2)}) copy-start(s32[4]{0:T(128)} %param.6) | copy-start | bytes 52
  6.5 109.3 %reduce-scatter.2.cloned.1.call-start = ((), (), s32[]{:S(2)}) async-start(), calls=%async_computation.2 | async-start | bytes 2359296 | tf_op jit(solution)/shard_map/reduce_scatter | solution.py:49
  7.9 28.0 %collective-permute-start = (bf16[1024,512]{1,0:T(8,128)(2,1)S(1)}, bf16[1024,512]{1,0:T(8,128)(2,1)S(1)}, u32[]{:S(2)}, u32[]{:S(2)}) collective-permute-start(bf16[1024,512]{1,0:T(8,128)(2,1)S(1)} %slice.16), channel_id=1, source_target_pairs={{4,0},{8,4},{12,8},{16,12},{20,16},{24,20},{28,24},{5,1},{9,5},{13... | collective-permute-start | bytes 3145736 | tf_op jit(solution)/shard_map/ppermute | solution.py:16
  18.3 17.6 %copy-start.1 = (bf16[3072,256]{1,0:T(8,128)(2,1)S(1)}, bf16[3072,256]{1,0:T(8,128)(2,1)}, u32[]{:S(2)}) copy-start(bf16[3072,256]{1,0:T(8,128)(2,1)} %param.4) | copy-start | bytes 4718596
Sparse Core Ops, SparseCore 0:
  45.6 70.2 reduce-scatter.1
where the time goes:
time: 134 us; the launch traced here: 133 us
  waiting for transfers between devices  88 us (66%)
  between operations  19.6 us (15%)
  blocking collectives  9.38 us (7%)
  matrix products  7.94 us (6%)
  local copies, waits for them, and re-layouts  5.3 us (4%)
  other arithmetic  1.95 us (1%)
    reduce_scatter x1, waiting for transfers between devices, per_device(): lax.psum_scatter(jnp.stack([lag_term(columns, lag_value) for lag_value in...  70.4 us
    ppermute x1, waiting for transfers between devices, shifted_2(): lax.ppermute(value, axis, [(source, source + steps) for source in range(i...  17.5 us
    all_to_all x1, blocking collectives, per_device(): lax.all_to_all(shares, 'lag', split_axis=1, concat_axis=2, tiled=True)  9.38 us
    dot_general x4, matrix products, product_over_time(): lax.dot_general(masked, shifted, (((0,), (0,)), ((), ())), preferred_elem...  7.94 us
  transfers between devices with their start and end apart: 2, of which 2 were waited for; matrix products, arithmetic and copies ran while one was open for 2% of the time, Pallas kernels for 0%

commit v1 on v0

v1 whole, which is shorter than its diff:
```python
import math

import jax
import jax.numpy as jnp
from jax import lax
from jax.experimental import pallas as pl
from jax.experimental.pallas import tpu as pltpu
from jax.experimental import pallas as pl
from jax.experimental.pallas import tpu as pltpu
from jax.experimental import pallas as pl
from jax.experimental.pallas import tpu as pltpu
from jax.experimental import pallas as pl
from jax.experimental.pallas import tpu as pltpu
from jax.experimental import pallas as pl
from jax.experimental.pallas import tpu as pltpu
from jax.sharding import PartitionSpec as P


LMAX = 1024
LBW = 2
NBLK = 2
FINE = 64.0
FULL = 32700.0
LEAST = -112.0 * FINE
SCALE_ROWS = 8
LANES = 128
LANES = 128
LANES = 128
LANES = 128
LANES = 128


def shifted_by(value, axis, steps):
    count = lax.axis_size(axis)
    initial, last = (max(0, -steps), min(count, count - steps))
    return lax.ppermute(value, axis, [(source, source + steps) for source in range(initial, last)])


def segment_ids(run_lengths, start_row, row_count):
    run_ends = jnp.cumsum(run_lengths)
    places = start_row + jnp.arange(row_count, dtype=jnp.int32)
    return jnp.sum((run_ends[None, :] <= places[:, None]).astype(jnp.int32), axis=1)


def product_over_time(masked, shifted):
    return lax.dot_general(
        masked, shifted, (((0,), (0,)), ((), ())), preferred_element_type=jnp.float32
    )


def per_device_plain(actuator_input, sensor_output, run_lengths, lag_offsets):
    samples = actuator_input.shape[0]
    devices_seg = lax.axis_size("seg")
    scaling = 1.0 / math.sqrt(samples * devices_seg)
    start_row = lax.axis_index("seg") * samples
    halo_rows = shifted_by(sensor_output[:LMAX], "seg", -1)
    idents = segment_ids(run_lengths, start_row, samples + LMAX)
    own_ids = idents[:samples]
    shifts = [lag_offsets[blk_num] + lag_step for blk_num in range(NBLK) for lag_step in range(LBW)]
    joined = jnp.concatenate([sensor_output, halo_rows], axis=0)

    def lag_term(lag_value):
        shifted = lax.dynamic_slice_in_dim(joined, lag_value, samples, 0)
        shifted_ids = lax.dynamic_slice_in_dim(idents, lag_value, samples, 0)
        masked = jnp.where((own_ids == shifted_ids)[:, None], actuator_input, jnp.zeros_like(actuator_input))
        return product_over_time(masked, shifted)

    shares = lax.psum_scatter(
        jnp.stack([lag_term(lag_value) for lag_value in shifts], axis=1),
        "seg",
        scatter_dimension=0,
        tiled=True,
    )
    result_rows = lax.all_to_all(shares, "lag", split_axis=1, concat_axis=2, tiled=True)
    return result_rows * scaling


def exchange(value, seg_bits, lag_bits):
    segs, lags = lax.axis_size("seg"), lax.axis_size("lag")
    pairs = [
        (s * lags + l, (s ^ seg_bits) * lags + (l ^ lag_bits)) for s in range(segs) for l in range(lags)
    ]
    return lax.ppermute(value, ("seg", "lag"), pairs)


def column_code(largest):
    return jnp.maximum(jnp.ceil(jnp.log2(largest) * FINE), LEAST)


def coded(value, code):
    held = jnp.round(value * (jnp.exp2(code * (-1.0 / FINE)) * FULL))
    return held.astype(jnp.int32).astype(jnp.int16)


def decoded(held, code):
    return held.astype(jnp.float32) * (jnp.exp2(code * (1.0 / FINE)) * (1.0 / FULL))


def codes_of(ref, at):
    return ref[pl.ds(at, SCALE_ROWS), :].astype(jnp.int32).astype(jnp.float32)


def lag_of(offsets_ref, which):
    return offsets_ref[which // LBW] + which % LBW


def fill_rows(turned, at_lane, masked, at_masked, runs, offsets, lag, lags, start_row, chunk):
    actuators = turned.shape[0]
    tiles = chunk // LANES
    lane = lax.broadcasted_iota(jnp.int32, (1, LANES), 1)
    ends, end = [], jnp.int32(0)
    for run in range(runs.shape[0]):
        end = end + runs[run]
        ends.append(end)
    for step in range(lags):
        shift = lag_of(offsets, lag ^ step)
        at = at_lane - shift
        base, turn = at // LANES, at % LANES
        low = jnp.broadcast_to(lane < LANES - turn, (actuators, LANES))
        pieces = [
            pltpu.roll(
                turned[:, pl.ds(pl.multiple_of((base + tile) * LANES, LANES), LANES)],
                (LANES - turn) % LANES,
                1,
            )
            for tile in range(tiles + 1)
        ]
        for tile in range(tiles):
            place = lane + (start_row + tile * LANES)
            crossed = jnp.zeros((1, LANES), jnp.int32)
            for end in ends:
                crossed = crossed + ((end <= place) & (end > place - shift)).astype(jnp.int32)
            keep = jnp.broadcast_to(crossed == 0, (actuators, LANES))
            value = jnp.where(low, pieces[tile], pieces[tile + 1])
            value = jnp.where(keep, value, jnp.zeros_like(value))
            masked[pl.ds(step * actuators, actuators), pl.ds(at_masked + tile * LANES, LANES)] = value


def inner_kernel(
    runs_ref, offsets_ref, actuators_ref, sensors_ref, out_ref, runs, offsets, held, sensed, turned, masked, sems
):
    chunk, lags = LMAX, lax.axis_size("lag")
    samples, _ = actuators_ref.shape
    chunks = samples // chunk
    copies = [
        pltpu.make_async_copy(runs_ref, runs, sems.at[0]),
        pltpu.make_async_copy(offsets_ref, offsets, sems.at[1]),
    ]
    for at in range(chunks):
        here = pl.ds(at * chunk, chunk)
        copies.append(pltpu.make_async_copy(actuators_ref.at[here, :], held.at[here, :], sems.at[2 + at]))
    for at in range(1, chunks):
        copies.append(
            pltpu.make_async_copy(
                sensors_ref.at[pl.ds(at * chunk, chunk), :],
                sensed.at[pl.ds((at - 1) * chunk, chunk), :],
                sems.at[1 + chunks + at],
            )
        )
    for copy in copies:
        copy.start()
    start_row = lax.axis_index("seg") * samples
    for at in range(chunks):
        copies[2 + at].wait()
        here = pl.ds(at * chunk, chunk)
        turned[:, here] = held[here, :].T
        if at == 0:
            copies[0].wait()
            copies[1].wait()
            continue
        fill_rows(
            turned, at * chunk, masked, (at - 1) * chunk, runs, offsets,
            lax.axis_index("lag"), lags, start_row + at * chunk, chunk,
        )
        copies[1 + chunks + at].wait()
        there = pl.ds((at - 1) * chunk, chunk)
        terms = jnp.dot(masked[:, there], sensed[there, :], preferred_element_type=jnp.float32)
        if at == 1:
            out_ref[...] = terms
        else:
            out_ref[...] += terms


def outer_kernel(
    runs_ref, offsets_ref, mine_ref, theirs_ref, actuators_ref, sensors_ref, inner_ref, *refs
):
    chunk, lags, segs = LMAX, lax.axis_size("lag"), lax.axis_size("seg")
    sends, keeps, own_ref = refs[:lags], (None,) + refs[lags : 2 * lags - 1], refs[2 * lags - 1]
    runs, offsets, held, sensed, turned, masked, terms, sems = refs[2 * lags :]
    samples, actuators = actuators_ref.shape
    here = pl.ds(0, chunk)
    copies = [
        pltpu.make_async_copy(actuators_ref.at[here, :], held, sems.at[2]),
        pltpu.make_async_copy(runs_ref, runs, sems.at[0]),
        pltpu.make_async_copy(offsets_ref, offsets, sems.at[1]),
        pltpu.make_async_copy(sensors_ref.at[here, :], sensed, sems.at[3]),
    ]
    for copy in copies:
        copy.start()
    seg, lag = lax.axis_index("seg"), lax.axis_index("lag")
    rows, far, half = actuators // segs, segs // 2, chunk // 2
    core = lag % 2
    turned[:, pl.ds(pl.multiple_of(core * half, LANES), half)] = mine_ref[...].T
    turned[:, pl.ds(pl.multiple_of((1 - core) * half, LANES), half)] = theirs_ref[...].T
    copies[0].wait()
    turned[:, pl.ds(chunk, chunk)] = held[...].T
    copies[1].wait()
    copies[2].wait()
    fill_rows(turned, chunk, masked, 0, runs, offsets, lag, lags, seg * samples, chunk)
    copies[3].wait()
    terms[...] = inner_ref[...] + jnp.dot(masked[...], sensed[...], preferred_element_type=jnp.float32)

    def half_of(step, near):
        return [
            terms[pl.ds(pl.multiple_of(step * actuators + (2 * block + near) * rows, rows), rows), :]
            for block in range(far)
        ]

    def send(step, near, ref):
        parts = half_of(step, near)
        largest = jnp.abs(parts[0])
        for part in parts[1:]:
            largest = jnp.maximum(largest, jnp.abs(part))
        code = column_code(jnp.max(largest, axis=0, keepdims=True))
        for block, part in enumerate(parts):
            ref[pl.ds(block * rows, rows), :] = coded(part, code)
        ref[pl.ds(far * rows, SCALE_ROWS), :] = jnp.broadcast_to(
            code.astype(jnp.int32), (SCALE_ROWS, code.shape[1])
        ).astype(jnp.int16)

    near_at = seg % 2
    for step in range(lags):
        send(step, 1 - near_at, sends[step])
        if step:
            send(step, near_at, keeps[step])
        else:
            for block, part in enumerate(half_of(step, near_at)):
                own_ref[pl.ds(block * rows, rows), :] = part


def middle_kernel(*refs):
    lags, segs = lax.axis_size("lag"), lax.axis_size("seg")
    far = segs // 2
    came, kept, own_ref = refs[:lags], (None,) + refs[lags : 2 * lags - 1], refs[2 * lags - 1]
    total_ref, sends = refs[2 * lags], refs[2 * lags + 1 :]
    rows = total_ref.shape[0] // lags
    far_at = lax.axis_index("seg") // 2
    came_codes = [codes_of(ref, far * rows)[:1] for ref in came]
    kept_codes = [None] + [codes_of(ref, far * rows)[:1] for ref in kept[1:]]

    def block_sum(step, block):
        here = pl.ds(pl.multiple_of(block * rows, rows), rows)
        first = own_ref[here, :] if step == 0 else decoded(kept[step][here, :], kept_codes[step])
        return first + decoded(came[step][here, :], came_codes[step])

    for step in range(lags):
        total_ref[pl.ds(step * rows, rows), :] = block_sum(step, far_at)
    sublane = lax.broadcasted_iota(jnp.int32, (SCALE_ROWS, total_ref.shape[1]), 0)
    for bits in range(1, far):
        codes = jnp.zeros(sublane.shape, jnp.int32)
        for step in range(lags):
            part = block_sum(step, far_at ^ bits)
            code = column_code(jnp.max(jnp.abs(part), axis=0, keepdims=True))
            sends[bits - 1][pl.ds(step * rows, rows), :] = coded(part, code)
            codes = jnp.where(sublane == step, jnp.broadcast_to(code.astype(jnp.int32), sublane.shape), codes)
        sends[bits - 1][pl.ds(lags * rows, SCALE_ROWS), :] = codes.astype(jnp.int16)


def last_kernel(scaling, total_ref, *refs):
    lags = lax.axis_size("lag")
    came, out_ref = refs[:-1], refs[-1]
    rows = total_ref.shape[0] // lags
    width = total_ref.shape[1]
    lag = lax.axis_index("lag")
    codes = [codes_of(ref, lags * rows) for ref in came]
    for step in range(lags):
        here = pl.ds(step * rows, rows)
        value = total_ref[here, :]
        for ref, code in zip(came, codes):
            value = value + decoded(ref[here, :], code[step : step + 1])
        out_ref[:, 0, pl.ds(pl.multiple_of((lag ^ step) * width, LANES), width)] = value * scaling


def per_device_staged(actuator_input, sensor_output, run_lengths, lag_offsets):
    samples, actuators = actuator_input.shape
    sensors = sensor_output.shape[1]
    segs, lags = lax.axis_size("seg"), lax.axis_size("lag")
    far, rows, chunk = segs // 2, actuators // segs, LMAX
    scaling = 1.0 / math.sqrt(samples * segs)
    lag = lax.axis_index("lag")
    spare = lags * actuators
    payload = jax.ShapeDtypeStruct((far * rows + SCALE_ROWS, sensors), jnp.int16)
    onward = jax.ShapeDtypeStruct((lags * rows + SCALE_ROWS, sensors), jnp.int16)
    vmem = pl.BlockSpec(memory_space=pltpu.VMEM)
    half = LMAX // 2
    core = lag % 2
    fetched = shifted_by(
        lax.dynamic_slice_in_dim(actuator_input, samples - LMAX + half * core, half, 0), "seg", 1
    )
    others = exchange(fetched, 0, 1)

    hbm = pl.BlockSpec(memory_space=pltpu.HBM)
    scalars = [pltpu.SMEM(run_lengths.shape, jnp.int32), pltpu.SMEM(lag_offsets.shape, jnp.int32)]
    chunks = samples // chunk
    inner = pl.pallas_call(
        inner_kernel,
        in_specs=[hbm] * 4,
        out_specs=vmem,
        out_shape=jax.ShapeDtypeStruct((spare, sensors), jnp.float32),
        scratch_shapes=scalars
        + [
            pltpu.VMEM((samples, actuators), jnp.bfloat16),
            pltpu.VMEM((samples - chunk, sensors), jnp.bfloat16),
            pltpu.VMEM((actuators, samples + LANES), jnp.bfloat16),
            pltpu.VMEM((spare, samples - chunk), jnp.bfloat16),
            pltpu.SemaphoreType.DMA((1 + 2 * chunks,)),
        ],
        compiler_params=pltpu.CompilerParams(vmem_limit_bytes=48 << 20),
        cost_estimate=pl.CostEstimate(
            flops=2 * spare * sensors * (samples - chunk), bytes_accessed=6 << 20, transcendentals=0
        ),
        name="inner",
    )(run_lengths, lag_offsets, actuator_input, sensor_output)

    packed = pl.pallas_call(
        outer_kernel,
        in_specs=[hbm] * 2 + [vmem] * 2 + [hbm] * 2 + [vmem],
        out_specs=[vmem] * (2 * lags),
        out_shape=[payload] * (2 * lags - 1) + [jax.ShapeDtypeStruct((far * rows, sensors), jnp.float32)],
        scratch_shapes=scalars
        + [
            pltpu.VMEM((chunk, actuators), jnp.bfloat16),
            pltpu.VMEM((chunk, sensors), jnp.bfloat16),
            pltpu.VMEM((actuators, 2 * chunk + LANES), jnp.bfloat16),
            pltpu.VMEM((spare, chunk), jnp.bfloat16),
            pltpu.VMEM((spare, sensors), jnp.float32),
            pltpu.SemaphoreType.DMA((4,)),
        ],
        compiler_params=pltpu.CompilerParams(vmem_limit_bytes=48 << 20),
        cost_estimate=pl.CostEstimate(
            flops=2 * spare * sensors * chunk, bytes_accessed=6 << 20, transcendentals=0
        ),
        name="outer",
    )(run_lengths, lag_offsets, fetched, others, actuator_input, sensor_output, inner)

    came, kept = [None] * lags, [None] * lags
    for place in range(lags // 2):
        low, high = (place + 1) % (lags // 2), lags // 2 + place
        came[low] = exchange(packed[low], 1, low)
        kept[high] = exchange(packed[lags + high - 1], 0, high)
        came[high] = exchange(packed[high], 1, high)
    for step in range(1, lags // 2):
        kept[step] = exchange(packed[lags + step - 1], 0, step)

    middle = pl.pallas_call(
        middle_kernel,
        in_specs=[vmem] * (2 * lags),
        out_specs=[vmem] * far,
        out_shape=[jax.ShapeDtypeStruct((lags * rows, sensors), jnp.float32)] + [onward] * (far - 1),
        compiler_params=pltpu.CompilerParams(vmem_limit_bytes=8 << 20),
        name="middle",
    )(*came, *kept[1:], packed[-1])

    arrived = [exchange(middle[bits], 2 * bits, 0) for bits in range(far - 1, 0, -1)][::-1]

    def last_body(*refs):
        return last_kernel(scaling, *refs)

    return pl.pallas_call(
        last_body,
        in_specs=[vmem] * far,
        out_specs=vmem,
        out_shape=jax.ShapeDtypeStruct((rows, 1, lags * sensors), jnp.float32),
        compiler_params=pltpu.CompilerParams(vmem_limit_bytes=8 << 20),
        name="last",
    )(middle[0], *arrived)


def solution(mesh):
    segs, lags = mesh.shape["seg"], mesh.shape["lag"]

    def per_device(actuator_input, sensor_output, run_lengths, lag_offsets):
        rows = actuator_input.shape[1] // segs
        staged = (
            4 <= segs <= 16
            and segs & (segs - 1) == 0
            and lags & (lags - 1) == 0
            and lags == NBLK * LBW
            and rows % 8 == 0
            and actuator_input.shape[0] % LMAX == 0
            and actuator_input.shape[0] > LMAX
        )
        chosen = per_device_staged if staged else per_device_plain
        return chosen(actuator_input, sensor_output, run_lengths, lag_offsets)

    mapped = jax.shard_map(
        per_device,
        mesh=mesh,
        in_specs=(P("seg", None), P("seg", "lag"), P(), P()),
        out_specs=P("seg", "lag", None),
        check_vma=False,
    )
    return mapped
    return mapped
    return mapped
    return mapped
```

time: 134 us -> 60.1 us (0.45)
  waiting for transfers between devices: 88 us -> 27.9 us
  between operations: 19.6 us -> 0.05 us
  starting transfers between devices: 1.29 us -> 18.9 us
  Pallas kernels: 0 us -> 9.38 us
  blocking collectives: 9.38 us -> 0 us
  matrix products: 7.94 us -> 0 us
  other arithmetic: 1.95 us -> 0 us
  local copies, waits for them, and re-layouts: 5.3 us -> 3.68 us
    reduce_scatter x1 -> x0, waiting for transfers between devices: 70.4 us -> none  [per_device(): lax.psum_scatter(jnp.stack([lag_term(columns, lag_value) for lag_value in...]
    ppermute x1 -> x12, starting transfers between devices: 1.29 us -> 18.9 us  [the longest x11 14 us: exchange(): return lax.ppermute(value, ('seg', 'lag'), pairs)]
    ppermute x1 -> x12, waiting for transfers between devices: 17.5 us -> 27.9 us  [the longest x11 22.3 us: exchange(): return lax.ppermute(value, ('seg', 'lag'), pairs)]
    all_to_all x1 -> x0, blocking collectives: 9.38 us -> none  [per_device(): lax.all_to_all(shares, 'lag', split_axis=1, concat_axis=2, tiled=True)]
    pallas_call x0 -> x4, Pallas kernels: none -> 9.38 us  [the longest x1 4.86 us: per_device_staged(): pl.pallas_call(inner_kernel, in_specs=[hbm] * 4, out_specs=vmem, out_shap...]
    dot_general x4 -> x0, matrix products: 7.94 us -> none  [product_over_time(): lax.dot_general(masked, shifted, (((0,), (0,)), ((), ())), preferred_elem...]
    slice x2 -> x0, local copies, waits for them, and re-layouts: 1.89 us -> none  [the longest x1 1.32 us: per_device(): halo_rows = shifted_2(sensor_output[:LMAX], 'seg', -1)]
    another operation x2 -> x0, other arithmetic: 1.7 us -> none  [the longest x1 1.52 us: per_device(): jnp.stack([lag_term(columns, lag_value) for lag_value in shifts], axis=1)]
  transfers between devices with their start and end apart: 2 -> 12, of which waited for: 2 -> 9; matrix products, arithmetic and copies ran while one was open for 2% -> 0% of each run, Pallas kernels for 0% -> 8%
where the time goes in v1:
time: 60.1 us; the launch traced here: 59.9 us
  waiting for transfers between devices  27.9 us (46%)
  starting transfers between devices  18.9 us (31%)
  Pallas kernels  9.38 us (16%)
  local copies, waits for them, and re-layouts  3.68 us (6%)
    ppermute x11, waiting for transfers between devices, exchange(): return lax.ppermute(value, ('seg', 'lag'), pairs)  22.3 us
    ppermute x11, starting transfers between devices, exchange(): return lax.ppermute(value, ('seg', 'lag'), pairs)  14 us
    ppermute x1, waiting for transfers between devices, shifted_by(): lax.ppermute(value, axis, [(source, source + steps) for source in range(i...  5.53 us
    ppermute x1, starting transfers between devices, shifted_by(): lax.ppermute(value, axis, [(source, source + steps) for source in range(i...  4.89 us
    pallas_call x1, Pallas kernels, per_device_staged(): pl.pallas_call(inner_kernel, in_specs=[hbm] * 4, out_specs=vmem, out_shap...  4.86 us
    pallas_call x1, Pallas kernels, per_device_staged(): pl.pallas_call(outer_kernel, in_specs=[hbm] * 2 + [vmem] * 2 + [hbm] * 2...  3.17 us
    unnamed x6, local copies, waits for them, and re-layouts  2.72 us
  transfers between devices with their start and end apart: 12, of which 9 were waited for; matrix products, arithmetic and copies ran while one was open for 0% of the time, Pallas kernels for 8%

profile of v1, /device:TPU:0, one launch (start us, length us, event | category | flops | bytes accessed | tf_op | source)
XLA Modules:
  0.0 59.9 jit_solution(18349777345629158205)
XLA Ops:
  0.0 1.0 %constant_dynamic-slice_fusion = bf16[512,256]{1,0:T(8,128)(2,1)S(1)} fusion(bf16[3072,256]{1,0:T(8,128)(2,1)} %actuators_ref.3, s32[]{:T(128)S(6)} %select_n.11), kind=kLoop, calls=%fused_computation | loop fusion | bytes 524292 | tf_op jit(solution)/shard_map/dynamic_slice | solution.py:298
  1.0 4.9 %collective-permute-start = (bf16[512,256]{1,0:T(8,128)(2,1)S(1)}, bf16[512,256]{1,0:T(8,128)(2,1)S(1)}, u32[]{:S(2)}, u32[]{:S(2)}) collective-permute-start(bf16[512,256]{1,0:T(8,128)(2,1)S(1)} %constant_dynamic-slice_fusion), channel_id=1, source_target_pairs={{0,4},{4,8},{8,12},{12,16},{16,20},{20,24},{24,28},{1,5},{5,9},{9,... | collective-permute-start | bytes 786440 | tf_op jit(solution)/shard_map/ppermute | solution.py:36
  5.9 5.5 %collective-permute-done.mine_ref = bf16[512,256]{1,0:T(8,128)(2,1)S(1)} collective-permute-done((bf16[512,256]{1,0:T(8,128)(2,1)S(1)}, bf16[512,256]{1,0:T(8,128)(2,1)S(1)}, u32[]{:S(2)}, u32[]{:S(2)}) %collective-permute-start) | collective-permute-done | bytes 262176 | tf_op jit(solution)/shard_map/ppermute | solution.py:36
  11.4 0.0 collective-permute-start.1
  11.4 0.0 copy-start
  11.4 1.4 %copy-done = bf16[3072,256]{1,0:T(8,128)(2,1)S(1)} copy-done((bf16[3072,256]{1,0:T(8,128)(2,1)S(1)}, bf16[3072,256]{1,0:T(8,128)(2,1)}, u32[]{:S(2)}) %copy-start) | copy-done | bytes 1572888
  12.8 0.0 copy-start.1
  12.8 0.7 %copy-done.1 = s32[4]{0:T(128)S(1)} copy-done((s32[4]{0:T(128)S(1)}, s32[4]{0:T(128)}, u32[]{:S(2)}) %copy-start.1) | copy-done | bytes 40
  13.5 0.0 copy-start.2
  13.5 0.7 %copy-done.2 = s32[2]{0:T(128)S(1)} copy-done((s32[2]{0:T(128)S(1)}, s32[2]{0:T(128)}, u32[]{:S(2)}) %copy-start.2) | copy-done | bytes 32
  14.1 4.9 %inner.1.inner_ref = f32[1024,512]{1,0:T(8,128)S(1)} custom-call(s32[4]{0:T(128)S(1)} %copy-done.1, s32[2]{0:T(128)S(1)} %copy-done.2, bf16[3072,256]{1,0:T(8,128)(2,1)S(1)} %copy-done, bf16[3072,512]{1,0:T(8,128)(2,1)} %sensors_ref.3), custom_call_target="tpu_custom_call" | custom-call | flops 2147483648 | bytes 6291456 | tf_op jit(solution)/shard_map/inner/pallas_call | solution.py:305
  19.0 0.0 collective-permute-done.1.theirs_ref
  19.0 3.2 %outer.1 = (s16[136,512]{1,0:T(8,128)(2,1)S(1)}, s16[136,512]{1,0:T(8,128)(2,1)S(1)}, s16[136,512]{1,0:T(8,128)(2,1)S(1)}, s16[136,512]{1,0:T(8,128)(2,1)S(1)}, ...) custom-call(s32[4]{0:T(128)S(1)} %copy-done.1, ...), custom_call_target="tpu_custom_call" | custom-call | flops 1073741824 | bytes 6291456 | tf_op jit(solution)/shard_map/outer/pallas_call | solution.py:325
  22.2 2.5 %collective-permute-start.2 = (s16[136,512]{1,0:T(8,128)(2,1)S(1)}, s16[136,512]{1,0:T(8,128)(2,1)S(1)}, u32[]{:S(2)}, u32[]{:S(2)}) collective-permute-start(s16[136,512]{1,0:T(8,128)(2,1)S(1)} %get-tuple-element.17), channel_id=1, source_target_pairs={{0,4},{1,5},{2,6},{3,7},{4,0},{5,1},{6,2},{7,3},{8,12},{9,13},{10,... | collective-permute-start | bytes 417800 | tf_op jit(solution)/shard_map/ppermute | solution.py:83
  24.7 0.2 collective-permute-start.3
  24.9 2.6 %collective-permute-start.4 = (s16[136,512]{1,0:T(8,128)(2,1)S(1)}, s16[136,512]{1,0:T(8,128)(2,1)S(1)}, u32[]{:S(2)}, u32[]{:S(2)}) collective-permute-start(s16[136,512]{1,0:T(8,128)(2,1)S(1)} %get-tuple-element.19), channel_id=1, source_target_pairs={{0,6},{1,7},{2,4},{3,5},{4,2},{5,3},{6,0},{7,1},{8,14},{9,15},{10,... | collective-permute-start | bytes 417800 | tf_op jit(solution)/shard_map/ppermute | solution.py:83
  27.5 0.0 collective-permute-start.5
  27.5 0.4 collective-permute-start.6
  28.0 1.3 %collective-permute-done.2.refs_0_ = s16[136,512]{1,0:T(8,128)(2,1)S(1)} collective-permute-done((s16[136,512]{1,0:T(8,128)(2,1)S(1)}, s16[136,512]{1,0:T(8,128)(2,1)S(1)}, u32[]{:S(2)}, u32[]{:S(2)}) %collective-permute-start.2) | collective-permute-done | bytes 139296 | tf_op jit(solution)/shard_map/ppermute | solution.py:83
  29.2 1.5 %collective-permute-start.7 = (s16[136,512]{1,0:T(8,128)(2,1)S(1)}, s16[136,512]{1,0:T(8,128)(2,1)S(1)}, u32[]{:S(2)}, u32[]{:S(2)}) collective-permute-start(s16[136,512]{1,0:T(8,128)(2,1)S(1)} %get-tuple-element.22), channel_id=1, source_target_pairs={{0,2},{1,3},{2,0},{3,1},{4,6},{5,7},{6,4},{7,5},{8,10},{9,11},{10,... | collective-permute-start | bytes 417800 | tf_op jit(solution)/shard_map/ppermute | solution.py:83
  30.8 1.1 %collective-permute-done.3.refs_1_ = s16[136,512]{1,0:T(8,128)(2,1)S(1)} collective-permute-done((s16[136,512]{1,0:T(8,128)(2,1)S(1)}, s16[136,512]{1,0:T(8,128)(2,1)S(1)}, u32[]{:S(2)}, u32[]{:S(2)}) %collective-permute-start.3) | collective-permute-done | bytes 139296 | tf_op jit(solution)/shard_map/ppermute | solution.py:83
  31.9 1.6 %collective-permute-start.8 = (s16[136,512]{1,0:T(8,128)(2,1)S(1)}, s16[136,512]{1,0:T(8,128)(2,1)S(1)}, u32[]{:S(2)}, u32[]{:S(2)}) collective-permute-start(s16[136,512]{1,0:T(8,128)(2,1)S(1)} %get-tuple-element.23), channel_id=1, source_target_pairs={{0,3},{1,2},{2,1},{3,0},{4,7},{5,6},{6,5},{7,4},{8,11},{9,10},{10,... | collective-permute-start | bytes 417800 | tf_op jit(solution)/shard_map/ppermute | solution.py:83
  33.5 2.8 %collective-permute-done.4.refs_2_ = s16[136,512]{1,0:T(8,128)(2,1)S(1)} collective-permute-done((s16[136,512]{1,0:T(8,128)(2,1)S(1)}, s16[136,512]{1,0:T(8,128)(2,1)S(1)}, u32[]{:S(2)}, u32[]{:S(2)}) %collective-permute-start.4) | collective-permute-done | bytes 139296 | tf_op jit(solution)/shard_map/ppermute | solution.py:83
  36.3 2.6 %collective-permute-done.5.refs_3_ = s16[136,512]{1,0:T(8,128)(2,1)S(1)} collective-permute-done((s16[136,512]{1,0:T(8,128)(2,1)S(1)}, s16[136,512]{1,0:T(8,128)(2,1)S(1)}, u32[]{:S(2)}, u32[]{:S(2)}) %collective-permute-start.5) | collective-permute-done | bytes 139296 | tf_op jit(solution)/shard_map/ppermute | solution.py:83
  38.9 0.0 collective-permute-done.6.refs_4_
  38.9 2.9 %collective-permute-done.7.refs_5_ = s16[136,512]{1,0:T(8,128)(2,1)S(1)} collective-permute-done((s16[136,512]{1,0:T(8,128)(2,1)S(1)}, s16[136,512]{1,0:T(8,128)(2,1)S(1)}, u32[]{:S(2)}, u32[]{:S(2)}) %collective-permute-start.7) | collective-permute-done | bytes 139296 | tf_op jit(solution)/shard_map/ppermute | solution.py:83
  41.8 0.8 %collective-permute-done.8.refs_6_ = s16[136,512]{1,0:T(8,128)(2,1)S(1)} collective-permute-done((s16[136,512]{1,0:T(8,128)(2,1)S(1)}, s16[136,512]{1,0:T(8,128)(2,1)S(1)}, u32[]{:S(2)}, u32[]{:S(2)}) %collective-permute-start.8) | collective-permute-done | bytes 139296 | tf_op jit(solution)/shard_map/ppermute | solution.py:83
  42.6 0.4 middle.1
  43.0 2.5 %collective-permute-start.9 = (s16[136,512]{1,0:T(8,128)(2,1)S(1)}, s16[136,512]{1,0:T(8,128)(2,1)S(1)}, u32[]{:S(2)}, u32[]{:S(2)}) collective-permute-start(s16[136,512]{1,0:T(8,128)(2,1)S(1)} %get-tuple-element.26), channel_id=1, source_target_pairs={{0,8},{1,9},{2,10},{3,11},{4,12},{5,13},{6,14},{7,15},{8,0},{9,1},... | collective-permute-start | bytes 417800 | tf_op jit(solution)/shard_map/ppermute | solution.py:83
  45.5 2.6 %collective-permute-start.10 = (s16[136,512]{1,0:T(8,128)(2,1)S(1)}, s16[136,512]{1,0:T(8,128)(2,1)S(1)}, u32[]{:S(2)}, u32[]{:S(2)}) collective-permute-start(s16[136,512]{1,0:T(8,128)(2,1)S(1)} %get-tuple-element.27), channel_id=1, source_target_pairs={{0,16},{1,17},{2,18},{3,19},{4,20},{5,21},{6,22},{7,23},{8,24},{9,... | collective-permute-start | bytes 417800 | tf_op jit(solution)/shard_map/ppermute | solution.py:83
  48.1 0.0 collective-permute-start.11
  48.1 4.5 %collective-permute-done.9.refs_1_ = s16[136,512]{1,0:T(8,128)(2,1)S(1)} collective-permute-done((s16[136,512]{1,0:T(8,128)(2,1)S(1)}, s16[136,512]{1,0:T(8,128)(2,1)S(1)}, u32[]{:S(2)}, u32[]{:S(2)}) %collective-permute-start.9) | collective-permute-done | bytes 139296 | tf_op jit(solution)/shard_map/ppermute | solution.py:83
  52.6 6.4 %collective-permute-done.10.refs_2_ = s16[136,512]{1,0:T(8,128)(2,1)S(1)} collective-permute-done((s16[136,512]{1,0:T(8,128)(2,1)S(1)}, s16[136,512]{1,0:T(8,128)(2,1)S(1)}, u32[]{:S(2)}, u32[]{:S(2)}) %collective-permute-start.10) | collective-permute-done | bytes 139296 | tf_op jit(solution)/shard_map/ppermute | solution.py:83
  59.0 0.0 collective-permute-done.11.refs_3_
  59.0 0.9 %last.1 = f32[32,1,2048]{2,1,0:T(1,128)} custom-call(f32[128,512]{1,0:T(8,128)S(1)} %get-tuple-element.25.refs_0_, s16[136,512]{1,0:T(8,128)(2,1)S(1)} %collective-permute-done.9.refs_1_, s16[136,512]{1,0:T(8,128)(2,1)S(1)} %collective-permute-done.10.refs_2_, s16[136,512]{1,0:T(8,128)(2,1)S(1)} %collective-permute-done.11.refs_3_), custom_call_target="tpu_custom_call" | custom-call | tf_op jit(solution)/shard_map/last/pallas_call | solution.py:369
Async XLA Ops:
  1.0 10.4 %collective-permute-start = (bf16[512,256]{1,0:T(8,128)(2,1)S(1)}, bf16[512,256]{1,0:T(8,128)(2,1)S(1)}, u32[]{:S(2)}, u32[]{:S(2)}) collective-permute-start(bf16[512,256]{1,0:T(8,128)(2,1)S(1)} %constant_dynamic-slice_fusion), channel_id=1, source_target_pairs={{0,4},{4,8},{8,12},{12,16},{16,20},{20,24},{24,28},{1,5},{5,9},{9,... | collective-permute-start | bytes 786440 | tf_op jit(solution)/shard_map/ppermute | solution.py:36
  11.4 7.6 %collective-permute-start.1 = (bf16[512,256]{1,0:T(8,128)(2,1)S(1)}, bf16[512,256]{1,0:T(8,128)(2,1)S(1)}, u32[]{:S(2)}, u32[]{:S(2)}) collective-permute-start(bf16[512,256]{1,0:T(8,128)(2,1)S(1)} %collective-permute-done.mine_ref), channel_id=1, source_target_pairs={{0,1},{1,0},{2,3},{3,2},{4,5},{5,4},{6,7},{7,6},{8,9},{9,8},{10,11... | collective-permute-start | bytes 786440 | tf_op jit(solution)/shard_map/ppermute | solution.py:83
  11.4 1.4 %copy-start = (bf16[3072,256]{1,0:T(8,128)(2,1)S(1)}, bf16[3072,256]{1,0:T(8,128)(2,1)}, u32[]{:S(2)}) copy-start(bf16[3072,256]{1,0:T(8,128)(2,1)} %actuators_ref.3) | copy-start | bytes 4718596
  12.8 0.7 %copy-start.1 = (s32[4]{0:T(128)S(1)}, s32[4]{0:T(128)}, u32[]{:S(2)}) copy-start(s32[4]{0:T(128)} %runs_ref.3) | copy-start | bytes 52
  13.5 0.7 %copy-start.2 = (s32[2]{0:T(128)S(1)}, s32[2]{0:T(128)}, u32[]{:S(2)}) copy-start(s32[2]{0:T(128)} %offsets_ref.3) | copy-start | bytes 28
  22.2 7.1 %collective-permute-start.2 = (s16[136,512]{1,0:T(8,128)(2,1)S(1)}, s16[136,512]{1,0:T(8,128)(2,1)S(1)}, u32[]{:S(2)}, u32[]{:S(2)}) collective-permute-start(s16[136,512]{1,0:T(8,128)(2,1)S(1)} %get-tuple-element.17), channel_id=1, source_target_pairs={{0,4},{1,5},{2,6},{3,7},{4,0},{5,1},{6,2},{7,3},{8,12},{9,13},{10,... | collective-permute-start | bytes 417800 | tf_op jit(solution)/shard_map/ppermute | solution.py:83
  24.7 7.2 %collective-permute-start.3 = (s16[136,512]{1,0:T(8,128)(2,1)S(1)}, s16[136,512]{1,0:T(8,128)(2,1)S(1)}, u32[]{:S(2)}, u32[]{:S(2)}) collective-permute-start(s16[136,512]{1,0:T(8,128)(2,1)S(1)} %get-tuple-element.18), channel_id=1, source_target_pairs={{0,5},{1,4},{2,7},{3,6},{4,1},{5,0},{6,3},{7,2},{8,13},{9,12},{10,... | collective-permute-start | bytes 417800 | tf_op jit(solution)/shard_map/ppermute | solution.py:83
  24.9 11.4 %collective-permute-start.4 = (s16[136,512]{1,0:T(8,128)(2,1)S(1)}, s16[136,512]{1,0:T(8,128)(2,1)S(1)}, u32[]{:S(2)}, u32[]{:S(2)}) collective-permute-start(s16[136,512]{1,0:T(8,128)(2,1)S(1)} %get-tuple-element.19), channel_id=1, source_target_pairs={{0,6},{1,7},{2,4},{3,5},{4,2},{5,3},{6,0},{7,1},{8,14},{9,15},{10,... | collective-permute-start | bytes 417800 | tf_op jit(solution)/shard_map/ppermute | solution.py:83
  27.5 11.3 %collective-permute-start.5 = (s16[136,512]{1,0:T(8,128)(2,1)S(1)}, s16[136,512]{1,0:T(8,128)(2,1)S(1)}, u32[]{:S(2)}, u32[]{:S(2)}) collective-permute-start(s16[136,512]{1,0:T(8,128)(2,1)S(1)} %get-tuple-element.20), channel_id=1, source_target_pairs={{0,7},{1,6},{2,5},{3,4},{4,3},{5,2},{6,1},{7,0},{8,15},{9,14},{10,... | collective-permute-start | bytes 417800 | tf_op jit(solution)/shard_map/ppermute | solution.py:83
  27.5 11.3 %collective-permute-start.6 = (s16[136,512]{1,0:T(8,128)(2,1)S(1)}, s16[136,512]{1,0:T(8,128)(2,1)S(1)}, u32[]{:S(2)}, u32[]{:S(2)}) collective-permute-start(s16[136,512]{1,0:T(8,128)(2,1)S(1)} %get-tuple-element.21), channel_id=1, source_target_pairs={{0,1},{1,0},{2,3},{3,2},{4,5},{5,4},{6,7},{7,6},{8,9},{9,8},{10,11... | collective-permute-start | bytes 417800 | tf_op jit(solution)/shard_map/ppermute | solution.py:83
  29.2 12.5 %collective-permute-start.7 = (s16[136,512]{1,0:T(8,128)(2,1)S(1)}, s16[136,512]{1,0:T(8,128)(2,1)S(1)}, u32[]{:S(2)}, u32[]{:S(2)}) collective-permute-start(s16[136,512]{1,0:T(8,128)(2,1)S(1)} %get-tuple-element.22), channel_id=1, source_target_pairs={{0,2},{1,3},{2,0},{3,1},{4,6},{5,7},{6,4},{7,5},{8,10},{9,11},{10,... | collective-permute-start | bytes 417800 | tf_op jit(solution)/shard_map/ppermute | solution.py:83
  31.9 10.7 %collective-permute-start.8 = (s16[136,512]{1,0:T(8,128)(2,1)S(1)}, s16[136,512]{1,0:T(8,128)(2,1)S(1)}, u32[]{:S(2)}, u32[]{:S(2)}) collective-permute-start(s16[136,512]{1,0:T(8,128)(2,1)S(1)} %get-tuple-element.23), channel_id=1, source_target_pairs={{0,3},{1,2},{2,1},{3,0},{4,7},{5,6},{6,5},{7,4},{8,11},{9,10},{10,... | collective-permute-start | bytes 417800 | tf_op jit(solution)/shard_map/ppermute | solution.py:83
  43.0 9.6 %collective-permute-start.9 = (s16[136,512]{1,0:T(8,128)(2,1)S(1)}, s16[136,512]{1,0:T(8,128)(2,1)S(1)}, u32[]{:S(2)}, u32[]{:S(2)}) collective-permute-start(s16[136,512]{1,0:T(8,128)(2,1)S(1)} %get-tuple-element.26), channel_id=1, source_target_pairs={{0,8},{1,9},{2,10},{3,11},{4,12},{5,13},{6,14},{7,15},{8,0},{9,1},... | collective-permute-start | bytes 417800 | tf_op jit(solution)/shard_map/ppermute | solution.py:83
  45.5 13.5 %collective-permute-start.10 = (s16[136,512]{1,0:T(8,128)(2,1)S(1)}, s16[136,512]{1,0:T(8,128)(2,1)S(1)}, u32[]{:S(2)}, u32[]{:S(2)}) collective-permute-start(s16[136,512]{1,0:T(8,128)(2,1)S(1)} %get-tuple-element.27), channel_id=1, source_target_pairs={{0,16},{1,17},{2,18},{3,19},{4,20},{5,21},{6,22},{7,23},{8,24},{9,... | collective-permute-start | bytes 417800 | tf_op jit(solution)/shard_map/ppermute | solution.py:83
  48.1 10.9 %collective-permute-start.11 = (s16[136,512]{1,0:T(8,128)(2,1)S(1)}, s16[136,512]{1,0:T(8,128)(2,1)S(1)}, u32[]{:S(2)}, u32[]{:S(2)}) collective-permute-start(s16[136,512]{1,0:T(8,128)(2,1)S(1)} %get-tuple-element.28), channel_id=1, source_target_pairs={{0,24},{1,25},{2,26},{3,27},{4,28},{5,29},{6,30},{7,31},{8,16},{9,... | collective-permute-start | bytes 417800 | tf_op jit(solution)/shard_map/ppermute | solution.py:83

commit v2 on v1

--- a/solution.py
+++ b/solution.py
@@ -3,6 +3,10 @@
 import jax
 import jax.numpy as jnp
 from jax import lax
+from jax.experimental import pallas as pl
+from jax.experimental.pallas import tpu as pltpu
+from jax.experimental import pallas as pl
+from jax.experimental.pallas import tpu as pltpu
 from jax.experimental import pallas as pl
 from jax.experimental.pallas import tpu as pltpu
 from jax.experimental import pallas as pl
@@ -23,6 +27,8 @@
 FULL = 32700.0
 LEAST = -112.0 * FINE
 SCALE_ROWS = 8
+LANES = 128
+LANES = 128
 LANES = 128
 LANES = 128
 LANES = 128
@@ -181,12 +187,22 @@
             out_ref[...] += terms
 
 
+def cut_kernel(actuators_ref, out_ref, sem):
+    half = out_ref.shape[0]
+    start = actuators_ref.shape[0] - LMAX + half * (lax.axis_index("lag") % 2)
+    copy = pltpu.make_async_copy(actuators_ref.at[pl.ds(pl.multiple_of(start, 8), half), :], out_ref, sem)
+    copy.start()
+    copy.wait()
+
+
 def outer_kernel(
-    runs_ref, offsets_ref, mine_ref, theirs_ref, actuators_ref, sensors_ref, inner_ref, *refs
+    runs_ref, offsets_ref, mine_ref, theirs_ref, actuators_ref, sensors_ref, inner_ref,
+    near_ref, near_own_ref, far_own_ref, *refs
 ):
     chunk, lags, segs = LMAX, lax.axis_size("lag"), lax.axis_size("seg")
-    sends, keeps, own_ref = refs[:lags], (None,) + refs[lags : 2 * lags - 1], refs[2 * lags - 1]
-    runs, offsets, held, sensed, turned, masked, terms, sems = refs[2 * lags :]
+    far = segs // 2
+    far_refs = (None,) + refs[: far - 1]
+    runs, offsets, held, sensed, turned, masked, terms, sems = refs[far - 1 :]
     samples, actuators = actuators_ref.shape
     here = pl.ds(0, chunk)
     copies = [
@@ -198,7 +214,7 @@
     for copy in copies:
         copy.start()
     seg, lag = lax.axis_index("seg"), lax.axis_index("lag")
-    rows, far, half = actuators // segs, segs // 2, chunk // 2
+    rows, half = actuators // segs, chunk // 2
     core = lag % 2
     turned[:, pl.ds(pl.multiple_of(core * half, LANES), half)] = mine_ref[...].T
     turned[:, pl.ds(pl.multiple_of((1 - core) * half, LANES), half)] = theirs_ref[...].T
@@ -210,74 +226,102 @@
     copies[3].wait()
     terms[...] = inner_ref[...] + jnp.dot(masked[...], sensed[...], preferred_element_type=jnp.float32)
 
-    def half_of(step, near):
-        return [
-            terms[pl.ds(pl.multiple_of(step * actuators + (2 * block + near) * rows, rows), rows), :]
-            for block in range(far)
+    near_at, far_at = seg % 2, seg // 2
+
+    def block_of(step, block, near, count):
+        start = step * actuators + (2 * block + near) * rows
+        return terms[pl.ds(pl.multiple_of(start, rows), count), :]
+
+    codes = []
+    for step in range(1, lags):
+        parts = [block_of(step, block, 1 - near_at, rows) for block in range(far)]
+        codes.append(put(near_ref, (step - 1) * far * rows, parts))
+        for block in range(far):
+            near_own_ref[pl.ds(((step - 1) * far + block) * rows, rows), :] = block_of(step, block, near_at, rows)
+    put_codes(near_ref, (lags - 1) * far * rows, codes)
+    for bits in range(1, far):
+        code = put(far_refs[bits], 0, [block_of(0, far_at ^ bits, 0, 2 * rows)])
+        put_codes(far_refs[bits], 2 * rows, [code])
+    far_own_ref[...] = block_of(0, far_at, 0, 2 * rows)
+
+
+def put(ref, at, parts):
+    largest = jnp.abs(parts[0])
+    for part in parts[1:]:
+        largest = jnp.maximum(largest, jnp.abs(part))
+    code = column_code(jnp.max(largest, axis=0, keepdims=True))
+    for part in parts:
+        ref[pl.ds(at, part.shape[0]), :] = coded(part, code)
+        at += part.shape[0]
+    return code
+
+
+def put_codes(ref, at, codes):
+    shape = (SCALE_ROWS, codes[0].shape[1])
+    sublane = lax.broadcasted_iota(jnp.int32, shape, 0)
+    rows = jnp.broadcast_to(codes[0].astype(jnp.int32), shape)
+    for row in range(1, len(codes)):
+        rows = jnp.where(sublane == row, jnp.broadcast_to(codes[row].astype(jnp.int32), shape), rows)
+    ref[pl.ds(at, SCALE_ROWS), :] = rows.astype(jnp.int16)
+
+
+def second_kernel(came_ref, near_own_ref, far_own_ref, *refs):
+    lags, segs = lax.axis_size("lag"), lax.axis_size("seg")
+    far, others = segs // 2, lags - 1
+    came_far = (None,) + refs[: far - 1]
+    total_ref, own_ref, near_ref = refs[far - 1 : far + 2]
+    far_refs = (None,) + refs[far + 2 :]
+    rows = own_ref.shape[0]
+    near_at, far_at = lax.axis_index("seg") % 2, lax.axis_index("seg") // 2
+    came_codes = codes_of(came_ref, others * far * rows)
+
+    def block_sum(step, block):
+        here = pl.ds(pl.multiple_of((step * far + block) * rows, rows), rows)
+        return near_own_ref[here, :] + decoded(came_ref[here, :], came_codes[step : step + 1])
+
+    for bits in range(far - 1, 0, -1):
+        codes = [
+            put(far_refs[bits], step * rows, [block_sum(step, far_at ^ bits)]) for step in range(others)
         ]
-
-    def send(step, near, ref):
-        parts = half_of(step, near)
-        largest = jnp.abs(parts[0])
-        for part in parts[1:]:
-            largest = jnp.maximum(largest, jnp.abs(part))
-        code = column_code(jnp.max(largest, axis=0, keepdims=True))
-        for block, part in enumerate(parts):
-            ref[pl.ds(block * rows, rows), :] = coded(part, code)
-        ref[pl.ds(far * rows, SCALE_ROWS), :] = jnp.broadcast_to(
-            code.astype(jnp.int32), (SCALE_ROWS, code.shape[1])
-        ).astype(jnp.int16)
-
-    near_at = seg % 2
-    for step in range(lags):
-        send(step, 1 - near_at, sends[step])
-        if step:
-            send(step, near_at, keeps[step])
-        else:
-            for block, part in enumerate(half_of(step, near_at)):
-                own_ref[pl.ds(block * rows, rows), :] = part
-
-
-def middle_kernel(*refs):
+        put_codes(far_refs[bits], others * rows, codes)
+    far_codes = [None] + [codes_of(ref, 2 * rows)[:1] for ref in came_far[1:]]
+
+    def near_sum(near):
+        here = pl.ds(pl.multiple_of(near * rows, rows), rows)
+        value = far_own_ref[here, :]
+        for bits in range(1, far):
+            value = value + decoded(came_far[bits][here, :], far_codes[bits])
+        return value
+
+    put_codes(near_ref, rows, [put(near_ref, 0, [near_sum(1 - near_at)])])
+    own_ref[...] = near_sum(near_at)
+    for step in range(others):
+        total_ref[pl.ds(step * rows, rows), :] = block_sum(step, far_at)
+
+
+def third_kernel(total_ref, *refs):
     lags, segs = lax.axis_size("lag"), lax.axis_size("seg")
     far = segs // 2
-    came, kept, own_ref = refs[:lags], (None,) + refs[lags : 2 * lags - 1], refs[2 * lags - 1]
-    total_ref, sends = refs[2 * lags], refs[2 * lags + 1 :]
-    rows = total_ref.shape[0] // lags
-    far_at = lax.axis_index("seg") // 2
-    came_codes = [codes_of(ref, far * rows)[:1] for ref in came]
-    kept_codes = [None] + [codes_of(ref, far * rows)[:1] for ref in kept[1:]]
-
-    def block_sum(step, block):
-        here = pl.ds(pl.multiple_of(block * rows, rows), rows)
-        first = own_ref[here, :] if step == 0 else decoded(kept[step][here, :], kept_codes[step])
-        return first + decoded(came[step][here, :], came_codes[step])
-
-    for step in range(lags):
-        total_ref[pl.ds(step * rows, rows), :] = block_sum(step, far_at)
-    sublane = lax.broadcasted_iota(jnp.int32, (SCALE_ROWS, total_ref.shape[1]), 0)
-    for bits in range(1, far):
-        codes = jnp.zeros(sublane.shape, jnp.int32)
-        for step in range(lags):
-            part = block_sum(step, far_at ^ bits)
-            code = column_code(jnp.max(jnp.abs(part), axis=0, keepdims=True))
-            sends[bits - 1][pl.ds(step * rows, rows), :] = coded(part, code)
-            codes = jnp.where(sublane == step, jnp.broadcast_to(code.astype(jnp.int32), sublane.shape), codes)
-        sends[bits - 1][pl.ds(lags * rows, SCALE_ROWS), :] = codes.astype(jnp.int16)
-
-
-def last_kernel(scaling, total_ref, *refs):
-    lags = lax.axis_size("lag")
-    came, out_ref = refs[:-1], refs[-1]
-    rows = total_ref.shape[0] // lags
-    width = total_ref.shape[1]
-    lag = lax.axis_index("lag")
-    codes = [codes_of(ref, lags * rows) for ref in came]
-    for step in range(lags):
+    came, sends = refs[: far - 1], refs[far - 1 :]
+    rows = total_ref.shape[0] // (lags - 1)
+    codes = [codes_of(ref, (lags - 1) * rows) for ref in came]
+    for step in range(lags - 1):
         here = pl.ds(step * rows, rows)
         value = total_ref[here, :]
         for ref, code in zip(came, codes):
             value = value + decoded(ref[here, :], code[step : step + 1])
+        put_codes(sends[step], rows, [put(sends[step], 0, [value])])
+
+
+def last_kernel(scaling, own_ref, near_ref, *refs):
+    came, out_ref = (None,) + refs[:-1], refs[-1]
+    rows, width = own_ref.shape
+    lag = lax.axis_index("lag")
+    for step in range(len(came)):
+        ref = came[step] if step else near_ref
+        value = decoded(ref[pl.ds(0, rows), :], codes_of(ref, rows)[:1])
+        if step == 0:
+            value = value + own_ref[...]
         out_ref[:, 0, pl.ds(pl.multiple_of((lag ^ step) * width, LANES), width)] = value * scaling
 
 
@@ -287,21 +331,37 @@
     segs, lags = lax.axis_size("seg"), lax.axis_size("lag")
     far, rows, chunk = segs // 2, actuators // segs, LMAX
     scaling = 1.0 / math.sqrt(samples * segs)
-    lag = lax.axis_index("lag")
     spare = lags * actuators
-    payload = jax.ShapeDtypeStruct((far * rows + SCALE_ROWS, sensors), jnp.int16)
-    onward = jax.ShapeDtypeStruct((lags * rows + SCALE_ROWS, sensors), jnp.int16)
+    others = lags - 1
+
+    def payload(count):
+        return jax.ShapeDtypeStruct((count * rows + SCALE_ROWS, sensors), jnp.int16)
+
+    def wide(count):
+        return jax.ShapeDtypeStruct((count * rows, sensors), jnp.float32)
+
     vmem = pl.BlockSpec(memory_space=pltpu.VMEM)
-    half = LMAX // 2
-    core = lag % 2
-    fetched = shifted_by(
-        lax.dynamic_slice_in_dim(actuator_input, samples - LMAX + half * core, half, 0), "seg", 1
-    )
-    others = exchange(fetched, 0, 1)
-
+    small = pltpu.CompilerParams(vmem_limit_bytes=8 << 20)
     hbm = pl.BlockSpec(memory_space=pltpu.HBM)
     scalars = [pltpu.SMEM(run_lengths.shape, jnp.int32), pltpu.SMEM(lag_offsets.shape, jnp.int32)]
     chunks = samples // chunk
+    run_lengths, lag_offsets, actuator_input, sensor_output = (
+        pltpu.with_memory_space_constraint(value, pltpu.HBM)
+        for value in (run_lengths, lag_offsets, actuator_input, sensor_output)
+    )
+
+    cut = pl.pallas_call(
+        cut_kernel,
+        in_specs=[hbm],
+        out_specs=vmem,
+        out_shape=jax.ShapeDtypeStruct((LMAX // 2, actuators), jnp.bfloat16),
+        scratch_shapes=[pltpu.SemaphoreType.DMA],
+        compiler_params=small,
+        name="cut",
+    )(actuator_input)
+    fetched = shifted_by(cut, "seg", 1)
+    swapped = exchange(fetched, 0, 1)
+
     inner = pl.pallas_call(
         inner_kernel,
         in_specs=[hbm] * 4,
@@ -325,8 +385,8 @@
     packed = pl.pallas_call(
         outer_kernel,
         in_specs=[hbm] * 2 + [vmem] * 2 + [hbm] * 2 + [vmem],
-        out_specs=[vmem] * (2 * lags),
-        out_shape=[payload] * (2 * lags - 1) + [jax.ShapeDtypeStruct((far * rows, sensors), jnp.float32)],
+        out_specs=[vmem] * (far + 2),
+        out_shape=[payload(others * far), wide(others * far), wide(2)] + [payload(2)] * (far - 1),
         scratch_shapes=scalars
         + [
             pltpu.VMEM((chunk, actuators), jnp.bfloat16),
@@ -341,39 +401,42 @@
             flops=2 * spare * sensors * chunk, bytes_accessed=6 << 20, transcendentals=0
         ),
         name="outer",
-    )(run_lengths, lag_offsets, fetched, others, actuator_input, sensor_output, inner)
-
-    came, kept = [None] * lags, [None] * lags
-    for place in range(lags // 2):
-        low, high = (place + 1) % (lags // 2), lags // 2 + place
-        came[low] = exchange(packed[low], 1, low)
-        kept[high] = exchange(packed[lags + high - 1], 0, high)
-        came[high] = exchange(packed[high], 1, high)
-    for step in range(1, lags // 2):
-        kept[step] = exchange(packed[lags + step - 1], 0, step)
-
-    middle = pl.pallas_call(
-        middle_kernel,
-        in_specs=[vmem] * (2 * lags),
-        out_specs=[vmem] * far,
-        out_shape=[jax.ShapeDtypeStruct((lags * rows, sensors), jnp.float32)] + [onward] * (far - 1),
-        compiler_params=pltpu.CompilerParams(vmem_limit_bytes=8 << 20),
-        name="middle",
-    )(*came, *kept[1:], packed[-1])
-
-    arrived = [exchange(middle[bits], 2 * bits, 0) for bits in range(far - 1, 0, -1)][::-1]
+    )(run_lengths, lag_offsets, fetched, swapped, actuator_input, sensor_output, inner)
+
+    masks = range(far - 1, 0, -1)
+    came = exchange(packed[0], 1, 0)
+    came_far = [exchange(packed[2 + bits], 2 * bits, 0) for bits in masks][::-1]
+    second = pl.pallas_call(
+        second_kernel,
+        in_specs=[vmem] * (far + 2),
+        out_specs=[vmem] * (far + 2),
+        out_shape=[wide(others), wide(1), payload(1)] + [payload(others)] * (far - 1),
+        compiler_params=small,
+        name="second",
+    )(came, packed[1], packed[2], *came_far)
+    came_far = [exchange(second[2 + bits], 2 * bits, 0) for bits in masks][::-1]
+    near = exchange(second[2], 1, 0)
+    third = pl.pallas_call(
+        third_kernel,
+        in_specs=[vmem] * far,
+        out_specs=[vmem] * others,
+        out_shape=[payload(1)] * others,
+        compiler_params=small,
+        name="third",
+    )(second[0], *came_far)
+    came = [exchange(third[step - 1], 0, step) for step in range(others, 0, -1)][::-1]
 
     def last_body(*refs):
         return last_kernel(scaling, *refs)
 
     return pl.pallas_call(
         last_body,
-        in_specs=[vmem] * far,
+        in_specs=[vmem] * (2 + others),
         out_specs=vmem,
         out_shape=jax.ShapeDtypeStruct((rows, 1, lags * sensors), jnp.float32),
-        compiler_params=pltpu.CompilerParams(vmem_limit_bytes=8 << 20),
+        compiler_params=small,
         name="last",
-    )(middle[0], *arrived)
+    )(second[1], near, *came)
 
 
 def solution(mesh):
@@ -404,3 +467,5 @@
     return mapped
     return mapped
     return mapped
+    return mapped
+    return mapped

time: 60.1 us -> 53.5 us (0.89)
  waiting for transfers between devices: 27.9 us -> 22.1 us
  local copies, waits for them, and re-layouts: 3.68 us -> 0 us
  Pallas kernels: 9.38 us -> 11.5 us
  starting transfers between devices: 18.9 us -> 19.6 us
    ppermute x11 -> x12, waiting for transfers between devices: 22.3 us -> 16.6 us  [exchange(): return lax.ppermute(value, ('seg', 'lag'), pairs)]
    unnamed x6 -> x0, local copies, waits for them, and re-layouts: 2.72 us -> none
    dynamic_slice x1 -> x0, local copies, waits for them, and re-layouts: 0.97 us -> none  [per_device_staged(): lax.dynamic_slice_in_dim(actuator_input, samples - LMAX + half * core, ha...]
    pallas_call x2 -> x4, Pallas kernels: 1.35 us -> 2.27 us  [the longest x1 0.96 us: per_device_staged(): pl.pallas_call(cut_kernel, in_specs=[hbm], out_specs=vmem, out_shape=jax....]
    ppermute x11 -> x12, starting transfers between devices: 14 us -> 14.7 us  [exchange(): return lax.ppermute(value, ('seg', 'lag'), pairs)]
    pallas_call x1, Pallas kernels: 4.86 us -> 5.56 us  [per_device_staged(): pl.pallas_call(inner_kernel, in_specs=[hbm] * 4, out_specs=vmem, out_shap...]
  transfers between devices with their start and end apart: 12 -> 13, of which waited for: 9 -> 5; matrix products, arithmetic and copies ran while one was open for 0% -> 0% of each run, Pallas kernels for 8% -> 11%
where the time goes in v2:
time: 53.5 us; the launch traced here: 53.3 us
  waiting for transfers between devices  22.1 us (41%)
  starting transfers between devices  19.6 us (37%)
  Pallas kernels  11.5 us (21%)
    ppermute x12, waiting for transfers between devices, exchange(): return lax.ppermute(value, ('seg', 'lag'), pairs)  16.6 us
    ppermute x12, starting transfers between devices, exchange(): return lax.ppermute(value, ('seg', 'lag'), pairs)  14.7 us
    pallas_call x1, Pallas kernels, per_device_staged(): pl.pallas_call(inner_kernel, in_specs=[hbm] * 4, out_specs=vmem, out_shap...  5.56 us
    ppermute x1, waiting for transfers between devices, shifted_by(): lax.ppermute(value, axis, [(source, source + steps) for source in range(i...  5.53 us
    ppermute x1, starting transfers between devices, shifted_by(): lax.ppermute(value, axis, [(source, source + steps) for source in range(i...  4.89 us
    pallas_call x1, Pallas kernels, per_device_staged(): pl.pallas_call(outer_kernel, in_specs=[hbm] * 2 + [vmem] * 2 + [hbm] * 2...  3.66 us
  transfers between devices with their start and end apart: 13, of which 5 were waited for; matrix products, arithmetic and copies ran while one was open for 0% of the time, Pallas kernels for 11%

profile of v2, /device:TPU:0, one launch (start us, length us, event | category | flops | bytes accessed | tf_op | source)
XLA Modules:
  0.0 53.3 jit_solution(12659078777621147562)
XLA Ops:
  0.0 1.0 %cut.1 = bf16[512,256]{1,0:T(8,128)(2,1)S(1)} custom-call(bf16[3072,256]{1,0:T(8,128)(2,1)} %actuators_ref.5), custom_call_target="tpu_custom_call" | custom-call | tf_op jit(solution)/shard_map/cut/pallas_call | solution.py:353
  1.0 4.9 %collective-permute-start = (bf16[512,256]{1,0:T(8,128)(2,1)S(1)}, bf16[512,256]{1,0:T(8,128)(2,1)S(1)}, u32[]{:S(2)}, u32[]{:S(2)}) collective-permute-start(bf16[512,256]{1,0:T(8,128)(2,1)S(1)} %cut.1), channel_id=1, source_target_pairs={{0,4},{4,8},{8,12},{12,16},{16,20},{20,24},{24,28},{1,5},{5,9},{9,... | collective-permute-start | bytes 786440 | tf_op jit(solution)/shard_map/ppermute | solution.py:42
  5.9 5.5 %collective-permute-done.mine_ref = bf16[512,256]{1,0:T(8,128)(2,1)S(1)} collective-permute-done((bf16[512,256]{1,0:T(8,128)(2,1)S(1)}, bf16[512,256]{1,0:T(8,128)(2,1)S(1)}, u32[]{:S(2)}, u32[]{:S(2)}) %collective-permute-start) | collective-permute-done | bytes 262176 | tf_op jit(solution)/shard_map/ppermute | solution.py:42
  11.4 0.0 collective-permute-start.1
  11.4 5.6 %inner.1.inner_ref = f32[1024,512]{1,0:T(8,128)S(1)} custom-call(s32[4]{0:T(128)} %runs_ref.3, s32[2]{0:T(128)} %offsets_ref.3, bf16[3072,256]{1,0:T(8,128)(2,1)} %actuators_ref.5, bf16[3072,512]{1,0:T(8,128)(2,1)} %sensors_ref.3), custom_call_target="tpu_custom_call" | custom-call | flops 2147483648 | bytes 6291456 | tf_op jit(solution)/shard_map/inner/pallas_call | solution.py:365
  17.0 0.0 collective-permute-done.1.theirs_ref
  17.0 3.7 %outer.1 = (s16[392,512]{1,0:T(8,128)(2,1)S(1)}, f32[384,512]{1,0:T(8,128)S(1)}, f32[64,512]{1,0:T(8,128)S(1)}, s16[72,512]{1,0:T(8,128)(2,1)S(1)}, s16[72,512]{...) custom-call(s32[4]{0:T(128)} %runs_ref.3, s32[2]{0:T(128)} %offsets_ref.3, ...), custom_call_target="tpu_custom_call" | custom-call | flops 1073741824 | bytes 6291456 | tf_op jit(solution)/shard_map/outer/pallas_call | solution.py:385
  20.6 2.6 %collective-permute-start.2 = (s16[392,512]{1,0:T(8,128)(2,1)S(1)}, s16[392,512]{1,0:T(8,128)(2,1)S(1)}, u32[]{:S(2)}, u32[]{:S(2)}) collective-permute-start(s16[392,512]{1,0:T(8,128)(2,1)S(1)} %get-tuple-element.20), channel_id=1, source_target_pairs={{0,4},{1,5},{2,6},{3,7},{4,0},{5,1},{6,2},{7,3},{8,12},{9,13},{10,... | collective-permute-start | bytes 1204232 | tf_op jit(solution)/shard_map/ppermute | solution.py:89
  23.2 1.6 %collective-permute-start.3 = (s16[72,512]{1,0:T(8,128)(2,1)S(1)}, s16[72,512]{1,0:T(8,128)(2,1)S(1)}, u32[]{:S(2)}, u32[]{:S(2)}) collective-permute-start(s16[72,512]{1,0:T(8,128)(2,1)S(1)} %get-tuple-element.23), channel_id=1, source_target_pairs={{0,8},{1,9},{2,10},{3,11},{4,12},{5,13},{6,14},{7,15},{8,0},{9,1},... | collective-permute-start | bytes 221192 | tf_op jit(solution)/shard_map/ppermute | solution.py:89
  24.8 2.6 %collective-permute-start.4 = (s16[72,512]{1,0:T(8,128)(2,1)S(1)}, s16[72,512]{1,0:T(8,128)(2,1)S(1)}, u32[]{:S(2)}, u32[]{:S(2)}) collective-permute-start(s16[72,512]{1,0:T(8,128)(2,1)S(1)} %get-tuple-element.24), channel_id=1, source_target_pairs={{0,16},{1,17},{2,18},{3,19},{4,20},{5,21},{6,22},{7,23},{8,24},{9,... | collective-permute-start | bytes 221192 | tf_op jit(solution)/shard_map/ppermute | solution.py:89
  27.4 0.2 collective-permute-start.5
  27.6 0.0 collective-permute-done.3.refs_0_
  27.6 6.1 %collective-permute-done.4.refs_1_ = s16[72,512]{1,0:T(8,128)(2,1)S(1)} collective-permute-done((s16[72,512]{1,0:T(8,128)(2,1)S(1)}, s16[72,512]{1,0:T(8,128)(2,1)S(1)}, u32[]{:S(2)}, u32[]{:S(2)}) %collective-permute-start.4) | collective-permute-done | bytes 73760 | tf_op jit(solution)/shard_map/ppermute | solution.py:89
  33.7 0.0 collective-permute-done.5.refs_2_
  33.7 0.0 collective-permute-done.2.came_ref
  33.7 0.4 second.1
  34.0 2.3 %collective-permute-start.7 = (s16[104,512]{1,0:T(8,128)(2,1)S(1)}, s16[104,512]{1,0:T(8,128)(2,1)S(1)}, u32[]{:S(2)}, u32[]{:S(2)}) collective-permute-start(s16[104,512]{1,0:T(8,128)(2,1)S(1)} %get-tuple-element.29), channel_id=1, source_target_pairs={{0,8},{1,9},{2,10},{3,11},{4,12},{5,13},{6,14},{7,15},{8,0},{9,1},... | collective-permute-start | bytes 319496 | tf_op jit(solution)/shard_map/ppermute | solution.py:89
  36.3 2.6 %collective-permute-start.8 = (s16[104,512]{1,0:T(8,128)(2,1)S(1)}, s16[104,512]{1,0:T(8,128)(2,1)S(1)}, u32[]{:S(2)}, u32[]{:S(2)}) collective-permute-start(s16[104,512]{1,0:T(8,128)(2,1)S(1)} %get-tuple-element.30), channel_id=1, source_target_pairs={{0,16},{1,17},{2,18},{3,19},{4,20},{5,21},{6,22},{7,23},{8,24},{9,... | collective-permute-start | bytes 319496 | tf_op jit(solution)/shard_map/ppermute | solution.py:89
  38.9 0.0 collective-permute-start.9
  38.9 1.0 %collective-permute-start.6 = (s16[40,512]{1,0:T(8,128)(2,1)S(1)}, s16[40,512]{1,0:T(8,128)(2,1)S(1)}, u32[]{:S(2)}, u32[]{:S(2)}) collective-permute-start(s16[40,512]{1,0:T(8,128)(2,1)S(1)} %get-tuple-element.27), channel_id=1, source_target_pairs={{0,4},{1,5},{2,6},{3,7},{4,0},{5,1},{6,2},{7,3},{8,12},{9,13},{10,... | collective-permute-start | bytes 122888 | tf_op jit(solution)/shard_map/ppermute | solution.py:89
  39.9 0.0 collective-permute-done.7.refs_0_
  39.9 7.3 %collective-permute-done.8.refs_1_ = s16[104,512]{1,0:T(8,128)(2,1)S(1)} collective-permute-done((s16[104,512]{1,0:T(8,128)(2,1)S(1)}, s16[104,512]{1,0:T(8,128)(2,1)S(1)}, u32[]{:S(2)}, u32[]{:S(2)}) %collective-permute-start.8) | collective-permute-done | bytes 106528 | tf_op jit(solution)/shard_map/ppermute | solution.py:89
  47.2 0.0 collective-permute-done.9.refs_2_
  47.2 0.2 third.1
  47.3 0.1 collective-permute-start.10
  47.4 1.6 %collective-permute-start.11 = (s16[40,512]{1,0:T(8,128)(2,1)S(1)}, s16[40,512]{1,0:T(8,128)(2,1)S(1)}, u32[]{:S(2)}, u32[]{:S(2)}) collective-permute-start(s16[40,512]{1,0:T(8,128)(2,1)S(1)} %get-tuple-element.33), channel_id=1, source_target_pairs={{0,2},{1,3},{2,0},{3,1},{4,6},{5,7},{6,4},{7,5},{8,10},{9,11},{10,... | collective-permute-start | bytes 122888 | tf_op jit(solution)/shard_map/ppermute | solution.py:89
  49.0 0.3 collective-permute-start.12
  49.3 0.0 collective-permute-done.6.refs_1_
  49.3 0.0 collective-permute-done.10.refs_2_
  49.3 2.2 %collective-permute-done.11.refs_3_ = s16[40,512]{1,0:T(8,128)(2,1)S(1)} collective-permute-done((s16[40,512]{1,0:T(8,128)(2,1)S(1)}, s16[40,512]{1,0:T(8,128)(2,1)S(1)}, u32[]{:S(2)}, u32[]{:S(2)}) %collective-permute-start.11) | collective-permute-done | bytes 40992 | tf_op jit(solution)/shard_map/ppermute | solution.py:89
  51.5 1.0 %collective-permute-done.12.refs_4_ = s16[40,512]{1,0:T(8,128)(2,1)S(1)} collective-permute-done((s16[40,512]{1,0:T(8,128)(2,1)S(1)}, s16[40,512]{1,0:T(8,128)(2,1)S(1)}, u32[]{:S(2)}, u32[]{:S(2)}) %collective-permute-start.12) | collective-permute-done | bytes 40992 | tf_op jit(solution)/shard_map/ppermute | solution.py:89
  52.5 0.8 %last.1 = f32[32,1,2048]{2,1,0:T(1,128)} custom-call(f32[32,512]{1,0:T(8,128)S(1)} %get-tuple-element.26.refs_0_, s16[40,512]{1,0:T(8,128)(2,1)S(1)} %collective-permute-done.6.refs_1_, s16[40,512]{1,0:T(8,128)(2,1)S(1)} %collective-permute-done.10.refs_2_, s16[40,512]{1,0:T(8,128)(2,1)S(1)} %collective-permute-done.11.refs_3_, ...), custom_call_target="tpu_custom_call" | custom-call | tf_op jit(solution)/shard_map/last/pallas_call | solution.py:432
Async XLA Ops:
  1.0 10.4 %collective-permute-start = (bf16[512,256]{1,0:T(8,128)(2,1)S(1)}, bf16[512,256]{1,0:T(8,128)(2,1)S(1)}, u32[]{:S(2)}, u32[]{:S(2)}) collective-permute-start(bf16[512,256]{1,0:T(8,128)(2,1)S(1)} %cut.1), channel_id=1, source_target_pairs={{0,4},{4,8},{8,12},{12,16},{16,20},{20,24},{24,28},{1,5},{5,9},{9,... | collective-permute-start | bytes 786440 | tf_op jit(solution)/shard_map/ppermute | solution.py:42
  11.4 5.6 %collective-permute-start.1 = (bf16[512,256]{1,0:T(8,128)(2,1)S(1)}, bf16[512,256]{1,0:T(8,128)(2,1)S(1)}, u32[]{:S(2)}, u32[]{:S(2)}) collective-permute-start(bf16[512,256]{1,0:T(8,128)(2,1)S(1)} %collective-permute-done.mine_ref), channel_id=1, source_target_pairs={{0,1},{1,0},{2,3},{3,2},{4,5},{5,4},{6,7},{7,6},{8,9},{9,8},{10,11... | collective-permute-start | bytes 786440 | tf_op jit(solution)/shard_map/ppermute | solution.py:89
  20.6 13.0 %collective-permute-start.2 = (s16[392,512]{1,0:T(8,128)(2,1)S(1)}, s16[392,512]{1,0:T(8,128)(2,1)S(1)}, u32[]{:S(2)}, u32[]{:S(2)}) collective-permute-start(s16[392,512]{1,0:T(8,128)(2,1)S(1)} %get-tuple-element.20), channel_id=1, source_target_pairs={{0,4},{1,5},{2,6},{3,7},{4,0},{5,1},{6,2},{7,3},{8,12},{9,13},{10,... | collective-permute-start | bytes 1204232 | tf_op jit(solution)/shard_map/ppermute | solution.py:89
  23.2 4.4 %collective-permute-start.3 = (s16[72,512]{1,0:T(8,128)(2,1)S(1)}, s16[72,512]{1,0:T(8,128)(2,1)S(1)}, u32[]{:S(2)}, u32[]{:S(2)}) collective-permute-start(s16[72,512]{1,0:T(8,128)(2,1)S(1)} %get-tuple-element.23), channel_id=1, source_target_pairs={{0,8},{1,9},{2,10},{3,11},{4,12},{5,13},{6,14},{7,15},{8,0},{9,1},... | collective-permute-start | bytes 221192 | tf_op jit(solution)/shard_map/ppermute | solution.py:89
  24.8 8.9 %collective-permute-start.4 = (s16[72,512]{1,0:T(8,128)(2,1)S(1)}, s16[72,512]{1,0:T(8,128)(2,1)S(1)}, u32[]{:S(2)}, u32[]{:S(2)}) collective-permute-start(s16[72,512]{1,0:T(8,128)(2,1)S(1)} %get-tuple-element.24), channel_id=1, source_target_pairs={{0,16},{1,17},{2,18},{3,19},{4,20},{5,21},{6,22},{7,23},{8,24},{9,... | collective-permute-start | bytes 221192 | tf_op jit(solution)/shard_map/ppermute | solution.py:89
  27.4 6.3 %collective-permute-start.5 = (s16[72,512]{1,0:T(8,128)(2,1)S(1)}, s16[72,512]{1,0:T(8,128)(2,1)S(1)}, u32[]{:S(2)}, u32[]{:S(2)}) collective-permute-start(s16[72,512]{1,0:T(8,128)(2,1)S(1)} %get-tuple-element.25), channel_id=1, source_target_pairs={{0,24},{1,25},{2,26},{3,27},{4,28},{5,29},{6,30},{7,31},{8,16},{9,... | collective-permute-start | bytes 221192 | tf_op jit(solution)/shard_map/ppermute | solution.py:89
  34.0 5.9 %collective-permute-start.7 = (s16[104,512]{1,0:T(8,128)(2,1)S(1)}, s16[104,512]{1,0:T(8,128)(2,1)S(1)}, u32[]{:S(2)}, u32[]{:S(2)}) collective-permute-start(s16[104,512]{1,0:T(8,128)(2,1)S(1)} %get-tuple-element.29), channel_id=1, source_target_pairs={{0,8},{1,9},{2,10},{3,11},{4,12},{5,13},{6,14},{7,15},{8,0},{9,1},... | collective-permute-start | bytes 319496 | tf_op jit(solution)/shard_map/ppermute | solution.py:89
  36.3 10.9 %collective-permute-start.8 = (s16[104,512]{1,0:T(8,128)(2,1)S(1)}, s16[104,512]{1,0:T(8,128)(2,1)S(1)}, u32[]{:S(2)}, u32[]{:S(2)}) collective-permute-start(s16[104,512]{1,0:T(8,128)(2,1)S(1)} %get-tuple-element.30), channel_id=1, source_target_pairs={{0,16},{1,17},{2,18},{3,19},{4,20},{5,21},{6,22},{7,23},{8,24},{9,... | collective-permute-start | bytes 319496 | tf_op jit(solution)/shard_map/ppermute | solution.py:89
  38.9 8.3 %collective-permute-start.9 = (s16[104,512]{1,0:T(8,128)(2,1)S(1)}, s16[104,512]{1,0:T(8,128)(2,1)S(1)}, u32[]{:S(2)}, u32[]{:S(2)}) collective-permute-start(s16[104,512]{1,0:T(8,128)(2,1)S(1)} %get-tuple-element.31), channel_id=1, source_target_pairs={{0,24},{1,25},{2,26},{3,27},{4,28},{5,29},{6,30},{7,31},{8,16},{9,... | collective-permute-start | bytes 319496 | tf_op jit(solution)/shard_map/ppermute | solution.py:89
  38.9 10.4 %collective-permute-start.6 = (s16[40,512]{1,0:T(8,128)(2,1)S(1)}, s16[40,512]{1,0:T(8,128)(2,1)S(1)}, u32[]{:S(2)}, u32[]{:S(2)}) collective-permute-start(s16[40,512]{1,0:T(8,128)(2,1)S(1)} %get-tuple-element.27), channel_id=1, source_target_pairs={{0,4},{1,5},{2,6},{3,7},{4,0},{5,1},{6,2},{7,3},{8,12},{9,13},{10,... | collective-permute-start | bytes 122888 | tf_op jit(solution)/shard_map/ppermute | solution.py:89
  47.3 1.9 %collective-permute-start.10 = (s16[40,512]{1,0:T(8,128)(2,1)S(1)}, s16[40,512]{1,0:T(8,128)(2,1)S(1)}, u32[]{:S(2)}, u32[]{:S(2)}) collective-permute-start(s16[40,512]{1,0:T(8,128)(2,1)S(1)} %get-tuple-element.32), channel_id=1, source_target_pairs={{0,1},{1,0},{2,3},{3,2},{4,5},{5,4},{6,7},{7,6},{8,9},{9,8},{10,11... | collective-permute-start | bytes 122888 | tf_op jit(solution)/shard_map/ppermute | solution.py:89
  47.4 4.1 %collective-permute-start.11 = (s16[40,512]{1,0:T(8,128)(2,1)S(1)}, s16[40,512]{1,0:T(8,128)(2,1)S(1)}, u32[]{:S(2)}, u32[]{:S(2)}) collective-permute-start(s16[40,512]{1,0:T(8,128)(2,1)S(1)} %get-tuple-element.33), channel_id=1, source_target_pairs={{0,2},{1,3},{2,0},{3,1},{4,6},{5,7},{6,4},{7,5},{8,10},{9,11},{10,... | collective-permute-start | bytes 122888 | tf_op jit(solution)/shard_map/ppermute | solution.py:89
  49.0 3.5 %collective-permute-start.12 = (s16[40,512]{1,0:T(8,128)(2,1)S(1)}, s16[40,512]{1,0:T(8,128)(2,1)S(1)}, u32[]{:S(2)}, u32[]{:S(2)}) collective-permute-start(s16[40,512]{1,0:T(8,128)(2,1)S(1)} %get-tuple-element.34), channel_id=1, source_target_pairs={{0,3},{1,2},{2,1},{3,0},{4,7},{5,6},{6,5},{7,4},{8,11},{9,10},{10,... | collective-permute-start | bytes 122888 | tf_op jit(solution)/shard_map/ppermute | solution.py:89

commit v3 on v2

--- a/solution.py
+++ b/solution.py
@@ -110,7 +110,7 @@
     return offsets_ref[which // LBW] + which % LBW
 
 
-def fill_rows(turned, at_lane, masked, at_masked, runs, offsets, lag, lags, start_row, chunk):
+def fill_rows(turned, at_lane, masked, at_masked, runs, offsets, lag, steps, start_row, chunk):
     actuators = turned.shape[0]
     tiles = chunk // LANES
     lane = lax.broadcasted_iota(jnp.int32, (1, LANES), 1)
@@ -118,7 +118,7 @@
     for run in range(runs.shape[0]):
         end = end + runs[run]
         ends.append(end)
-    for step in range(lags):
+    for number, step in enumerate(steps):
         shift = lag_of(offsets, lag ^ step)
         at = at_lane - shift
         base, turn = at // LANES, at % LANES
@@ -139,11 +139,12 @@
             keep = jnp.broadcast_to(crossed == 0, (actuators, LANES))
             value = jnp.where(low, pieces[tile], pieces[tile + 1])
             value = jnp.where(keep, value, jnp.zeros_like(value))
-            masked[pl.ds(step * actuators, actuators), pl.ds(at_masked + tile * LANES, LANES)] = value
+            masked[pl.ds(number * actuators, actuators), pl.ds(at_masked + tile * LANES, LANES)] = value
 
 
 def inner_kernel(
-    runs_ref, offsets_ref, actuators_ref, sensors_ref, out_ref, runs, offsets, held, sensed, turned, masked, sems
+    runs_ref, offsets_ref, actuators_ref, sensors_ref, out_ref, first_turned_ref, first_sensed_ref,
+    runs, offsets, held, sensed, turned, masked, sems
 ):
     chunk, lags = LMAX, lax.axis_size("lag")
     samples, _ = actuators_ref.shape
@@ -163,6 +164,9 @@
                 sems.at[1 + chunks + at],
             )
         )
+    copies.append(
+        pltpu.make_async_copy(sensors_ref.at[pl.ds(0, chunk), :], first_sensed_ref, sems.at[1 + 2 * chunks])
+    )
     for copy in copies:
         copy.start()
     start_row = lax.axis_index("seg") * samples
@@ -171,12 +175,13 @@
         here = pl.ds(at * chunk, chunk)
         turned[:, here] = held[here, :].T
         if at == 0:
+            first_turned_ref[...] = turned[:, here]
             copies[0].wait()
             copies[1].wait()
             continue
         fill_rows(
             turned, at * chunk, masked, (at - 1) * chunk, runs, offsets,
-            lax.axis_index("lag"), lags, start_row + at * chunk, chunk,
+            lax.axis_index("lag"), range(lags), start_row + at * chunk, chunk,
         )
         copies[1 + chunks + at].wait()
         there = pl.ds((at - 1) * chunk, chunk)
@@ -185,6 +190,7 @@
             out_ref[...] = terms
         else:
             out_ref[...] += terms
+    copies[-1].wait()
 
 
 def cut_kernel(actuators_ref, out_ref, sem):
@@ -196,20 +202,14 @@
 
 
 def outer_kernel(
-    runs_ref, offsets_ref, mine_ref, theirs_ref, actuators_ref, sensors_ref, inner_ref,
-    near_ref, near_own_ref, far_own_ref, *refs
+    steps, samples, runs_ref, offsets_ref, mine_ref, theirs_ref, first_turned_ref, sensed_ref, inner_ref,
+    near_ref, own_ref, runs, offsets, turned, masked, terms, sems
 ):
-    chunk, lags, segs = LMAX, lax.axis_size("lag"), lax.axis_size("seg")
-    far = segs // 2
-    far_refs = (None,) + refs[: far - 1]
-    runs, offsets, held, sensed, turned, masked, terms, sems = refs[far - 1 :]
-    samples, actuators = actuators_ref.shape
-    here = pl.ds(0, chunk)
+    chunk, segs = LMAX, lax.axis_size("seg")
+    far, actuators = segs // 2, inner_ref.shape[0] // lax.axis_size("lag")
     copies = [
-        pltpu.make_async_copy(actuators_ref.at[here, :], held, sems.at[2]),
         pltpu.make_async_copy(runs_ref, runs, sems.at[0]),
         pltpu.make_async_copy(offsets_ref, offsets, sems.at[1]),
-        pltpu.make_async_copy(sensors_ref.at[here, :], sensed, sems.at[3]),
     ]
     for copy in copies:
         copy.start()
@@ -218,31 +218,28 @@
     core = lag % 2
     turned[:, pl.ds(pl.multiple_of(core * half, LANES), half)] = mine_ref[...].T
     turned[:, pl.ds(pl.multiple_of((1 - core) * half, LANES), half)] = theirs_ref[...].T
-    copies[0].wait()
-    turned[:, pl.ds(chunk, chunk)] = held[...].T
-    copies[1].wait()
-    copies[2].wait()
-    fill_rows(turned, chunk, masked, 0, runs, offsets, lag, lags, seg * samples, chunk)
-    copies[3].wait()
-    terms[...] = inner_ref[...] + jnp.dot(masked[...], sensed[...], preferred_element_type=jnp.float32)
-
-    near_at, far_at = seg % 2, seg // 2
-
-    def block_of(step, block, near, count):
-        start = step * actuators + (2 * block + near) * rows
-        return terms[pl.ds(pl.multiple_of(start, rows), count), :]
+    turned[:, pl.ds(chunk, chunk)] = first_turned_ref[...]
+    for copy in copies:
+        copy.wait()
+    fill_rows(turned, chunk, masked, 0, runs, offsets, lag, steps, seg * samples, chunk)
+    for number, step in enumerate(steps):
+        here = pl.ds(number * actuators, actuators)
+        terms[here, :] = inner_ref[pl.ds(step * actuators, actuators), :]
+    terms[...] += jnp.dot(masked[...], sensed_ref[...], preferred_element_type=jnp.float32)
+
+    near_at = seg % 2
+
+    def block_of(number, block, near):
+        start = number * actuators + (2 * block + near) * rows
+        return terms[pl.ds(pl.multiple_of(start, rows), rows), :]
 
     codes = []
-    for step in range(1, lags):
-        parts = [block_of(step, block, 1 - near_at, rows) for block in range(far)]
-        codes.append(put(near_ref, (step - 1) * far * rows, parts))
+    for number in range(len(steps)):
+        parts = [block_of(number, block, 1 - near_at) for block in range(far)]
+        codes.append(put(near_ref, number * far * rows, parts))
         for block in range(far):
-            near_own_ref[pl.ds(((step - 1) * far + block) * rows, rows), :] = block_of(step, block, near_at, rows)
-    put_codes(near_ref, (lags - 1) * far * rows, codes)
-    for bits in range(1, far):
-        code = put(far_refs[bits], 0, [block_of(0, far_at ^ bits, 0, 2 * rows)])
-        put_codes(far_refs[bits], 2 * rows, [code])
-    far_own_ref[...] = block_of(0, far_at, 0, 2 * rows)
+            own_ref[pl.ds((number * far + block) * rows, rows), :] = block_of(number, block, near_at)
+    put_codes(near_ref, len(steps) * far * rows, codes)
 
 
 def put(ref, at, parts):
@@ -265,63 +262,51 @@
     ref[pl.ds(at, SCALE_ROWS), :] = rows.astype(jnp.int16)
 
 
-def second_kernel(came_ref, near_own_ref, far_own_ref, *refs):
-    lags, segs = lax.axis_size("lag"), lax.axis_size("seg")
-    far, others = segs // 2, lags - 1
-    came_far = (None,) + refs[: far - 1]
-    total_ref, own_ref, near_ref = refs[far - 1 : far + 2]
-    far_refs = (None,) + refs[far + 2 :]
-    rows = own_ref.shape[0]
-    near_at, far_at = lax.axis_index("seg") % 2, lax.axis_index("seg") // 2
-    came_codes = codes_of(came_ref, others * far * rows)
-
-    def block_sum(step, block):
-        here = pl.ds(pl.multiple_of((step * far + block) * rows, rows), rows)
-        return near_own_ref[here, :] + decoded(came_ref[here, :], came_codes[step : step + 1])
+def second_kernel(count, came_ref, own_ref, total_ref, *far_refs):
+    far = lax.axis_size("seg") // 2
+    far_refs = (None,) + far_refs
+    rows = total_ref.shape[0] // count
+    far_at = lax.axis_index("seg") // 2
+    codes_came = codes_of(came_ref, count * far * rows)
+
+    def block_sum(number, block):
+        here = pl.ds(pl.multiple_of((number * far + block) * rows, rows), rows)
+        return own_ref[here, :] + decoded(came_ref[here, :], codes_came[number : number + 1])
 
     for bits in range(far - 1, 0, -1):
         codes = [
-            put(far_refs[bits], step * rows, [block_sum(step, far_at ^ bits)]) for step in range(others)
+            put(far_refs[bits], number * rows, [block_sum(number, far_at ^ bits)]) for number in range(count)
         ]
-        put_codes(far_refs[bits], others * rows, codes)
-    far_codes = [None] + [codes_of(ref, 2 * rows)[:1] for ref in came_far[1:]]
-
-    def near_sum(near):
-        here = pl.ds(pl.multiple_of(near * rows, rows), rows)
-        value = far_own_ref[here, :]
-        for bits in range(1, far):
-            value = value + decoded(came_far[bits][here, :], far_codes[bits])
-        return value
-
-    put_codes(near_ref, rows, [put(near_ref, 0, [near_sum(1 - near_at)])])
-    own_ref[...] = near_sum(near_at)
-    for step in range(others):
-        total_ref[pl.ds(step * rows, rows), :] = block_sum(step, far_at)
-
-
-def third_kernel(total_ref, *refs):
-    lags, segs = lax.axis_size("lag"), lax.axis_size("seg")
-    far = segs // 2
-    came, sends = refs[: far - 1], refs[far - 1 :]
-    rows = total_ref.shape[0] // (lags - 1)
-    codes = [codes_of(ref, (lags - 1) * rows) for ref in came]
-    for step in range(lags - 1):
-        here = pl.ds(step * rows, rows)
+        put_codes(far_refs[bits], count * rows, codes)
+    for number in range(count):
+        total_ref[pl.ds(number * rows, rows), :] = block_sum(number, far_at)
+
+
+def third_kernel(steps, total_ref, *refs):
+    far = lax.axis_size("seg") // 2
+    came, outs = refs[: far - 1], refs[far - 1 :]
+    rows = total_ref.shape[0] // len(steps)
+    codes = [codes_of(ref, len(steps) * rows) for ref in came]
+    for number, step in enumerate(steps):
+        here = pl.ds(number * rows, rows)
         value = total_ref[here, :]
         for ref, code in zip(came, codes):
-            value = value + decoded(ref[here, :], code[step : step + 1])
-        put_codes(sends[step], rows, [put(sends[step], 0, [value])])
-
-
-def last_kernel(scaling, own_ref, near_ref, *refs):
+            value = value + decoded(ref[here, :], code[number : number + 1])
+        if step:
+            put_codes(outs[number], rows, [put(outs[number], 0, [value])])
+        else:
+            outs[number][...] = value
+
+
+def last_kernel(scaling, own_ref, *refs):
     came, out_ref = (None,) + refs[:-1], refs[-1]
     rows, width = own_ref.shape
     lag = lax.axis_index("lag")
     for step in range(len(came)):
-        ref = came[step] if step else near_ref
-        value = decoded(ref[pl.ds(0, rows), :], codes_of(ref, rows)[:1])
-        if step == 0:
-            value = value + own_ref[...]
+        if step:
+            value = decoded(came[step][pl.ds(0, rows), :], codes_of(came[step], rows)[:1])
+        else:
+            value = own_ref[...]
         out_ref[:, 0, pl.ds(pl.multiple_of((lag ^ step) * width, LANES), width)] = value * scaling
 
 
@@ -332,7 +317,6 @@
     far, rows, chunk = segs // 2, actuators // segs, LMAX
     scaling = 1.0 / math.sqrt(samples * segs)
     spare = lags * actuators
-    others = lags - 1
 
     def payload(count):
         return jax.ShapeDtypeStruct((count * rows + SCALE_ROWS, sensors), jnp.int16)
@@ -362,81 +346,107 @@
     fetched = shifted_by(cut, "seg", 1)
     swapped = exchange(fetched, 0, 1)
 
-    inner = pl.pallas_call(
+    inner, first_turned, first_sensed = pl.pallas_call(
         inner_kernel,
         in_specs=[hbm] * 4,
-        out_specs=vmem,
-        out_shape=jax.ShapeDtypeStruct((spare, sensors), jnp.float32),
+        out_specs=[vmem] * 3,
+        out_shape=[
+            jax.ShapeDtypeStruct((spare, sensors), jnp.float32),
+            jax.ShapeDtypeStruct((actuators, chunk), jnp.bfloat16),
+            jax.ShapeDtypeStruct((chunk, sensors), jnp.bfloat16),
+        ],
         scratch_shapes=scalars
         + [
             pltpu.VMEM((samples, actuators), jnp.bfloat16),
             pltpu.VMEM((samples - chunk, sensors), jnp.bfloat16),
             pltpu.VMEM((actuators, samples + LANES), jnp.bfloat16),
             pltpu.VMEM((spare, samples - chunk), jnp.bfloat16),
-            pltpu.SemaphoreType.DMA((1 + 2 * chunks,)),
+            pltpu.SemaphoreType.DMA((2 + 2 * chunks,)),
         ],
-        compiler_params=pltpu.CompilerParams(vmem_limit_bytes=48 << 20),
+        compiler_params=pltpu.CompilerParams(vmem_limit_bytes=40 << 20),
         cost_estimate=pl.CostEstimate(
             flops=2 * spare * sensors * (samples - chunk), bytes_accessed=6 << 20, transcendentals=0
         ),
         name="inner",
     )(run_lengths, lag_offsets, actuator_input, sensor_output)
 
-    packed = pl.pallas_call(
-        outer_kernel,
-        in_specs=[hbm] * 2 + [vmem] * 2 + [hbm] * 2 + [vmem],
-        out_specs=[vmem] * (far + 2),
-        out_shape=[payload(others * far), wide(others * far), wide(2)] + [payload(2)] * (far - 1),
-        scratch_shapes=scalars
-        + [
-            pltpu.VMEM((chunk, actuators), jnp.bfloat16),
-            pltpu.VMEM((chunk, sensors), jnp.bfloat16),
-            pltpu.VMEM((actuators, 2 * chunk + LANES), jnp.bfloat16),
-            pltpu.VMEM((spare, chunk), jnp.bfloat16),
-            pltpu.VMEM((spare, sensors), jnp.float32),
-            pltpu.SemaphoreType.DMA((4,)),
-        ],
-        compiler_params=pltpu.CompilerParams(vmem_limit_bytes=48 << 20),
-        cost_estimate=pl.CostEstimate(
-            flops=2 * spare * sensors * chunk, bytes_accessed=6 << 20, transcendentals=0
-        ),
-        name="outer",
-    )(run_lengths, lag_offsets, fetched, swapped, actuator_input, sensor_output, inner)
+    def outer(name, steps):
+        def body(*refs):
+            outer_kernel(steps, samples, *refs)
+
+        return pl.pallas_call(
+            body,
+            in_specs=[hbm] * 2 + [vmem] * 5,
+            out_specs=[vmem] * 2,
+            out_shape=[payload(len(steps) * far), wide(len(steps) * far)],
+            scratch_shapes=scalars
+            + [
+                pltpu.VMEM((actuators, 2 * chunk + LANES), jnp.bfloat16),
+                pltpu.VMEM((len(steps) * actuators, chunk), jnp.bfloat16),
+                pltpu.VMEM((len(steps) * actuators, sensors), jnp.float32),
+                pltpu.SemaphoreType.DMA((2,)),
+            ],
+            compiler_params=pltpu.CompilerParams(vmem_limit_bytes=24 << 20),
+            cost_estimate=pl.CostEstimate(
+                flops=2 * len(steps) * actuators * sensors * chunk, bytes_accessed=4 << 20, transcendentals=0
+            ),
+            name=name,
+        )(run_lengths, lag_offsets, fetched, swapped, first_turned, first_sensed, inner)
+
+    def second(name, steps, came, own):
+        def body(*refs):
+            second_kernel(len(steps), *refs)
+
+        return pl.pallas_call(
+            body,
+            in_specs=[vmem] * 2,
+            out_specs=[vmem] * far,
+            out_shape=[wide(len(steps))] + [payload(len(steps))] * (far - 1),
+            compiler_params=small,
+            cost_estimate=pl.CostEstimate(flops=1 << 20, bytes_accessed=2 << 20, transcendentals=0),
+            name=name,
+        )(came, own)
+
+    def third(name, steps, total, *came):
+        def body(*refs):
+            third_kernel(steps, *refs)
+
+        return pl.pallas_call(
+            body,
+            in_specs=[vmem] * far,
+            out_specs=[vmem] * len(steps),
+            out_shape=[payload(1) if step else wide(1) for step in steps],
+            compiler_params=small,
+            cost_estimate=pl.CostEstimate(flops=1 << 20, bytes_accessed=1 << 20, transcendentals=0),
+            name=name,
+        )(total, *came)
 
     masks = range(far - 1, 0, -1)
-    came = exchange(packed[0], 1, 0)
-    came_far = [exchange(packed[2 + bits], 2 * bits, 0) for bits in masks][::-1]
-    second = pl.pallas_call(
-        second_kernel,
-        in_specs=[vmem] * (far + 2),
-        out_specs=[vmem] * (far + 2),
-        out_shape=[wide(others), wide(1), payload(1)] + [payload(others)] * (far - 1),
-        compiler_params=small,
-        name="second",
-    )(came, packed[1], packed[2], *came_far)
-    came_far = [exchange(second[2 + bits], 2 * bits, 0) for bits in masks][::-1]
-    near = exchange(second[2], 1, 0)
-    third = pl.pallas_call(
-        third_kernel,
-        in_specs=[vmem] * far,
-        out_specs=[vmem] * others,
-        out_shape=[payload(1)] * others,
-        compiler_params=small,
-        name="third",
-    )(second[0], *came_far)
-    came = [exchange(third[step - 1], 0, step) for step in range(others, 0, -1)][::-1]
+    groups = (tuple(range(lags - 1, lags // 2 - 1, -1)), tuple(range(lags // 2 - 1, -1, -1)))
+    names = ("a", "b")
+    near, kept, total, ended = {}, {}, {}, {}
+    for name, steps in zip(names, groups):
+        send, kept[name] = outer("outer_" + name, steps)
+        near[name] = exchange(send, 1, 0)
+    for name, steps in zip(names, groups):
+        total[name], *sends = second("second_" + name, steps, near[name], kept[name])
+        near[name] = [exchange(sends[bits - 1], 2 * bits, 0) for bits in masks][::-1]
+    for name, steps in zip(names, groups):
+        outs = third("third_" + name, steps, total[name], *near[name])
+        for step, out in zip(steps, outs):
+            ended[step] = exchange(out, 0, step) if step else out
 
     def last_body(*refs):
         return last_kernel(scaling, *refs)
 
     return pl.pallas_call(
         last_body,
-        in_specs=[vmem] * (2 + others),
+        in_specs=[vmem] * lags,
         out_specs=vmem,
         out_shape=jax.ShapeDtypeStruct((rows, 1, lags * sensors), jnp.float32),
         compiler_params=small,
         name="last",
-    )(second[1], near, *came)
+    )(*[ended[step] for step in range(lags)])
 
 
 def solution(mesh):

time: 53.5 us -> 48.6 us (0.908)
  waiting for transfers between devices: 22.1 us -> 16 us
  starting transfers between devices: 19.6 us -> 21 us
    ppermute x12, waiting for transfers between devices: 16.6 us -> 10.5 us  [exchange(): return lax.ppermute(value, ('seg', 'lag'), pairs)]
    ppermute x12, starting transfers between devices: 14.7 us -> 16.1 us  [exchange(): return lax.ppermute(value, ('seg', 'lag'), pairs)]
    pallas_call x5 -> x8, Pallas kernels: 10.5 us -> 10.4 us  [the longest x1 5.6 us: per_device_staged(): pl.pallas_call(inner_kernel, in_specs=[hbm] * 4, out_specs=[vmem] * 3, ou...]
  transfers between devices with their start and end apart: 13 -> 13, of which waited for: 5 -> 4; matrix products, arithmetic and copies ran while one was open for 0% -> 0% of each run, Pallas kernels for 11% -> 16%
where the time goes in v3:
time: 48.6 us; the launch traced here: 48.4 us
  starting transfers between devices  21 us (43%)
  waiting for transfers between devices  16 us (33%)
  Pallas kernels  11.3 us (23%)
    ppermute x12, starting transfers between devices, exchange(): return lax.ppermute(value, ('seg', 'lag'), pairs)  16.1 us
    ppermute x12, waiting for transfers between devices, exchange(): return lax.ppermute(value, ('seg', 'lag'), pairs)  10.5 us
    pallas_call x1, Pallas kernels, per_device_staged(): pl.pallas_call(inner_kernel, in_specs=[hbm] * 4, out_specs=[vmem] * 3, ou...  5.6 us
    ppermute x1, waiting for transfers between devices, shifted_by(): lax.ppermute(value, axis, [(source, source + steps) for source in range(i...  5.53 us
    ppermute x1, starting transfers between devices, shifted_by(): lax.ppermute(value, axis, [(source, source + steps) for source in range(i...  4.89 us
    pallas_call x2, Pallas kernels, outer(): pl.pallas_call(body, in_specs=[hbm] * 2 + [vmem] * 5, out_specs=[vmem] *...  3.42 us
  transfers between devices with their start and end apart: 13, of which 4 were waited for; matrix products, arithmetic and copies ran while one was open for 0% of the time, Pallas kernels for 16%

profile of v3, /device:TPU:0, one launch (start us, length us, event | category | flops | bytes accessed | tf_op | source)
XLA Modules:
  0.0 48.4 jit_solution(10045883469635910155)
XLA Ops:
  0.0 1.0 %cut.1 = bf16[512,256]{1,0:T(8,128)(2,1)S(1)} custom-call(bf16[3072,256]{1,0:T(8,128)(2,1)} %actuators_ref.3), custom_call_target="tpu_custom_call" | custom-call | tf_op jit(solution)/shard_map/cut/pallas_call | solution.py:337
  1.0 4.9 %collective-permute-start = (bf16[512,256]{1,0:T(8,128)(2,1)S(1)}, bf16[512,256]{1,0:T(8,128)(2,1)S(1)}, u32[]{:S(2)}, u32[]{:S(2)}) collective-permute-start(bf16[512,256]{1,0:T(8,128)(2,1)S(1)} %cut.1), channel_id=1, source_target_pairs={{0,4},{4,8},{8,12},{12,16},{16,20},{20,24},{24,28},{1,5},{5,9},{9,... | collective-permute-start | bytes 786440 | tf_op jit(solution)/shard_map/ppermute | solution.py:42
  5.9 5.5 %collective-permute-done.refs_2_ = bf16[512,256]{1,0:T(8,128)(2,1)S(1)} collective-permute-done((bf16[512,256]{1,0:T(8,128)(2,1)S(1)}, bf16[512,256]{1,0:T(8,128)(2,1)S(1)}, u32[]{:S(2)}, u32[]{:S(2)}) %collective-permute-start) | collective-permute-done | bytes 262176 | tf_op jit(solution)/shard_map/ppermute | solution.py:42
  11.4 0.0 collective-permute-start.1
  11.4 5.6 %inner.1 = (f32[1024,512]{1,0:T(8,128)S(1)}, bf16[256,1024]{1,0:T(8,128)(2,1)S(1)}, bf16[1024,512]{1,0:T(8,128)(2,1)S(1)}) custom-call(s32[4]{0:T(128)} %refs_0_.3, s32[2]{0:T(128)} %refs_1_.3, bf16[3072,256]{1,0:T(8,128)(2,1)} %actuators_ref.3, bf16[3072,512]{1,0:T(8,128)(2,1)} %sensors_ref.1), custom_call_target="tpu_custom_call" | custom-call | flops 2147483648 | bytes 6291456 | tf_op jit(solution)/shard_map/inner/pallas_call | solution.py:349
  17.0 0.0 collective-permute-done.1.refs_3_
  17.0 1.7 %outer_a.1 = (s16[264,512]{1,0:T(8,128)(2,1)S(1)}, f32[256,512]{1,0:T(8,128)S(1)}) custom-call(s32[4]{0:T(128)} %refs_0_.3, s32[2]{0:T(128)} %refs_1_.3, bf16[512,256]{1,0:T(8,128)(2,1)S(1)} %collective-permute-done.refs_2_, bf16[512,256]{1,0:T(8,128)(2,1)S(1)} %collective-permute-done.1.refs_3_, bf16[256,1024]{1,0:T(8,128)(2,1)S(1)} %get-tuple-element.24.refs_4_, ...), custom_call_target="tpu_custom_call" | custom-call | flops 536870912 | bytes 4194304 | tf_op jit(solution)/shard_map/outer_a/pallas_call | solution.py:377
  18.7 2.5 %collective-permute-start.7 = (s16[264,512]{1,0:T(8,128)(2,1)S(1)}, s16[264,512]{1,0:T(8,128)(2,1)S(1)}, u32[]{:S(2)}, u32[]{:S(2)}) collective-permute-start(s16[264,512]{1,0:T(8,128)(2,1)S(1)} %get-tuple-element.35), channel_id=1, source_target_pairs={{0,4},{1,5},{2,6},{3,7},{4,0},{5,1},{6,2},{7,3},{8,12},{9,13},{10,... | collective-permute-start | bytes 811016 | tf_op jit(solution)/shard_map/ppermute | solution.py:89
  21.3 1.7 %outer_b.1 = (s16[264,512]{1,0:T(8,128)(2,1)S(1)}, f32[256,512]{1,0:T(8,128)S(1)}) custom-call(s32[4]{0:T(128)} %refs_0_.3, s32[2]{0:T(128)} %refs_1_.3, bf16[512,256]{1,0:T(8,128)(2,1)S(1)} %collective-permute-done.refs_2_, bf16[512,256]{1,0:T(8,128)(2,1)S(1)} %collective-permute-done.1.refs_3_, bf16[256,1024]{1,0:T(8,128)(2,1)S(1)} %get-tuple-element.24.refs_4_, ...), custom_call_target="tpu_custom_call" | custom-call | flops 536870912 | bytes 4194304 | tf_op jit(solution)/shard_map/outer_b/pallas_call | solution.py:377
  23.0 0.1 collective-permute-start.2
  23.1 5.5 %collective-permute-done.7.refs_0_ = s16[264,512]{1,0:T(8,128)(2,1)S(1)} collective-permute-done((s16[264,512]{1,0:T(8,128)(2,1)S(1)}, s16[264,512]{1,0:T(8,128)(2,1)S(1)}, u32[]{:S(2)}, u32[]{:S(2)}) %collective-permute-start.7) | collective-permute-done | bytes 270368 | tf_op jit(solution)/shard_map/ppermute | solution.py:89
  28.6 0.2 second_a.1
  28.8 5.1 %collective-permute-start.10 = (s16[72,512]{1,0:T(8,128)(2,1)S(1)}, s16[72,512]{1,0:T(8,128)(2,1)S(1)}, u32[]{:S(2)}, u32[]{:S(2)}) collective-permute-start(s16[72,512]{1,0:T(8,128)(2,1)S(1)} %get-tuple-element.40), channel_id=1, source_target_pairs={{0,24},{1,25},{2,26},{3,27},{4,28},{5,29},{6,30},{7,31},{8,16},{9,... | collective-permute-start | bytes 221192 | tf_op jit(solution)/shard_map/ppermute | solution.py:89
  33.9 0.0 collective-permute-start.8
  33.9 0.6 %collective-permute-start.9 = (s16[72,512]{1,0:T(8,128)(2,1)S(1)}, s16[72,512]{1,0:T(8,128)(2,1)S(1)}, u32[]{:S(2)}, u32[]{:S(2)}) collective-permute-start(s16[72,512]{1,0:T(8,128)(2,1)S(1)} %get-tuple-element.39), channel_id=1, source_target_pairs={{0,16},{1,17},{2,18},{3,19},{4,20},{5,21},{6,22},{7,23},{8,24},{9,... | collective-permute-start | bytes 221192 | tf_op jit(solution)/shard_map/ppermute | solution.py:89
  34.5 0.0 collective-permute-done.2.refs_0_
  34.5 0.2 second_b.1
  34.7 2.5 %collective-permute-start.3 = (s16[72,512]{1,0:T(8,128)(2,1)S(1)}, s16[72,512]{1,0:T(8,128)(2,1)S(1)}, u32[]{:S(2)}, u32[]{:S(2)}) collective-permute-start(s16[72,512]{1,0:T(8,128)(2,1)S(1)} %get-tuple-element.30), channel_id=1, source_target_pairs={{0,8},{1,9},{2,10},{3,11},{4,12},{5,13},{6,14},{7,15},{8,0},{9,1},... | collective-permute-start | bytes 221192 | tf_op jit(solution)/shard_map/ppermute | solution.py:89
  37.2 2.6 %collective-permute-start.4 = (s16[72,512]{1,0:T(8,128)(2,1)S(1)}, s16[72,512]{1,0:T(8,128)(2,1)S(1)}, u32[]{:S(2)}, u32[]{:S(2)}) collective-permute-start(s16[72,512]{1,0:T(8,128)(2,1)S(1)} %get-tuple-element.31), channel_id=1, source_target_pairs={{0,16},{1,17},{2,18},{3,19},{4,20},{5,21},{6,22},{7,23},{8,24},{9,... | collective-permute-start | bytes 221192 | tf_op jit(solution)/shard_map/ppermute | solution.py:89
  39.8 0.0 collective-permute-done.10.refs_3_
  39.8 0.9 %collective-permute-start.5 = (s16[72,512]{1,0:T(8,128)(2,1)S(1)}, s16[72,512]{1,0:T(8,128)(2,1)S(1)}, u32[]{:S(2)}, u32[]{:S(2)}) collective-permute-start(s16[72,512]{1,0:T(8,128)(2,1)S(1)} %get-tuple-element.32), channel_id=1, source_target_pairs={{0,24},{1,25},{2,26},{3,27},{4,28},{5,29},{6,30},{7,31},{8,16},{9,... | collective-permute-start | bytes 221192 | tf_op jit(solution)/shard_map/ppermute | solution.py:89
  40.7 0.0 collective-permute-done.8.refs_1_
  40.7 0.0 collective-permute-done.9.refs_2_
  40.7 0.1 third_a.1
  40.9 1.6 %collective-permute-start.11 = (s16[40,512]{1,0:T(8,128)(2,1)S(1)}, s16[40,512]{1,0:T(8,128)(2,1)S(1)}, u32[]{:S(2)}, u32[]{:S(2)}) collective-permute-start(s16[40,512]{1,0:T(8,128)(2,1)S(1)} %get-tuple-element.41), channel_id=1, source_target_pairs={{0,2},{1,3},{2,0},{3,1},{4,6},{5,7},{6,4},{7,5},{8,10},{9,11},{10,... | collective-permute-start | bytes 122888 | tf_op jit(solution)/shard_map/ppermute | solution.py:89
  42.5 0.0 collective-permute-start.12
  42.5 0.0 collective-permute-done.3.refs_1_
  42.5 3.8 %collective-permute-done.4.refs_2_ = s16[72,512]{1,0:T(8,128)(2,1)S(1)} collective-permute-done((s16[72,512]{1,0:T(8,128)(2,1)S(1)}, s16[72,512]{1,0:T(8,128)(2,1)S(1)}, u32[]{:S(2)}, u32[]{:S(2)}) %collective-permute-start.4) | collective-permute-done | bytes 73760 | tf_op jit(solution)/shard_map/ppermute | solution.py:89
  46.2 0.0 collective-permute-done.5.refs_3_
  46.3 0.1 third_b.1
  46.3 0.1 collective-permute-start.6
  46.4 0.0 collective-permute-done.11.refs_2_
  46.4 0.0 collective-permute-done.12.refs_3_
  46.4 1.2 %collective-permute-done.6.refs_1_ = s16[40,512]{1,0:T(8,128)(2,1)S(1)} collective-permute-done((s16[40,512]{1,0:T(8,128)(2,1)S(1)}, s16[40,512]{1,0:T(8,128)(2,1)S(1)}, u32[]{:S(2)}, u32[]{:S(2)}) %collective-permute-start.6) | collective-permute-done | bytes 40992 | tf_op jit(solution)/shard_map/ppermute | solution.py:89
  47.6 0.8 %last.1 = f32[32,1,2048]{2,1,0:T(1,128)} custom-call(f32[32,512]{1,0:T(8,128)S(1)} %get-tuple-element.33.refs_0_, s16[40,512]{1,0:T(8,128)(2,1)S(1)} %collective-permute-done.6.refs_1_, s16[40,512]{1,0:T(8,128)(2,1)S(1)} %collective-permute-done.11.refs_2_, s16[40,512]{1,0:T(8,128)(2,1)S(1)} %collective-permute-done.12.refs_3_), custom_call_target="tpu_custom_call" | custom-call | tf_op jit(solution)/shard_map/last/pallas_call | solution.py:442
Async XLA Ops:
  1.0 10.4 %collective-permute-start = (bf16[512,256]{1,0:T(8,128)(2,1)S(1)}, bf16[512,256]{1,0:T(8,128)(2,1)S(1)}, u32[]{:S(2)}, u32[]{:S(2)}) collective-permute-start(bf16[512,256]{1,0:T(8,128)(2,1)S(1)} %cut.1), channel_id=1, source_target_pairs={{0,4},{4,8},{8,12},{12,16},{16,20},{20,24},{24,28},{1,5},{5,9},{9,... | collective-permute-start | bytes 786440 | tf_op jit(solution)/shard_map/ppermute | solution.py:42
  11.4 5.6 %collective-permute-start.1 = (bf16[512,256]{1,0:T(8,128)(2,1)S(1)}, bf16[512,256]{1,0:T(8,128)(2,1)S(1)}, u32[]{:S(2)}, u32[]{:S(2)}) collective-permute-start(bf16[512,256]{1,0:T(8,128)(2,1)S(1)} %collective-permute-done.refs_2_), channel_id=1, source_target_pairs={{0,1},{1,0},{2,3},{3,2},{4,5},{5,4},{6,7},{7,6},{8,9},{9,8},{10,11... | collective-permute-start | bytes 786440 | tf_op jit(solution)/shard_map/ppermute | solution.py:89
  18.7 9.9 %collective-permute-start.7 = (s16[264,512]{1,0:T(8,128)(2,1)S(1)}, s16[264,512]{1,0:T(8,128)(2,1)S(1)}, u32[]{:S(2)}, u32[]{:S(2)}) collective-permute-start(s16[264,512]{1,0:T(8,128)(2,1)S(1)} %get-tuple-element.35), channel_id=1, source_target_pairs={{0,4},{1,5},{2,6},{3,7},{4,0},{5,1},{6,2},{7,3},{8,12},{9,13},{10,... | collective-permute-start | bytes 811016 | tf_op jit(solution)/shard_map/ppermute | solution.py:89
  23.0 11.6 %collective-permute-start.2 = (s16[264,512]{1,0:T(8,128)(2,1)S(1)}, s16[264,512]{1,0:T(8,128)(2,1)S(1)}, u32[]{:S(2)}, u32[]{:S(2)}) collective-permute-start(s16[264,512]{1,0:T(8,128)(2,1)S(1)} %get-tuple-element.27), channel_id=1, source_target_pairs={{0,4},{1,5},{2,6},{3,7},{4,0},{5,1},{6,2},{7,3},{8,12},{9,13},{10,... | collective-permute-start | bytes 811016 | tf_op jit(solution)/shard_map/ppermute | solution.py:89
  28.8 11.0 %collective-permute-start.10 = (s16[72,512]{1,0:T(8,128)(2,1)S(1)}, s16[72,512]{1,0:T(8,128)(2,1)S(1)}, u32[]{:S(2)}, u32[]{:S(2)}) collective-permute-start(s16[72,512]{1,0:T(8,128)(2,1)S(1)} %get-tuple-element.40), channel_id=1, source_target_pairs={{0,24},{1,25},{2,26},{3,27},{4,28},{5,29},{6,30},{7,31},{8,16},{9,... | collective-permute-start | bytes 221192 | tf_op jit(solution)/shard_map/ppermute | solution.py:89
  33.9 6.8 %collective-permute-start.8 = (s16[72,512]{1,0:T(8,128)(2,1)S(1)}, s16[72,512]{1,0:T(8,128)(2,1)S(1)}, u32[]{:S(2)}, u32[]{:S(2)}) collective-permute-start(s16[72,512]{1,0:T(8,128)(2,1)S(1)} %get-tuple-element.38), channel_id=1, source_target_pairs={{0,8},{1,9},{2,10},{3,11},{4,12},{5,13},{6,14},{7,15},{8,0},{9,1},... | collective-permute-start | bytes 221192 | tf_op jit(solution)/shard_map/ppermute | solution.py:89
  33.9 6.8 %collective-permute-start.9 = (s16[72,512]{1,0:T(8,128)(2,1)S(1)}, s16[72,512]{1,0:T(8,128)(2,1)S(1)}, u32[]{:S(2)}, u32[]{:S(2)}) collective-permute-start(s16[72,512]{1,0:T(8,128)(2,1)S(1)} %get-tuple-element.39), channel_id=1, source_target_pairs={{0,16},{1,17},{2,18},{3,19},{4,20},{5,21},{6,22},{7,23},{8,24},{9,... | collective-permute-start | bytes 221192 | tf_op jit(solution)/shard_map/ppermute | solution.py:89
  34.7 7.8 %collective-permute-start.3 = (s16[72,512]{1,0:T(8,128)(2,1)S(1)}, s16[72,512]{1,0:T(8,128)(2,1)S(1)}, u32[]{:S(2)}, u32[]{:S(2)}) collective-permute-start(s16[72,512]{1,0:T(8,128)(2,1)S(1)} %get-tuple-element.30), channel_id=1, source_target_pairs={{0,8},{1,9},{2,10},{3,11},{4,12},{5,13},{6,14},{7,15},{8,0},{9,1},... | collective-permute-start | bytes 221192 | tf_op jit(solution)/shard_map/ppermute | solution.py:89
  37.2 9.0 %collective-permute-start.4 = (s16[72,512]{1,0:T(8,128)(2,1)S(1)}, s16[72,512]{1,0:T(8,128)(2,1)S(1)}, u32[]{:S(2)}, u32[]{:S(2)}) collective-permute-start(s16[72,512]{1,0:T(8,128)(2,1)S(1)} %get-tuple-element.31), channel_id=1, source_target_pairs={{0,16},{1,17},{2,18},{3,19},{4,20},{5,21},{6,22},{7,23},{8,24},{9,... | collective-permute-start | bytes 221192 | tf_op jit(solution)/shard_map/ppermute | solution.py:89
  39.8 6.5 %collective-permute-start.5 = (s16[72,512]{1,0:T(8,128)(2,1)S(1)}, s16[72,512]{1,0:T(8,128)(2,1)S(1)}, u32[]{:S(2)}, u32[]{:S(2)}) collective-permute-start(s16[72,512]{1,0:T(8,128)(2,1)S(1)} %get-tuple-element.32), channel_id=1, source_target_pairs={{0,24},{1,25},{2,26},{3,27},{4,28},{5,29},{6,30},{7,31},{8,16},{9,... | collective-permute-start | bytes 221192 | tf_op jit(solution)/shard_map/ppermute | solution.py:89
  40.9 5.6 %collective-permute-start.11 = (s16[40,512]{1,0:T(8,128)(2,1)S(1)}, s16[40,512]{1,0:T(8,128)(2,1)S(1)}, u32[]{:S(2)}, u32[]{:S(2)}) collective-permute-start(s16[40,512]{1,0:T(8,128)(2,1)S(1)} %get-tuple-element.41), channel_id=1, source_target_pairs={{0,2},{1,3},{2,0},{3,1},{4,6},{5,7},{6,4},{7,5},{8,10},{9,11},{10,... | collective-permute-start | bytes 122888 | tf_op jit(solution)/shard_map/ppermute | solution.py:89
  42.5 3.9 %collective-permute-start.12 = (s16[40,512]{1,0:T(8,128)(2,1)S(1)}, s16[40,512]{1,0:T(8,128)(2,1)S(1)}, u32[]{:S(2)}, u32[]{:S(2)}) collective-permute-start(s16[40,512]{1,0:T(8,128)(2,1)S(1)} %get-tuple-element.42), channel_id=1, source_target_pairs={{0,3},{1,2},{2,1},{3,0},{4,7},{5,6},{6,5},{7,4},{8,11},{9,10},{10,... | collective-permute-start | bytes 122888 | tf_op jit(solution)/shard_map/ppermute | solution.py:89
  46.3 1.3 %collective-permute-start.6 = (s16[40,512]{1,0:T(8,128)(2,1)S(1)}, s16[40,512]{1,0:T(8,128)(2,1)S(1)}, u32[]{:S(2)}, u32[]{:S(2)}) collective-permute-start(s16[40,512]{1,0:T(8,128)(2,1)S(1)} %get-tuple-element.34), channel_id=1, source_target_pairs={{0,1},{1,0},{2,3},{3,2},{4,5},{5,4},{6,7},{7,6},{8,9},{9,8},{10,11... | collective-permute-start | bytes 122888 | tf_op jit(solution)/shard_map/ppermute | solution.py:89

commit v4 on v3

--- a/solution.py
+++ b/solution.py
@@ -93,17 +93,51 @@
     return jnp.maximum(jnp.ceil(jnp.log2(largest) * FINE), LEAST)
 
 
-def coded(value, code):
-    held = jnp.round(value * (jnp.exp2(code * (-1.0 / FINE)) * FULL))
-    return held.astype(jnp.int32).astype(jnp.int16)
-
-
-def decoded(held, code):
-    return held.astype(jnp.float32) * (jnp.exp2(code * (1.0 / FINE)) * (1.0 / FULL))
-
-
-def codes_of(ref, at):
-    return ref[pl.ds(at, SCALE_ROWS), :].astype(jnp.int32).astype(jnp.float32)
+def scale_rows(count, width):
+    return -(-count * (width // LANES) // SCALE_ROWS) * SCALE_ROWS
+
+
+def put(ref, at, parts, stride):
+    largest = jnp.abs(parts[0])
+    for part in parts[1:]:
+        largest = jnp.maximum(largest, jnp.abs(part))
+    code = column_code(jnp.max(largest, axis=0, keepdims=True))
+    factor = jnp.exp2(code * (-1.0 / FINE)) * FULL
+    rows, width = parts[0].shape
+    for number, part in enumerate(parts):
+        held = jnp.round(part * factor).astype(jnp.int32).astype(jnp.int16)
+        for lanes in range(width // LANES):
+            ref[pl.ds(at + number * stride + lanes * rows, rows), :] = held[:, lanes * LANES : (lanes + 1) * LANES]
+    return code
+
+
+def put_codes(ref, at, codes):
+    width = codes[0].shape[1]
+    pieces = [code[:, start : start + LANES] for code in codes for start in range(0, width, LANES)]
+    count = scale_rows(len(codes), width)
+    shape = (count, LANES)
+    sublane = lax.broadcasted_iota(jnp.int32, shape, 0)
+    rows = jnp.broadcast_to(pieces[0].astype(jnp.int32), shape)
+    for row in range(1, len(pieces)):
+        rows = jnp.where(sublane == row, jnp.broadcast_to(pieces[row].astype(jnp.int32), shape), rows)
+    ref[pl.ds(at, count), :] = rows.astype(jnp.int16)
+
+
+def scales_of(ref, at, count, width):
+    codes = ref[pl.ds(at, scale_rows(count, width)), :].astype(jnp.int32).astype(jnp.float32)
+    return jnp.exp2(codes * (1.0 / FINE)) * (1.0 / FULL)
+
+
+def opened(ref, at, scales, number, rows, width):
+    lanes = width // LANES
+    return jnp.concatenate(
+        [
+            ref[pl.ds(at + block * rows, rows), :].astype(jnp.float32)
+            * scales[number * lanes + block : number * lanes + block + 1]
+            for block in range(lanes)
+        ],
+        axis=1,
+    )
 
 
 def lag_of(offsets_ref, which):
@@ -201,12 +235,12 @@
     copy.wait()
 
 
-def outer_kernel(
+def outer_terms(
     steps, samples, runs_ref, offsets_ref, mine_ref, theirs_ref, first_turned_ref, sensed_ref, inner_ref,
-    near_ref, own_ref, runs, offsets, turned, masked, terms, sems
+    runs, offsets, turned, masked, terms, sems
 ):
     chunk, segs = LMAX, lax.axis_size("seg")
-    far, actuators = segs // 2, inner_ref.shape[0] // lax.axis_size("lag")
+    actuators = inner_ref.shape[0] // lax.axis_size("lag")
     copies = [
         pltpu.make_async_copy(runs_ref, runs, sems.at[0]),
         pltpu.make_async_copy(offsets_ref, offsets, sems.at[1]),
@@ -227,87 +261,122 @@
         terms[here, :] = inner_ref[pl.ds(step * actuators, actuators), :]
     terms[...] += jnp.dot(masked[...], sensed_ref[...], preferred_element_type=jnp.float32)
 
-    near_at = seg % 2
-
     def block_of(number, block, near):
         start = number * actuators + (2 * block + near) * rows
         return terms[pl.ds(pl.multiple_of(start, rows), rows), :]
 
+    return block_of, rows, rows * (inner_ref.shape[1] // LANES)
+
+
+def outer_group_kernel(steps, samples, *refs):
+    far, inputs = lax.axis_size("seg") // 2, refs[:7]
+    send_ref, own_ref = refs[7:9]
+    block_of, rows, size = outer_terms(steps, samples, *inputs, *refs[-6:])
+    near_at = lax.axis_index("seg") % 2
     codes = []
     for number in range(len(steps)):
         parts = [block_of(number, block, 1 - near_at) for block in range(far)]
-        codes.append(put(near_ref, number * far * rows, parts))
+        codes.append(put(send_ref, number * far * size, parts, size))
         for block in range(far):
             own_ref[pl.ds((number * far + block) * rows, rows), :] = block_of(number, block, near_at)
-    put_codes(near_ref, len(steps) * far * rows, codes)
-
-
-def put(ref, at, parts):
-    largest = jnp.abs(parts[0])
-    for part in parts[1:]:
-        largest = jnp.maximum(largest, jnp.abs(part))
-    code = column_code(jnp.max(largest, axis=0, keepdims=True))
-    for part in parts:
-        ref[pl.ds(at, part.shape[0]), :] = coded(part, code)
-        at += part.shape[0]
-    return code
-
-
-def put_codes(ref, at, codes):
-    shape = (SCALE_ROWS, codes[0].shape[1])
-    sublane = lax.broadcasted_iota(jnp.int32, shape, 0)
-    rows = jnp.broadcast_to(codes[0].astype(jnp.int32), shape)
-    for row in range(1, len(codes)):
-        rows = jnp.where(sublane == row, jnp.broadcast_to(codes[row].astype(jnp.int32), shape), rows)
-    ref[pl.ds(at, SCALE_ROWS), :] = rows.astype(jnp.int16)
+    put_codes(send_ref, len(steps) * far * size, codes)
+
+
+def outer_near_kernel(samples, *refs):
+    far, inputs = lax.axis_size("seg") // 2, refs[:7]
+    send_one_ref, send_own_ref, kept_one_ref, own_ref = refs[7:11]
+    block_of, rows, size = outer_terms((1, 0), samples, *inputs, *refs[-6:])
+    near_at = lax.axis_index("seg") % 2
+
+    def send(ref, number, near):
+        parts = [block_of(number, block, near) for block in range(far)]
+        put_codes(ref, far * size, [put(ref, 0, parts, size)])
+
+    send(send_one_ref, 0, 1 - near_at)
+    send(send_own_ref, 1, 1 - near_at)
+    send(kept_one_ref, 0, near_at)
+    for block in range(far):
+        own_ref[pl.ds(block * rows, rows), :] = block_of(1, block, near_at)
+
+
+def second_near_kernel(came_one_ref, came_own_ref, kept_one_ref, own_ref, total_ref, *far_refs):
+    far = lax.axis_size("seg") // 2
+    far_refs = (None,) + far_refs
+    rows, sensors = total_ref.shape[0] // 2, total_ref.shape[1]
+    size = rows * (sensors // LANES)
+    far_at = lax.axis_index("seg") // 2
+    one, own, kept = (
+        scales_of(ref, far * size, 1, sensors) for ref in (came_one_ref, came_own_ref, kept_one_ref)
+    )
+
+    def block_sum(step, block):
+        at = pl.multiple_of(block * size, rows)
+        if step:
+            return opened(came_one_ref, at, one, 0, rows, sensors) + opened(kept_one_ref, at, kept, 0, rows, sensors)
+        mine = own_ref[pl.ds(pl.multiple_of(block * rows, rows), rows), :]
+        return mine + opened(came_own_ref, at, own, 0, rows, sensors)
+
+    for bits in range(far - 1, 0, -1):
+        codes = [put(far_refs[bits], step * size, [block_sum(step, far_at ^ bits)], size) for step in range(2)]
+        put_codes(far_refs[bits], 2 * size, codes)
+    for step in range(2):
+        total_ref[pl.ds(step * rows, rows), :] = block_sum(step, far_at)
+
+
+def far_sum(start, came, scales, number, rows, sensors):
+    value = start
+    size = rows * (sensors // LANES)
+    for ref, scale in zip(came, scales):
+        value = value + opened(ref, pl.multiple_of(number * size, rows), scale, number, rows, sensors)
+    return value
 
 
 def second_kernel(count, came_ref, own_ref, total_ref, *far_refs):
     far = lax.axis_size("seg") // 2
     far_refs = (None,) + far_refs
-    rows = total_ref.shape[0] // count
+    rows, sensors = total_ref.shape[0] // count, total_ref.shape[1]
+    size = rows * (sensors // LANES)
     far_at = lax.axis_index("seg") // 2
-    codes_came = codes_of(came_ref, count * far * rows)
+    scales = scales_of(came_ref, count * far * size, count, sensors)
 
     def block_sum(number, block):
-        here = pl.ds(pl.multiple_of((number * far + block) * rows, rows), rows)
-        return own_ref[here, :] + decoded(came_ref[here, :], codes_came[number : number + 1])
+        at = number * far + block
+        return own_ref[pl.ds(pl.multiple_of(at * rows, rows), rows), :] + opened(
+            came_ref, pl.multiple_of(at * size, rows), scales, number, rows, sensors
+        )
 
     for bits in range(far - 1, 0, -1):
-        codes = [
-            put(far_refs[bits], number * rows, [block_sum(number, far_at ^ bits)]) for number in range(count)
-        ]
-        put_codes(far_refs[bits], count * rows, codes)
+        codes = [put(far_refs[bits], number * size, [block_sum(number, far_at ^ bits)], size) for number in range(count)]
+        put_codes(far_refs[bits], count * size, codes)
     for number in range(count):
         total_ref[pl.ds(number * rows, rows), :] = block_sum(number, far_at)
 
 
-def third_kernel(steps, total_ref, *refs):
-    far = lax.axis_size("seg") // 2
-    came, outs = refs[: far - 1], refs[far - 1 :]
-    rows = total_ref.shape[0] // len(steps)
-    codes = [codes_of(ref, len(steps) * rows) for ref in came]
+def third_kernel(count, total_ref, *refs):
+    came, outs = refs[:-count], refs[-count:]
+    rows, sensors = total_ref.shape[0] // count, total_ref.shape[1]
+    size = rows * (sensors // LANES)
+    scales = [scales_of(ref, count * size, count, sensors) for ref in came]
+    for number in range(count):
+        value = far_sum(total_ref[pl.ds(number * rows, rows), :], came, scales, number, rows, sensors)
+        put_codes(outs[number], size, [put(outs[number], 0, [value], size)])
+
+
+def last_kernel(scaling, steps, total_ref, *refs):
+    far, out_ref = lax.axis_size("seg") // 2, refs[-1]
+    came_far, came = refs[: far - 1], refs[far - 1 : -1]
+    rows, sensors = total_ref.shape[0] // 2, total_ref.shape[1]
+    size = rows * (sensors // LANES)
+    lag = lax.axis_index("lag")
+
+    def write(step, value):
+        out_ref[:, 0, pl.ds(pl.multiple_of((lag ^ step) * sensors, LANES), sensors)] = value * scaling
+
     for number, step in enumerate(steps):
-        here = pl.ds(number * rows, rows)
-        value = total_ref[here, :]
-        for ref, code in zip(came, codes):
-            value = value + decoded(ref[here, :], code[number : number + 1])
-        if step:
-            put_codes(outs[number], rows, [put(outs[number], 0, [value])])
-        else:
-            outs[number][...] = value
-
-
-def last_kernel(scaling, own_ref, *refs):
-    came, out_ref = (None,) + refs[:-1], refs[-1]
-    rows, width = own_ref.shape
-    lag = lax.axis_index("lag")
-    for step in range(len(came)):
-        if step:
-            value = decoded(came[step][pl.ds(0, rows), :], codes_of(came[step], rows)[:1])
-        else:
-            value = own_ref[...]
-        out_ref[:, 0, pl.ds(pl.multiple_of((lag ^ step) * width, LANES), width)] = value * scaling
+        write(step, opened(came[number], 0, scales_of(came[number], size, 1, sensors), 0, rows, sensors))
+    scales = [scales_of(ref, 2 * size, 2, sensors) for ref in came_far]
+    for step in range(2):
+        write(step, far_sum(total_ref[pl.ds(step * rows, rows), :], came_far, scales, step, rows, sensors))
 
 
 def per_device_staged(actuator_input, sensor_output, run_lengths, lag_offsets):
@@ -318,8 +387,10 @@
     scaling = 1.0 / math.sqrt(samples * segs)
     spare = lags * actuators
 
-    def payload(count):
-        return jax.ShapeDtypeStruct((count * rows + SCALE_ROWS, sensors), jnp.int16)
+    def payload(count, codes):
+        return jax.ShapeDtypeStruct(
+            (count * rows * (sensors // LANES) + scale_rows(codes, sensors), LANES), jnp.int16
+        )
 
     def wide(count):
         return jax.ShapeDtypeStruct((count * rows, sensors), jnp.float32)
@@ -370,112 +441,114 @@
         name="inner",
     )(run_lengths, lag_offsets, actuator_input, sensor_output)
 
-    def outer(name, steps):
-        def body(*refs):
-            outer_kernel(steps, samples, *refs)
-
+    def outer(name, body, count, shapes):
         return pl.pallas_call(
             body,
             in_specs=[hbm] * 2 + [vmem] * 5,
-            out_specs=[vmem] * 2,
-            out_shape=[payload(len(steps) * far), wide(len(steps) * far)],
+            out_specs=[vmem] * len(shapes),
+            out_shape=shapes,
             scratch_shapes=scalars
             + [
                 pltpu.VMEM((actuators, 2 * chunk + LANES), jnp.bfloat16),
-                pltpu.VMEM((len(steps) * actuators, chunk), jnp.bfloat16),
-                pltpu.VMEM((len(steps) * actuators, sensors), jnp.float32),
+                pltpu.VMEM((count * actuators, chunk), jnp.bfloat16),
+                pltpu.VMEM((count * actuators, sensors), jnp.float32),
                 pltpu.SemaphoreType.DMA((2,)),
             ],
             compiler_params=pltpu.CompilerParams(vmem_limit_bytes=24 << 20),
             cost_estimate=pl.CostEstimate(
-                flops=2 * len(steps) * actuators * sensors * chunk, bytes_accessed=4 << 20, transcendentals=0
+                flops=2 * count * actuators * sensors * chunk, bytes_accessed=4 << 20, transcendentals=0
             ),
             name=name,
         )(run_lengths, lag_offsets, fetched, swapped, first_turned, first_sensed, inner)
 
-    def second(name, steps, came, own):
-        def body(*refs):
-            second_kernel(len(steps), *refs)
-
+    def local(name, body, shapes, *operands):
         return pl.pallas_call(
             body,
-            in_specs=[vmem] * 2,
-            out_specs=[vmem] * far,
-            out_shape=[wide(len(steps))] + [payload(len(steps))] * (far - 1),
-            compiler_params=small,
-            cost_estimate=pl.CostEstimate(flops=1 << 20, bytes_accessed=2 << 20, transcendentals=0),
-            name=name,
-        )(came, own)
-
-    def third(name, steps, total, *came):
-        def body(*refs):
-            third_kernel(steps, *refs)
-
-        return pl.pallas_call(
-            body,
-            in_specs=[vmem] * far,
-            out_specs=[vmem] * len(steps),
-            out_shape=[payload(1) if step else wide(1) for step in steps],
+            in_specs=[vmem] * len(operands),
+            out_specs=[vmem] * len(shapes),
+            out_shape=shapes,
             compiler_params=small,
             cost_estimate=pl.CostEstimate(flops=1 << 20, bytes_accessed=1 << 20, transcendentals=0),
             name=name,
-        )(total, *came)
-
-    masks = range(far - 1, 0, -1)
-    groups = (tuple(range(lags - 1, lags // 2 - 1, -1)), tuple(range(lags // 2 - 1, -1, -1)))
-    names = ("a", "b")
-    near, kept, total, ended = {}, {}, {}, {}
-    for name, steps in zip(names, groups):
-        send, kept[name] = outer("outer_" + name, steps)
-        near[name] = exchange(send, 1, 0)
-    for name, steps in zip(names, groups):
-        total[name], *sends = second("second_" + name, steps, near[name], kept[name])
-        near[name] = [exchange(sends[bits - 1], 2 * bits, 0) for bits in masks][::-1]
-    for name, steps in zip(names, groups):
-        outs = third("third_" + name, steps, total[name], *near[name])
-        for step, out in zip(steps, outs):
-            ended[step] = exchange(out, 0, step) if step else out
+        )(*operands)
+
+    def far_exchange(sends):
+        came = [None] * (far - 1)
+        for bits in range(far - 1, 0, -1):
+            came[bits - 1] = exchange(sends[bits - 1], 2 * bits, 0)
+        return came
+
+    steps = tuple(range(lags - 1, 1, -1))
+    count = len(steps)
+
+    def outer_a(*refs):
+        outer_group_kernel(steps, samples, *refs)
+
+    def outer_b(*refs):
+        outer_near_kernel(samples, *refs)
+
+    def second_a(*refs):
+        second_kernel(count, *refs)
+
+    def third_a(*refs):
+        third_kernel(count, *refs)
 
     def last_body(*refs):
-        return last_kernel(scaling, *refs)
-
-    return pl.pallas_call(
+        last_kernel(scaling, steps, *refs)
+
+    send_a, own_a = outer("outer_a", outer_a, count, [payload(count * far, count), wide(count * far)])
+    came_a = exchange(send_a, 1, 0)
+    send_one, send_own, kept_one, own_b = outer("outer_b", outer_b, 2, [payload(far, 1)] * 3 + [wide(far)])
+    came_one = exchange(send_one, 1, 1)
+    came_own = exchange(send_own, 1, 0)
+    kept_one = exchange(kept_one, 0, 1)
+    total_a, *sends_a = local("second_a", second_a, [wide(count)] + [payload(count, count)] * (far - 1), came_a, own_a)
+    far_a = far_exchange(sends_a)
+    total_b, *sends_b = local(
+        "second_b",
+        second_near_kernel,
+        [wide(2)] + [payload(2, 2)] * (far - 1),
+        came_one,
+        came_own,
+        kept_one,
+        own_b,
+    )
+    far_b = far_exchange(sends_b)
+    outs = local("third_a", third_a, [payload(1, 1)] * count, total_a, *far_a)
+    came = [exchange(out, 0, step) for step, out in zip(steps, outs)]
+    return local(
+        "last",
         last_body,
-        in_specs=[vmem] * lags,
-        out_specs=vmem,
-        out_shape=jax.ShapeDtypeStruct((rows, 1, lags * sensors), jnp.float32),
-        compiler_params=small,
-        name="last",
-    )(*[ended[step] for step in range(lags)])
+        [jax.ShapeDtypeStruct((rows, 1, lags * sensors), jnp.float32)],
+        total_b,
+        *far_b,
+        *came,
+    )[0]
 
 
 def solution(mesh):
     segs, lags = mesh.shape["seg"], mesh.shape["lag"]
 
     def per_device(actuator_input, sensor_output, run_lengths, lag_offsets):
-        rows = actuator_input.shape[1] // segs
+        rows, sensors = actuator_input.shape[1] // segs, sensor_output.shape[1]
         staged = (
             4 <= segs <= 16
             and segs & (segs - 1) == 0
             and lags & (lags - 1) == 0
             and lags == NBLK * LBW
+            and lags >= 4
             and rows % 8 == 0
+            and sensors % LANES == 0
             and actuator_input.shape[0] % LMAX == 0
             and actuator_input.shape[0] > LMAX
         )
         chosen = per_device_staged if staged else per_device_plain
         return chosen(actuator_input, sensor_output, run_lengths, lag_offsets)
 
-    mapped = jax.shard_map(
+    return jax.shard_map(
         per_device,
         mesh=mesh,
         in_specs=(P("seg", None), P("seg", "lag"), P(), P()),
         out_specs=P("seg", "lag", None),
         check_vma=False,
     )
-    return mapped
-    return mapped
-    return mapped
-    return mapped
-    return mapped
-    return mapped

time: 48.6 us -> 46.7 us (0.961)
  waiting for transfers between devices: 16 us -> 11.9 us
  starting transfers between devices: 21 us -> 23.2 us
    ppermute x12 -> x13, waiting for transfers between devices: 10.5 us -> 6.37 us  [exchange(): return lax.ppermute(value, ('seg', 'lag'), pairs)]
    ppermute x12 -> x13, starting transfers between devices: 16.1 us -> 18.3 us  [exchange(): return lax.ppermute(value, ('seg', 'lag'), pairs)]
    pallas_call x5 -> x4, Pallas kernels: 1.36 us -> 1.36 us  [local(): pl.pallas_call(body, in_specs=[vmem] * len(operands), out_specs=[vmem] *...]
  transfers between devices with their start and end apart: 13 -> 14, of which waited for: 4 -> 4; matrix products, arithmetic and copies ran while one was open for 0% -> 0% of each run, Pallas kernels for 16% -> 17%
where the time goes in v4:
time: 46.7 us; the launch traced here: 46.5 us
  starting transfers between devices  23.2 us (50%)
  waiting for transfers between devices  11.9 us (25%)
  Pallas kernels  11.3 us (24%)
    ppermute x13, starting transfers between devices, exchange(): return lax.ppermute(value, ('seg', 'lag'), pairs)  18.3 us
    ppermute x13, waiting for transfers between devices, exchange(): return lax.ppermute(value, ('seg', 'lag'), pairs)  6.37 us
    pallas_call x1, Pallas kernels, per_device_staged(): pl.pallas_call(inner_kernel, in_specs=[hbm] * 4, out_specs=[vmem] * 3, ou...  5.6 us
    ppermute x1, waiting for transfers between devices, shifted_by(): lax.ppermute(value, axis, [(source, source + steps) for source in range(i...  5.53 us
    ppermute x1, starting transfers between devices, shifted_by(): lax.ppermute(value, axis, [(source, source + steps) for source in range(i...  4.89 us
    pallas_call x2, Pallas kernels, outer(): pl.pallas_call(body, in_specs=[hbm] * 2 + [vmem] * 5, out_specs=[vmem] *...  3.41 us
    pallas_call x4, Pallas kernels, local(): pl.pallas_call(body, in_specs=[vmem] * len(operands), out_specs=[vmem] *...  1.36 us
    pallas_call x1, Pallas kernels, per_device_staged(): pl.pallas_call(cut_kernel, in_specs=[hbm], out_specs=vmem, out_shape=jax....  0.96 us
  transfers between devices with their start and end apart: 14, of which 4 were waited for; matrix products, arithmetic and copies ran while one was open for 0% of the time, Pallas kernels for 17%

profile of v4, /device:TPU:0, one launch (start us, length us, event | category | flops | bytes accessed | tf_op | source)
XLA Modules:
  0.0 46.5 jit_solution(179192723838125991)
XLA Ops:
  0.0 1.0 %cut.1 = bf16[512,256]{1,0:T(8,128)(2,1)S(1)} custom-call(bf16[3072,256]{1,0:T(8,128)(2,1)} %actuators_ref.3), custom_call_target="tpu_custom_call" | custom-call | tf_op jit(solution)/shard_map/cut/pallas_call | solution.py:408
  1.0 4.9 %collective-permute-start = (bf16[512,256]{1,0:T(8,128)(2,1)S(1)}, bf16[512,256]{1,0:T(8,128)(2,1)S(1)}, u32[]{:S(2)}, u32[]{:S(2)}) collective-permute-start(bf16[512,256]{1,0:T(8,128)(2,1)S(1)} %cut.1), channel_id=1, source_target_pairs={{0,4},{4,8},{8,12},{12,16},{16,20},{20,24},{24,28},{1,5},{5,9},{9,... | collective-permute-start | bytes 786440 | tf_op jit(solution)/shard_map/ppermute | solution.py:42
  5.9 5.5 %collective-permute-done.refs_2_ = bf16[512,256]{1,0:T(8,128)(2,1)S(1)} collective-permute-done((bf16[512,256]{1,0:T(8,128)(2,1)S(1)}, bf16[512,256]{1,0:T(8,128)(2,1)S(1)}, u32[]{:S(2)}, u32[]{:S(2)}) %collective-permute-start) | collective-permute-done | bytes 262176 | tf_op jit(solution)/shard_map/ppermute | solution.py:42
  11.4 0.0 collective-permute-start.1
  11.4 5.6 %inner.1 = (f32[1024,512]{1,0:T(8,128)S(1)}, bf16[256,1024]{1,0:T(8,128)(2,1)S(1)}, bf16[1024,512]{1,0:T(8,128)(2,1)S(1)}) custom-call(s32[4]{0:T(128)} %refs_0_.3, s32[2]{0:T(128)} %refs_1_.3, bf16[3072,256]{1,0:T(8,128)(2,1)} %actuators_ref.3, bf16[3072,512]{1,0:T(8,128)(2,1)} %sensors_ref.1), custom_call_target="tpu_custom_call" | custom-call | flops 2147483648 | bytes 6291456 | tf_op jit(solution)/shard_map/inner/pallas_call | solution.py:420
  17.0 0.0 collective-permute-done.1.refs_3_
  17.0 1.7 %outer_a.1 = (s16[1032,128]{1,0:T(8,128)(2,1)S(1)}, f32[256,512]{1,0:T(8,128)S(1)}) custom-call(s32[4]{0:T(128)} %refs_0_.3, s32[2]{0:T(128)} %refs_1_.3, bf16[512,256]{1,0:T(8,128)(2,1)S(1)} %collective-permute-done.refs_2_, bf16[512,256]{1,0:T(8,128)(2,1)S(1)} %collective-permute-done.1.refs_3_, bf16[256,1024]{1,0:T(8,128)(2,1)S(1)} %get-tuple-element.24.refs_4_, ...), custom_call_target="tpu_custom_call" | custom-call | flops 536870912 | bytes 4194304 | tf_op jit(solution)/shard_map/outer_a/pallas_call | solution.py:445
  18.7 2.5 %collective-permute-start.8 = (s16[1032,128]{1,0:T(8,128)(2,1)S(1)}, s16[1032,128]{1,0:T(8,128)(2,1)S(1)}, u32[]{:S(2)}, u32[]{:S(2)}) collective-permute-start(s16[1032,128]{1,0:T(8,128)(2,1)S(1)} %get-tuple-element.35), channel_id=1, source_target_pairs={{0,4},{1,5},{2,6},{3,7},{4,0},{5,1},{6,2},{7,3},{8,12},{9,13},{10,... | collective-permute-start | bytes 792584 | tf_op jit(solution)/shard_map/ppermute | solution.py:89
  21.3 1.7 %outer_b.1 = (s16[520,128]{1,0:T(8,128)(2,1)S(1)}, s16[520,128]{1,0:T(8,128)(2,1)S(1)}, s16[520,128]{1,0:T(8,128)(2,1)S(1)}, f32[128,512]{1,0:T(8,128)S(1)}) custom-call(s32[4]{0:T(128)} %refs_0_.3, s32[2]{0:T(128)} %refs_1_.3, bf16[512,256]{1,0:T(8,128)(2,1)S(1)} %collective-permute-done.refs_2_, bf16[512,256]{1,0:T(8,128)(2,1)S(1)} %collective-permute-done.1.refs_3_, ...), custom_call_target="tpu_custom_call" | custom-call | flops 536870912 | bytes 4194304 | tf_op jit(solution)/shard_map/outer_b/pallas_call | solution.py:445
  23.0 0.2 collective-permute-start.2
  23.2 1.7 %collective-permute-start.3 = (s16[520,128]{1,0:T(8,128)(2,1)S(1)}, s16[520,128]{1,0:T(8,128)(2,1)S(1)}, u32[]{:S(2)}, u32[]{:S(2)}) collective-permute-start(s16[520,128]{1,0:T(8,128)(2,1)S(1)} %get-tuple-element.28), channel_id=1, source_target_pairs={{0,4},{1,5},{2,6},{3,7},{4,0},{5,1},{6,2},{7,3},{8,12},{9,13},{10,... | collective-permute-start | bytes 399368 | tf_op jit(solution)/shard_map/ppermute | solution.py:89
  24.9 0.0 collective-permute-start.4
  24.9 3.6 %collective-permute-done.8.refs_0_ = s16[1032,128]{1,0:T(8,128)(2,1)S(1)} collective-permute-done((s16[1032,128]{1,0:T(8,128)(2,1)S(1)}, s16[1032,128]{1,0:T(8,128)(2,1)S(1)}, u32[]{:S(2)}, u32[]{:S(2)}) %collective-permute-start.8) | collective-permute-done | bytes 264224 | tf_op jit(solution)/shard_map/ppermute | solution.py:89
  28.5 0.2 second_a.1
  28.7 4.1 %collective-permute-start.10 = (s16[264,128]{1,0:T(8,128)(2,1)S(1)}, s16[264,128]{1,0:T(8,128)(2,1)S(1)}, u32[]{:S(2)}, u32[]{:S(2)}) collective-permute-start(s16[264,128]{1,0:T(8,128)(2,1)S(1)} %get-tuple-element.39), channel_id=1, source_target_pairs={{0,16},{1,17},{2,18},{3,19},{4,20},{5,21},{6,22},{7,23},{8,24},{9,... | collective-permute-start | bytes 202760 | tf_op jit(solution)/shard_map/ppermute | solution.py:89
  32.8 1.3 %collective-permute-start.11 = (s16[264,128]{1,0:T(8,128)(2,1)S(1)}, s16[264,128]{1,0:T(8,128)(2,1)S(1)}, u32[]{:S(2)}, u32[]{:S(2)}) collective-permute-start(s16[264,128]{1,0:T(8,128)(2,1)S(1)} %get-tuple-element.40), channel_id=1, source_target_pairs={{0,24},{1,25},{2,26},{3,27},{4,28},{5,29},{6,30},{7,31},{8,16},{9,... | collective-permute-start | bytes 202760 | tf_op jit(solution)/shard_map/ppermute | solution.py:89
  34.1 0.0 collective-permute-done.2.came_one_ref
  34.1 0.2 collective-permute-start.9
  34.4 0.0 collective-permute-done.3.came_own_ref
  34.4 0.0 collective-permute-done.4.kept_one_ref
  34.4 0.2 second_b.1
  34.6 2.4 %collective-permute-start.5 = (s16[264,128]{1,0:T(8,128)(2,1)S(1)}, s16[264,128]{1,0:T(8,128)(2,1)S(1)}, u32[]{:S(2)}, u32[]{:S(2)}) collective-permute-start(s16[264,128]{1,0:T(8,128)(2,1)S(1)} %get-tuple-element.32), channel_id=1, source_target_pairs={{0,8},{1,9},{2,10},{3,11},{4,12},{5,13},{6,14},{7,15},{8,0},{9,1},... | collective-permute-start | bytes 202760 | tf_op jit(solution)/shard_map/ppermute | solution.py:89
  37.0 2.6 %collective-permute-start.6 = (s16[264,128]{1,0:T(8,128)(2,1)S(1)}, s16[264,128]{1,0:T(8,128)(2,1)S(1)}, u32[]{:S(2)}, u32[]{:S(2)}) collective-permute-start(s16[264,128]{1,0:T(8,128)(2,1)S(1)} %get-tuple-element.33), channel_id=1, source_target_pairs={{0,16},{1,17},{2,18},{3,19},{4,20},{5,21},{6,22},{7,23},{8,24},{9,... | collective-permute-start | bytes 202760 | tf_op jit(solution)/shard_map/ppermute | solution.py:89
  39.6 0.0 collective-permute-done.10.refs_2_
  39.6 1.5 %collective-permute-start.7 = (s16[264,128]{1,0:T(8,128)(2,1)S(1)}, s16[264,128]{1,0:T(8,128)(2,1)S(1)}, u32[]{:S(2)}, u32[]{:S(2)}) collective-permute-start(s16[264,128]{1,0:T(8,128)(2,1)S(1)} %get-tuple-element.34), channel_id=1, source_target_pairs={{0,24},{1,25},{2,26},{3,27},{4,28},{5,29},{6,30},{7,31},{8,16},{9,... | collective-permute-start | bytes 202760 | tf_op jit(solution)/shard_map/ppermute | solution.py:89
  41.1 0.0 collective-permute-done.11.refs_3_
  41.1 0.0 collective-permute-done.9.refs_1_
  41.1 0.1 third_a.1
  41.2 0.1 collective-permute-start.12
  41.3 1.6 %collective-permute-start.13 = (s16[136,128]{1,0:T(8,128)(2,1)S(1)}, s16[136,128]{1,0:T(8,128)(2,1)S(1)}, u32[]{:S(2)}, u32[]{:S(2)}) collective-permute-start(s16[136,128]{1,0:T(8,128)(2,1)S(1)} %get-tuple-element.42), channel_id=1, source_target_pairs={{0,2},{1,3},{2,0},{3,1},{4,6},{5,7},{6,4},{7,5},{8,10},{9,11},{10,... | collective-permute-start | bytes 104456 | tf_op jit(solution)/shard_map/ppermute | solution.py:89
  42.9 0.0 collective-permute-done.5.refs_1_
  42.9 1.3 %collective-permute-done.6.refs_2_ = s16[264,128]{1,0:T(8,128)(2,1)S(1)} collective-permute-done((s16[264,128]{1,0:T(8,128)(2,1)S(1)}, s16[264,128]{1,0:T(8,128)(2,1)S(1)}, u32[]{:S(2)}, u32[]{:S(2)}) %collective-permute-start.6) | collective-permute-done | bytes 67616 | tf_op jit(solution)/shard_map/ppermute | solution.py:89
  44.3 1.5 %collective-permute-done.7.refs_3_ = s16[264,128]{1,0:T(8,128)(2,1)S(1)} collective-permute-done((s16[264,128]{1,0:T(8,128)(2,1)S(1)}, s16[264,128]{1,0:T(8,128)(2,1)S(1)}, u32[]{:S(2)}, u32[]{:S(2)}) %collective-permute-start.7) | collective-permute-done | bytes 67616 | tf_op jit(solution)/shard_map/ppermute | solution.py:89
  45.7 0.0 collective-permute-done.12.refs_4_
  45.7 0.0 collective-permute-done.13.refs_5_
  45.7 0.8 %last.1 = f32[32,1,2048]{2,1,0:T(1,128)} custom-call(f32[64,512]{1,0:T(8,128)S(1)} %get-tuple-element.31.refs_0_, s16[264,128]{1,0:T(8,128)(2,1)S(1)} %collective-permute-done.5.refs_1_, s16[264,128]{1,0:T(8,128)(2,1)S(1)} %collective-permute-done.6.refs_2_, s16[264,128]{1,0:T(8,128)(2,1)S(1)} %collective-permute-done.7.refs_3_, ...), custom_call_target="tpu_custom_call" | custom-call | flops 1048576 | bytes 1048576 | tf_op jit(solution)/shard_map/last/pallas_call | solution.py:465
Async XLA Ops:
  1.0 10.4 %collective-permute-start = (bf16[512,256]{1,0:T(8,128)(2,1)S(1)}, bf16[512,256]{1,0:T(8,128)(2,1)S(1)}, u32[]{:S(2)}, u32[]{:S(2)}) collective-permute-start(bf16[512,256]{1,0:T(8,128)(2,1)S(1)} %cut.1), channel_id=1, source_target_pairs={{0,4},{4,8},{8,12},{12,16},{16,20},{20,24},{24,28},{1,5},{5,9},{9,... | collective-permute-start | bytes 786440 | tf_op jit(solution)/shard_map/ppermute | solution.py:42
  11.4 5.6 %collective-permute-start.1 = (bf16[512,256]{1,0:T(8,128)(2,1)S(1)}, bf16[512,256]{1,0:T(8,128)(2,1)S(1)}, u32[]{:S(2)}, u32[]{:S(2)}) collective-permute-start(bf16[512,256]{1,0:T(8,128)(2,1)S(1)} %collective-permute-done.refs_2_), channel_id=1, source_target_pairs={{0,1},{1,0},{2,3},{3,2},{4,5},{5,4},{6,7},{7,6},{8,9},{9,8},{10,11... | collective-permute-start | bytes 786440 | tf_op jit(solution)/shard_map/ppermute | solution.py:89
  18.7 9.8 %collective-permute-start.8 = (s16[1032,128]{1,0:T(8,128)(2,1)S(1)}, s16[1032,128]{1,0:T(8,128)(2,1)S(1)}, u32[]{:S(2)}, u32[]{:S(2)}) collective-permute-start(s16[1032,128]{1,0:T(8,128)(2,1)S(1)} %get-tuple-element.35), channel_id=1, source_target_pairs={{0,4},{1,5},{2,6},{3,7},{4,0},{5,1},{6,2},{7,3},{8,12},{9,13},{10,... | collective-permute-start | bytes 792584 | tf_op jit(solution)/shard_map/ppermute | solution.py:89
  23.0 11.1 %collective-permute-start.2 = (s16[520,128]{1,0:T(8,128)(2,1)S(1)}, s16[520,128]{1,0:T(8,128)(2,1)S(1)}, u32[]{:S(2)}, u32[]{:S(2)}) collective-permute-start(s16[520,128]{1,0:T(8,128)(2,1)S(1)} %get-tuple-element.27), channel_id=1, source_target_pairs={{0,5},{1,4},{2,7},{3,6},{4,1},{5,0},{6,3},{7,2},{8,13},{9,12},{10,... | collective-permute-start | bytes 399368 | tf_op jit(solution)/shard_map/ppermute | solution.py:89
  23.2 11.2 %collective-permute-start.3 = (s16[520,128]{1,0:T(8,128)(2,1)S(1)}, s16[520,128]{1,0:T(8,128)(2,1)S(1)}, u32[]{:S(2)}, u32[]{:S(2)}) collective-permute-start(s16[520,128]{1,0:T(8,128)(2,1)S(1)} %get-tuple-element.28), channel_id=1, source_target_pairs={{0,4},{1,5},{2,6},{3,7},{4,0},{5,1},{6,2},{7,3},{8,12},{9,13},{10,... | collective-permute-start | bytes 399368 | tf_op jit(solution)/shard_map/ppermute | solution.py:89
  24.9 9.4 %collective-permute-start.4 = (s16[520,128]{1,0:T(8,128)(2,1)S(1)}, s16[520,128]{1,0:T(8,128)(2,1)S(1)}, u32[]{:S(2)}, u32[]{:S(2)}) collective-permute-start(s16[520,128]{1,0:T(8,128)(2,1)S(1)} %get-tuple-element.29), channel_id=1, source_target_pairs={{0,1},{1,0},{2,3},{3,2},{4,5},{5,4},{6,7},{7,6},{8,9},{9,8},{10,11... | collective-permute-start | bytes 399368 | tf_op jit(solution)/shard_map/ppermute | solution.py:89
  28.7 10.9 %collective-permute-start.10 = (s16[264,128]{1,0:T(8,128)(2,1)S(1)}, s16[264,128]{1,0:T(8,128)(2,1)S(1)}, u32[]{:S(2)}, u32[]{:S(2)}) collective-permute-start(s16[264,128]{1,0:T(8,128)(2,1)S(1)} %get-tuple-element.39), channel_id=1, source_target_pairs={{0,16},{1,17},{2,18},{3,19},{4,20},{5,21},{6,22},{7,23},{8,24},{9,... | collective-permute-start | bytes 202760 | tf_op jit(solution)/shard_map/ppermute | solution.py:89
  32.8 8.3 %collective-permute-start.11 = (s16[264,128]{1,0:T(8,128)(2,1)S(1)}, s16[264,128]{1,0:T(8,128)(2,1)S(1)}, u32[]{:S(2)}, u32[]{:S(2)}) collective-permute-start(s16[264,128]{1,0:T(8,128)(2,1)S(1)} %get-tuple-element.40), channel_id=1, source_target_pairs={{0,24},{1,25},{2,26},{3,27},{4,28},{5,29},{6,30},{7,31},{8,16},{9,... | collective-permute-start | bytes 202760 | tf_op jit(solution)/shard_map/ppermute | solution.py:89
  34.1 7.0 %collective-permute-start.9 = (s16[264,128]{1,0:T(8,128)(2,1)S(1)}, s16[264,128]{1,0:T(8,128)(2,1)S(1)}, u32[]{:S(2)}, u32[]{:S(2)}) collective-permute-start(s16[264,128]{1,0:T(8,128)(2,1)S(1)} %get-tuple-element.38), channel_id=1, source_target_pairs={{0,8},{1,9},{2,10},{3,11},{4,12},{5,13},{6,14},{7,15},{8,0},{9,1},... | collective-permute-start | bytes 202760 | tf_op jit(solution)/shard_map/ppermute | solution.py:89
  34.6 8.3 %collective-permute-start.5 = (s16[264,128]{1,0:T(8,128)(2,1)S(1)}, s16[264,128]{1,0:T(8,128)(2,1)S(1)}, u32[]{:S(2)}, u32[]{:S(2)}) collective-permute-start(s16[264,128]{1,0:T(8,128)(2,1)S(1)} %get-tuple-element.32), channel_id=1, source_target_pairs={{0,8},{1,9},{2,10},{3,11},{4,12},{5,13},{6,14},{7,15},{8,0},{9,1},... | collective-permute-start | bytes 202760 | tf_op jit(solution)/shard_map/ppermute | solution.py:89
  37.0 7.2 %collective-permute-start.6 = (s16[264,128]{1,0:T(8,128)(2,1)S(1)}, s16[264,128]{1,0:T(8,128)(2,1)S(1)}, u32[]{:S(2)}, u32[]{:S(2)}) collective-permute-start(s16[264,128]{1,0:T(8,128)(2,1)S(1)} %get-tuple-element.33), channel_id=1, source_target_pairs={{0,16},{1,17},{2,18},{3,19},{4,20},{5,21},{6,22},{7,23},{8,24},{9,... | collective-permute-start | bytes 202760 | tf_op jit(solution)/shard_map/ppermute | solution.py:89
  39.6 6.1 %collective-permute-start.7 = (s16[264,128]{1,0:T(8,128)(2,1)S(1)}, s16[264,128]{1,0:T(8,128)(2,1)S(1)}, u32[]{:S(2)}, u32[]{:S(2)}) collective-permute-start(s16[264,128]{1,0:T(8,128)(2,1)S(1)} %get-tuple-element.34), channel_id=1, source_target_pairs={{0,24},{1,25},{2,26},{3,27},{4,28},{5,29},{6,30},{7,31},{8,16},{9,... | collective-permute-start | bytes 202760 | tf_op jit(solution)/shard_map/ppermute | solution.py:89
  41.2 4.5 %collective-permute-start.12 = (s16[136,128]{1,0:T(8,128)(2,1)S(1)}, s16[136,128]{1,0:T(8,128)(2,1)S(1)}, u32[]{:S(2)}, u32[]{:S(2)}) collective-permute-start(s16[136,128]{1,0:T(8,128)(2,1)S(1)} %get-tuple-element.41), channel_id=1, source_target_pairs={{0,3},{1,2},{2,1},{3,0},{4,7},{5,6},{6,5},{7,4},{8,11},{9,10},{10,... | collective-permute-start | bytes 104456 | tf_op jit(solution)/shard_map/ppermute | solution.py:89
  41.3 4.4 %collective-permute-start.13 = (s16[136,128]{1,0:T(8,128)(2,1)S(1)}, s16[136,128]{1,0:T(8,128)(2,1)S(1)}, u32[]{:S(2)}, u32[]{:S(2)}) collective-permute-start(s16[136,128]{1,0:T(8,128)(2,1)S(1)} %get-tuple-element.42), channel_id=1, source_target_pairs={{0,2},{1,3},{2,0},{3,1},{4,6},{5,7},{6,4},{7,5},{8,10},{9,11},{10,... | collective-permute-start | bytes 104456 | tf_op jit(solution)/shard_map/ppermute | solution.py:89

commit v5 on v4

--- a/solution.py
+++ b/solution.py
@@ -144,22 +144,37 @@
     return offsets_ref[which // LBW] + which % LBW
 
 
-def fill_rows(turned, at_lane, masked, at_masked, runs, offsets, lag, steps, start_row, chunk):
-    actuators = turned.shape[0]
+def put_turned(turned, at_lane, value):
+    segs = lax.axis_size("seg")
+    actuators = value.shape[1]
+    rows, near_at = actuators // segs, lax.axis_index("seg") % 2
+    across = value.T
+    for at in range(segs):
+        mine = (near_at + at + 1) % 2
+        start = mine * (actuators // 2) + (at // 2) * rows
+        turned[pl.ds(pl.multiple_of(start, rows), rows), pl.ds(at_lane, value.shape[0])] = across[
+            at * rows : (at + 1) * rows
+        ]
+
+
+def fill_rows(turned, at_lane, masked, at_masked, runs, offsets, lag, blocks, start_row, chunk):
     tiles = chunk // LANES
     lane = lax.broadcasted_iota(jnp.int32, (1, LANES), 1)
     ends, end = [], jnp.int32(0)
     for run in range(runs.shape[0]):
         end = end + runs[run]
         ends.append(end)
-    for number, step in enumerate(steps):
+    at_row = 0
+    for step, first_row, actuators in blocks:
         shift = lag_of(offsets, lag ^ step)
         at = at_lane - shift
         base, turn = at // LANES, at % LANES
         low = jnp.broadcast_to(lane < LANES - turn, (actuators, LANES))
         pieces = [
             pltpu.roll(
-                turned[:, pl.ds(pl.multiple_of((base + tile) * LANES, LANES), LANES)],
+                turned[
+                    pl.ds(first_row, actuators), pl.ds(pl.multiple_of((base + tile) * LANES, LANES), LANES)
+                ],
                 (LANES - turn) % LANES,
                 1,
             )
@@ -173,15 +188,16 @@
             keep = jnp.broadcast_to(crossed == 0, (actuators, LANES))
             value = jnp.where(low, pieces[tile], pieces[tile + 1])
             value = jnp.where(keep, value, jnp.zeros_like(value))
-            masked[pl.ds(number * actuators, actuators), pl.ds(at_masked + tile * LANES, LANES)] = value
+            masked[pl.ds(at_row, actuators), pl.ds(at_masked + tile * LANES, LANES)] = value
+        at_row += actuators
 
 
 def inner_kernel(
     runs_ref, offsets_ref, actuators_ref, sensors_ref, out_ref, first_turned_ref, first_sensed_ref,
-    runs, offsets, held, sensed, turned, masked, sems
+    runs_out, offsets_out, runs, offsets, held, sensed, turned, masked, sems
 ):
     chunk, lags = LMAX, lax.axis_size("lag")
-    samples, _ = actuators_ref.shape
+    samples, actuators = actuators_ref.shape
     chunks = samples // chunk
     copies = [
         pltpu.make_async_copy(runs_ref, runs, sems.at[0]),
@@ -201,21 +217,23 @@
     copies.append(
         pltpu.make_async_copy(sensors_ref.at[pl.ds(0, chunk), :], first_sensed_ref, sems.at[1 + 2 * chunks])
     )
+    copies.append(pltpu.make_async_copy(runs_ref, runs_out, sems.at[2 + 2 * chunks]))
+    copies.append(pltpu.make_async_copy(offsets_ref, offsets_out, sems.at[3 + 2 * chunks]))
     for copy in copies:
         copy.start()
     start_row = lax.axis_index("seg") * samples
     for at in range(chunks):
         copies[2 + at].wait()
         here = pl.ds(at * chunk, chunk)
-        turned[:, here] = held[here, :].T
+        put_turned(turned, at * chunk, held[here, :])
         if at == 0:
-            first_turned_ref[...] = turned[:, here]
+            first_turned_ref[:, pl.ds(chunk, chunk)] = turned[:, here]
             copies[0].wait()
             copies[1].wait()
             continue
         fill_rows(
             turned, at * chunk, masked, (at - 1) * chunk, runs, offsets,
-            lax.axis_index("lag"), range(lags), start_row + at * chunk, chunk,
+            lax.axis_index("lag"), [(step, 0, actuators) for step in range(lags)], start_row + at * chunk, chunk,
         )
         copies[1 + chunks + at].wait()
         there = pl.ds((at - 1) * chunk, chunk)
@@ -224,7 +242,8 @@
             out_ref[...] = terms
         else:
             out_ref[...] += terms
-    copies[-1].wait()
+    for copy in copies[-3:]:
+        copy.wait()
 
 
 def cut_kernel(actuators_ref, out_ref, sem):
@@ -236,67 +255,72 @@
 
 
 def outer_terms(
-    steps, samples, runs_ref, offsets_ref, mine_ref, theirs_ref, first_turned_ref, sensed_ref, inner_ref,
-    runs, offsets, turned, masked, terms, sems
+    blocks, samples, runs_ref, offsets_ref, turned, sensed_ref, inner_ref, runs, offsets, masked, terms, sems, tails=()
 ):
-    chunk, segs = LMAX, lax.axis_size("seg")
-    actuators = inner_ref.shape[0] // lax.axis_size("lag")
+    chunk = LMAX
     copies = [
         pltpu.make_async_copy(runs_ref, runs, sems.at[0]),
         pltpu.make_async_copy(offsets_ref, offsets, sems.at[1]),
     ]
     for copy in copies:
         copy.start()
-    seg, lag = lax.axis_index("seg"), lax.axis_index("lag")
-    rows, half = actuators // segs, chunk // 2
-    core = lag % 2
-    turned[:, pl.ds(pl.multiple_of(core * half, LANES), half)] = mine_ref[...].T
-    turned[:, pl.ds(pl.multiple_of((1 - core) * half, LANES), half)] = theirs_ref[...].T
-    turned[:, pl.ds(chunk, chunk)] = first_turned_ref[...]
+    actuators = inner_ref.shape[0] // lax.axis_size("lag")
+    lag, half = lax.axis_index("lag"), chunk // 2
+    for number, tail_ref in enumerate(tails):
+        place = (lag + number) % 2
+        put_turned(turned, pl.multiple_of(place * half, LANES), tail_ref[...])
     for copy in copies:
         copy.wait()
-    fill_rows(turned, chunk, masked, 0, runs, offsets, lag, steps, seg * samples, chunk)
-    for number, step in enumerate(steps):
-        here = pl.ds(number * actuators, actuators)
-        terms[here, :] = inner_ref[pl.ds(step * actuators, actuators), :]
+    fill_rows(turned, chunk, masked, 0, runs, offsets, lag, blocks, lax.axis_index("seg") * samples, chunk)
+    at = 0
+    for step, first, count in blocks:
+        terms[pl.ds(at, count), :] = inner_ref[pl.ds(step * actuators + first, count), :]
+        at += count
     terms[...] += jnp.dot(masked[...], sensed_ref[...], preferred_element_type=jnp.float32)
 
-    def block_of(number, block, near):
-        start = number * actuators + (2 * block + near) * rows
-        return terms[pl.ds(pl.multiple_of(start, rows), rows), :]
-
-    return block_of, rows, rows * (inner_ref.shape[1] // LANES)
-
-
-def outer_group_kernel(steps, samples, *refs):
-    far, inputs = lax.axis_size("seg") // 2, refs[:7]
-    send_ref, own_ref = refs[7:9]
-    block_of, rows, size = outer_terms(steps, samples, *inputs, *refs[-6:])
-    near_at = lax.axis_index("seg") % 2
+
+def outer_first_kernel(
+    steps, samples, turned_in_ref, runs_ref, offsets_ref, mine_ref, theirs_ref, sensed_ref, inner_ref,
+    turned, send_ref, *scratch
+):
+    far = lax.axis_size("seg") // 2
+    half = turned.shape[0] // 2
+    terms = scratch[3]
+    blocks = [(step, 0, half) for step in steps]
+    outer_terms(
+        blocks, samples, runs_ref, offsets_ref, turned, sensed_ref, inner_ref, *scratch, tails=(mine_ref, theirs_ref)
+    )
+    rows = half // far
+    size = rows * (terms.shape[1] // LANES)
     codes = []
     for number in range(len(steps)):
-        parts = [block_of(number, block, 1 - near_at) for block in range(far)]
+        parts = [terms[pl.ds(number * half + block * rows, rows), :] for block in range(far)]
         codes.append(put(send_ref, number * far * size, parts, size))
-        for block in range(far):
-            own_ref[pl.ds((number * far + block) * rows, rows), :] = block_of(number, block, near_at)
     put_codes(send_ref, len(steps) * far * size, codes)
 
 
-def outer_near_kernel(samples, *refs):
-    far, inputs = lax.axis_size("seg") // 2, refs[:7]
-    send_one_ref, send_own_ref, kept_one_ref, own_ref = refs[7:11]
-    block_of, rows, size = outer_terms((1, 0), samples, *inputs, *refs[-6:])
-    near_at = lax.axis_index("seg") % 2
-
-    def send(ref, number, near):
-        parts = [block_of(number, block, near) for block in range(far)]
+def outer_rest_kernel(
+    steps, samples, runs_ref, offsets_ref, turned, sensed_ref, inner_ref,
+    own_group_ref, send_one_ref, send_own_ref, kept_one_ref, own_ref, *scratch
+):
+    far = lax.axis_size("seg") // 2
+    actuators = turned.shape[0]
+    half = actuators // 2
+    terms = scratch[3]
+    blocks = [(1, 0, actuators), (0, 0, actuators)] + [(step, half, half) for step in steps]
+    outer_terms(blocks, samples, runs_ref, offsets_ref, turned, sensed_ref, inner_ref, *scratch)
+    rows = half // far
+    size = rows * (terms.shape[1] // LANES)
+
+    def send(ref, at):
+        parts = [terms[pl.ds(at + block * rows, rows), :] for block in range(far)]
         put_codes(ref, far * size, [put(ref, 0, parts, size)])
 
-    send(send_one_ref, 0, 1 - near_at)
-    send(send_own_ref, 1, 1 - near_at)
-    send(kept_one_ref, 0, near_at)
-    for block in range(far):
-        own_ref[pl.ds(block * rows, rows), :] = block_of(1, block, near_at)
+    send(send_one_ref, 0)
+    send(send_own_ref, actuators)
+    send(kept_one_ref, half)
+    own_ref[...] = terms[pl.ds(actuators + half, half), :]
+    own_group_ref[...] = terms[pl.ds(2 * actuators, len(steps) * half), :]
 
 
 def second_near_kernel(came_one_ref, came_own_ref, kept_one_ref, own_ref, total_ref, *far_refs):
@@ -363,20 +387,27 @@
 
 
 def last_kernel(scaling, steps, total_ref, *refs):
-    far, out_ref = lax.axis_size("seg") // 2, refs[-1]
-    came_far, came = refs[: far - 1], refs[far - 1 : -1]
+    far = lax.axis_size("seg") // 2
+    out_ref, ready, sems = refs[-3:]
+    came_far, came = refs[: far - 1], refs[far - 1 : -3]
     rows, sensors = total_ref.shape[0] // 2, total_ref.shape[1]
     size = rows * (sensors // LANES)
     lag = lax.axis_index("lag")
+    copies = []
 
     def write(step, value):
-        out_ref[:, 0, pl.ds(pl.multiple_of((lag ^ step) * sensors, LANES), sensors)] = value * scaling
+        there = pl.ds(pl.multiple_of((lag ^ step) * sensors, LANES), sensors)
+        ready[:, 0, there] = value * scaling
+        copies.append(pltpu.make_async_copy(ready.at[:, :, there], out_ref.at[:, :, there], sems.at[step]))
+        copies[-1].start()
 
     for number, step in enumerate(steps):
         write(step, opened(came[number], 0, scales_of(came[number], size, 1, sensors), 0, rows, sensors))
     scales = [scales_of(ref, 2 * size, 2, sensors) for ref in came_far]
     for step in range(2):
         write(step, far_sum(total_ref[pl.ds(step * rows, rows), :], came_far, scales, step, rows, sensors))
+    for copy in copies:
+        copy.wait()
 
 
 def per_device_staged(actuator_input, sensor_output, run_lengths, lag_offsets):
@@ -417,14 +448,17 @@
     fetched = shifted_by(cut, "seg", 1)
     swapped = exchange(fetched, 0, 1)
 
-    inner, first_turned, first_sensed = pl.pallas_call(
+    across = jax.ShapeDtypeStruct((actuators, 2 * chunk + LANES), jnp.bfloat16)
+    inner, first_turned, first_sensed, runs_held, offsets_held = pl.pallas_call(
         inner_kernel,
         in_specs=[hbm] * 4,
-        out_specs=[vmem] * 3,
+        out_specs=[vmem] * 5,
         out_shape=[
             jax.ShapeDtypeStruct((spare, sensors), jnp.float32),
-            jax.ShapeDtypeStruct((actuators, chunk), jnp.bfloat16),
+            across,
             jax.ShapeDtypeStruct((chunk, sensors), jnp.bfloat16),
+            jax.ShapeDtypeStruct(run_lengths.shape, jnp.int32),
+            jax.ShapeDtypeStruct(lag_offsets.shape, jnp.int32),
         ],
         scratch_shapes=scalars
         + [
@@ -432,7 +466,7 @@
             pltpu.VMEM((samples - chunk, sensors), jnp.bfloat16),
             pltpu.VMEM((actuators, samples + LANES), jnp.bfloat16),
             pltpu.VMEM((spare, samples - chunk), jnp.bfloat16),
-            pltpu.SemaphoreType.DMA((2 + 2 * chunks,)),
+            pltpu.SemaphoreType.DMA((4 + 2 * chunks,)),
         ],
         compiler_params=pltpu.CompilerParams(vmem_limit_bytes=40 << 20),
         cost_estimate=pl.CostEstimate(
@@ -441,25 +475,25 @@
         name="inner",
     )(run_lengths, lag_offsets, actuator_input, sensor_output)
 
-    def outer(name, body, count, shapes):
+    def outer(name, body, count, shapes, aliases, *operands):
         return pl.pallas_call(
             body,
-            in_specs=[hbm] * 2 + [vmem] * 5,
+            in_specs=[vmem] * len(operands),
             out_specs=[vmem] * len(shapes),
             out_shape=shapes,
+            input_output_aliases=aliases,
             scratch_shapes=scalars
             + [
-                pltpu.VMEM((actuators, 2 * chunk + LANES), jnp.bfloat16),
-                pltpu.VMEM((count * actuators, chunk), jnp.bfloat16),
-                pltpu.VMEM((count * actuators, sensors), jnp.float32),
+                pltpu.VMEM((count, chunk), jnp.bfloat16),
+                pltpu.VMEM((count, sensors), jnp.float32),
                 pltpu.SemaphoreType.DMA((2,)),
             ],
             compiler_params=pltpu.CompilerParams(vmem_limit_bytes=24 << 20),
             cost_estimate=pl.CostEstimate(
-                flops=2 * count * actuators * sensors * chunk, bytes_accessed=4 << 20, transcendentals=0
+                flops=2 * count * sensors * chunk, bytes_accessed=4 << 20, transcendentals=0
             ),
             name=name,
-        )(run_lengths, lag_offsets, fetched, swapped, first_turned, first_sensed, inner)
+        )(*operands)
 
     def local(name, body, shapes, *operands):
         return pl.pallas_call(
@@ -482,10 +516,10 @@
     count = len(steps)
 
     def outer_a(*refs):
-        outer_group_kernel(steps, samples, *refs)
+        outer_first_kernel(steps, samples, *refs)
 
     def outer_b(*refs):
-        outer_near_kernel(samples, *refs)
+        outer_rest_kernel(steps, samples, *refs)
 
     def second_a(*refs):
         second_kernel(count, *refs)
@@ -496,9 +530,33 @@
     def last_body(*refs):
         last_kernel(scaling, steps, *refs)
 
-    send_a, own_a = outer("outer_a", outer_a, count, [payload(count * far, count), wide(count * far)])
+    turned, send_a = outer(
+        "outer_a",
+        outer_a,
+        count * actuators // 2,
+        [across, payload(count * far, count)],
+        {0: 0},
+        first_turned,
+        runs_held,
+        offsets_held,
+        fetched,
+        swapped,
+        first_sensed,
+        inner,
+    )
     came_a = exchange(send_a, 1, 0)
-    send_one, send_own, kept_one, own_b = outer("outer_b", outer_b, 2, [payload(far, 1)] * 3 + [wide(far)])
+    own_a, send_one, send_own, kept_one, own_b = outer(
+        "outer_b",
+        outer_b,
+        (4 + count) * actuators // 2,
+        [wide(count * far)] + [payload(far, 1)] * 3 + [wide(far)],
+        {},
+        runs_held,
+        offsets_held,
+        turned,
+        first_sensed,
+        inner,
+    )
     came_one = exchange(send_one, 1, 1)
     came_own = exchange(send_own, 1, 0)
     kept_one = exchange(kept_one, 0, 1)
@@ -516,14 +574,18 @@
     far_b = far_exchange(sends_b)
     outs = local("third_a", third_a, [payload(1, 1)] * count, total_a, *far_a)
     came = [exchange(out, 0, step) for step, out in zip(steps, outs)]
-    return local(
-        "last",
+    return pl.pallas_call(
         last_body,
-        [jax.ShapeDtypeStruct((rows, 1, lags * sensors), jnp.float32)],
-        total_b,
-        *far_b,
-        *came,
-    )[0]
+        in_specs=[vmem] * (far + count),
+        out_specs=hbm,
+        out_shape=jax.ShapeDtypeStruct((rows, 1, lags * sensors), jnp.float32),
+        scratch_shapes=[
+            pltpu.VMEM((rows, 1, lags * sensors), jnp.float32),
+            pltpu.SemaphoreType.DMA((lags,)),
+        ],
+        compiler_params=small,
+        name="last",
+    )(total_b, *far_b, *came)
 
 
 def solution(mesh):

time: 46.7 us -> 46.3 us (level)
  waiting for transfers between devices: 11.9 us -> 13 us
  starting transfers between devices: 23.2 us -> 22.2 us
    ppermute x13, waiting for transfers between devices: 6.37 us -> 7.46 us  [exchange(): return lax.ppermute(value, ('seg', 'lag'), pairs)]
    ppermute x13, starting transfers between devices: 18.3 us -> 17.3 us  [exchange(): return lax.ppermute(value, ('seg', 'lag'), pairs)]
    pallas_call x4 -> x3, Pallas kernels: 1.36 us -> 0.53 us  [local(): pl.pallas_call(body, in_specs=[vmem] * len(operands), out_specs=[vmem] *...]
    pallas_call x3 -> x4, Pallas kernels: 9.01 us -> 9.37 us  [the longest x1 5.63 us: per_device_staged(): pl.pallas_call(inner_kernel, in_specs=[hbm] * 4, out_specs=[vmem] * 5, ou...]
  transfers between devices with their start and end apart: 14 -> 14, of which waited for: 4 -> 5; matrix products, arithmetic and copies ran while one was open for 0% -> 0% of each run, Pallas kernels for 17% -> 17%
where the time goes in v5:
time: 46.3 us; the launch traced here: 46.2 us
  starting transfers between devices  22.2 us (48%)
  waiting for transfers between devices  13 us (28%)
  Pallas kernels  10.9 us (24%)
    ppermute x13, starting transfers between devices, exchange(): return lax.ppermute(value, ('seg', 'lag'), pairs)  17.3 us
    ppermute x13, waiting for transfers between devices, exchange(): return lax.ppermute(value, ('seg', 'lag'), pairs)  7.46 us
    pallas_call x1, Pallas kernels, per_device_staged(): pl.pallas_call(inner_kernel, in_specs=[hbm] * 4, out_specs=[vmem] * 5, ou...  5.63 us
    ppermute x1, waiting for transfers between devices, shifted_by(): lax.ppermute(value, axis, [(source, source + steps) for source in range(i...  5.53 us
    ppermute x1, starting transfers between devices, shifted_by(): lax.ppermute(value, axis, [(source, source + steps) for source in range(i...  4.89 us
    pallas_call x2, Pallas kernels, outer(): pl.pallas_call(body, in_specs=[vmem] * len(operands), out_specs=[vmem] *...  2.95 us
    pallas_call x1, Pallas kernels, per_device_staged(): pl.pallas_call(cut_kernel, in_specs=[hbm], out_specs=vmem, out_shape=jax....  0.96 us
  transfers between devices with their start and end apart: 14, of which 5 were waited for; matrix products, arithmetic and copies ran while one was open for 0% of the time, Pallas kernels for 17%

profile of v5, /device:TPU:0, one launch (start us, length us, event | category | flops | bytes accessed | tf_op | source)
XLA Modules:
  0.0 46.2 jit_solution(3635409498175813350)
XLA Ops:
  0.0 1.0 %cut.1 = bf16[512,256]{1,0:T(8,128)(2,1)S(1)} custom-call(bf16[3072,256]{1,0:T(8,128)(2,1)} %actuators_ref.3), custom_call_target="tpu_custom_call" | custom-call | tf_op jit(solution)/shard_map/cut/pallas_call | solution.py:439
  1.0 4.9 %collective-permute-start = (bf16[512,256]{1,0:T(8,128)(2,1)S(1)}, bf16[512,256]{1,0:T(8,128)(2,1)S(1)}, u32[]{:S(2)}, u32[]{:S(2)}) collective-permute-start(bf16[512,256]{1,0:T(8,128)(2,1)S(1)} %cut.1), channel_id=1, source_target_pairs={{0,4},{4,8},{8,12},{12,16},{16,20},{20,24},{24,28},{1,5},{5,9},{9,... | collective-permute-start | bytes 786440 | tf_op jit(solution)/shard_map/ppermute | solution.py:42
  5.9 5.5 %collective-permute-done.refs_3_ = bf16[512,256]{1,0:T(8,128)(2,1)S(1)} collective-permute-done((bf16[512,256]{1,0:T(8,128)(2,1)S(1)}, bf16[512,256]{1,0:T(8,128)(2,1)S(1)}, u32[]{:S(2)}, u32[]{:S(2)}) %collective-permute-start) | collective-permute-done | bytes 262176 | tf_op jit(solution)/shard_map/ppermute | solution.py:42
  11.4 0.0 collective-permute-start.1
  11.4 5.6 %inner.1 = (f32[1024,512]{1,0:T(8,128)S(1)}, bf16[256,2176]{1,0:T(8,128)(2,1)S(1)}, bf16[1024,512]{1,0:T(8,128)(2,1)S(1)}, s32[4]{0:T(128)S(1)}, s32[2]{0:T(128)S(1)}) custom-call(s32[4]{0:T(128)} %runs_ref.1, s32[2]{0:T(128)} %offsets_ref.1, bf16[3072,256]{1,0:T(8,128)(2,1)} %actuators_ref.3, bf16[3072,512]{1,0:T(8,128)(2,1)} %sensors_ref.1), custom_call_target="tpu_custom_call" | custom-call | flops 2147483648 | bytes 6291456 | tf_op jit(solution)/shard_map/inner/pallas_call | solution.py:452
  17.0 0.0 collective-permute-done.1.refs_4_
  17.0 1.2 %outer_a.1 = (bf16[256,2176]{1,0:T(8,128)(2,1)S(1)}, s16[1032,128]{1,0:T(8,128)(2,1)S(1)}) custom-call(bf16[256,2176]{1,0:T(8,128)(2,1)S(1)} %get-tuple-element.29.refs_0_, s32[4]{0:T(128)S(1)} %get-tuple-element.27.refs_1_.refs_0_, s32[2]{0:T(128)S(1)} %get-tuple-element.28.refs_2_.refs_1_, ...), custom_call_target="tpu_custom_call", output_to_operand_aliasing={{0}: (0, {})} | custom-call | flops 268435456 | bytes 4194304 | tf_op jit(solution)/shard_map/outer_a/pallas_call | solution.py:479
  18.3 2.5 %collective-permute-start.8 = (s16[1032,128]{1,0:T(8,128)(2,1)S(1)}, s16[1032,128]{1,0:T(8,128)(2,1)S(1)}, u32[]{:S(2)}, u32[]{:S(2)}) collective-permute-start(s16[1032,128]{1,0:T(8,128)(2,1)S(1)} %get-tuple-element.41), channel_id=1, source_target_pairs={{0,4},{1,5},{2,6},{3,7},{4,0},{5,1},{6,2},{7,3},{8,12},{9,13},{10,... | collective-permute-start | bytes 792584 | tf_op jit(solution)/shard_map/ppermute | solution.py:89
  20.8 1.7 %outer_b.1 = (f32[256,512]{1,0:T(8,128)S(1)}, s16[520,128]{1,0:T(8,128)(2,1)S(1)}, s16[520,128]{1,0:T(8,128)(2,1)S(1)}, s16[520,128]{1,0:T(8,128)(2,1)S(1)}, f32[128,512]{1,0:T(8,128)S(1)}) custom-call(s32[4]{0:T(128)S(1)} %get-tuple-element.27.refs_1_.refs_0_, s32[2]{0:T(128)S(1)} %get-tuple-element.28.refs_2_.refs_1_, ...), custom_call_target="tpu_custom_call" | custom-call | flops 805306368 | bytes 4194304 | tf_op jit(solution)/shard_map/outer_b/pallas_call | solution.py:479
  22.6 0.2 collective-permute-start.2
  22.8 1.7 %collective-permute-start.3 = (s16[520,128]{1,0:T(8,128)(2,1)S(1)}, s16[520,128]{1,0:T(8,128)(2,1)S(1)}, u32[]{:S(2)}, u32[]{:S(2)}) collective-permute-start(s16[520,128]{1,0:T(8,128)(2,1)S(1)} %get-tuple-element.34), channel_id=1, source_target_pairs={{0,4},{1,5},{2,6},{3,7},{4,0},{5,1},{6,2},{7,3},{8,12},{9,13},{10,... | collective-permute-start | bytes 399368 | tf_op jit(solution)/shard_map/ppermute | solution.py:89
  24.5 0.0 collective-permute-start.4
  24.5 3.5 %collective-permute-done.8.refs_0_ = s16[1032,128]{1,0:T(8,128)(2,1)S(1)} collective-permute-done((s16[1032,128]{1,0:T(8,128)(2,1)S(1)}, s16[1032,128]{1,0:T(8,128)(2,1)S(1)}, u32[]{:S(2)}, u32[]{:S(2)}) %collective-permute-start.8) | collective-permute-done | bytes 264224 | tf_op jit(solution)/shard_map/ppermute | solution.py:89
  28.0 0.2 second_a.1
  28.2 3.1 %collective-permute-start.9 = (s16[264,128]{1,0:T(8,128)(2,1)S(1)}, s16[264,128]{1,0:T(8,128)(2,1)S(1)}, u32[]{:S(2)}, u32[]{:S(2)}) collective-permute-start(s16[264,128]{1,0:T(8,128)(2,1)S(1)} %get-tuple-element.44), channel_id=1, source_target_pairs={{0,8},{1,9},{2,10},{3,11},{4,12},{5,13},{6,14},{7,15},{8,0},{9,1},... | collective-permute-start | bytes 202760 | tf_op jit(solution)/shard_map/ppermute | solution.py:89
  31.3 2.6 %collective-permute-start.10 = (s16[264,128]{1,0:T(8,128)(2,1)S(1)}, s16[264,128]{1,0:T(8,128)(2,1)S(1)}, u32[]{:S(2)}, u32[]{:S(2)}) collective-permute-start(s16[264,128]{1,0:T(8,128)(2,1)S(1)} %get-tuple-element.45), channel_id=1, source_target_pairs={{0,16},{1,17},{2,18},{3,19},{4,20},{5,21},{6,22},{7,23},{8,24},{9,... | collective-permute-start | bytes 202760 | tf_op jit(solution)/shard_map/ppermute | solution.py:89
  33.9 0.0 collective-permute-done.2.came_one_ref
  33.9 1.1 %collective-permute-start.11 = (s16[264,128]{1,0:T(8,128)(2,1)S(1)}, s16[264,128]{1,0:T(8,128)(2,1)S(1)}, u32[]{:S(2)}, u32[]{:S(2)}) collective-permute-start(s16[264,128]{1,0:T(8,128)(2,1)S(1)} %get-tuple-element.46), channel_id=1, source_target_pairs={{0,24},{1,25},{2,26},{3,27},{4,28},{5,29},{6,30},{7,31},{8,16},{9,... | collective-permute-start | bytes 202760 | tf_op jit(solution)/shard_map/ppermute | solution.py:89
  35.0 0.0 collective-permute-done.3.came_own_ref
  35.0 0.0 collective-permute-done.4.kept_one_ref
  35.0 0.2 second_b.1
  35.2 1.4 %collective-permute-start.5 = (s16[264,128]{1,0:T(8,128)(2,1)S(1)}, s16[264,128]{1,0:T(8,128)(2,1)S(1)}, u32[]{:S(2)}, u32[]{:S(2)}) collective-permute-start(s16[264,128]{1,0:T(8,128)(2,1)S(1)} %get-tuple-element.38), channel_id=1, source_target_pairs={{0,8},{1,9},{2,10},{3,11},{4,12},{5,13},{6,14},{7,15},{8,0},{9,1},... | collective-permute-start | bytes 202760 | tf_op jit(solution)/shard_map/ppermute | solution.py:89
  36.6 2.6 %collective-permute-start.6 = (s16[264,128]{1,0:T(8,128)(2,1)S(1)}, s16[264,128]{1,0:T(8,128)(2,1)S(1)}, u32[]{:S(2)}, u32[]{:S(2)}) collective-permute-start(s16[264,128]{1,0:T(8,128)(2,1)S(1)} %get-tuple-element.39), channel_id=1, source_target_pairs={{0,16},{1,17},{2,18},{3,19},{4,20},{5,21},{6,22},{7,23},{8,24},{9,... | collective-permute-start | bytes 202760 | tf_op jit(solution)/shard_map/ppermute | solution.py:89
  39.2 0.0 collective-permute-done.9.refs_1_
  39.2 0.5 %collective-permute-start.7 = (s16[264,128]{1,0:T(8,128)(2,1)S(1)}, s16[264,128]{1,0:T(8,128)(2,1)S(1)}, u32[]{:S(2)}, u32[]{:S(2)}) collective-permute-start(s16[264,128]{1,0:T(8,128)(2,1)S(1)} %get-tuple-element.40), channel_id=1, source_target_pairs={{0,24},{1,25},{2,26},{3,27},{4,28},{5,29},{6,30},{7,31},{8,16},{9,... | collective-permute-start | bytes 202760 | tf_op jit(solution)/shard_map/ppermute | solution.py:89
  39.7 0.0 collective-permute-done.10.refs_2_
  39.7 1.0 %collective-permute-done.11.refs_3_ = s16[264,128]{1,0:T(8,128)(2,1)S(1)} collective-permute-done((s16[264,128]{1,0:T(8,128)(2,1)S(1)}, s16[264,128]{1,0:T(8,128)(2,1)S(1)}, u32[]{:S(2)}, u32[]{:S(2)}) %collective-permute-start.11) | collective-permute-done | bytes 67616 | tf_op jit(solution)/shard_map/ppermute | solution.py:89
  40.7 0.1 third_a.1
  40.8 0.1 collective-permute-start.12
  40.9 1.6 %collective-permute-start.13 = (s16[136,128]{1,0:T(8,128)(2,1)S(1)}, s16[136,128]{1,0:T(8,128)(2,1)S(1)}, u32[]{:S(2)}, u32[]{:S(2)}) collective-permute-start(s16[136,128]{1,0:T(8,128)(2,1)S(1)} %get-tuple-element.48), channel_id=1, source_target_pairs={{0,2},{1,3},{2,0},{3,1},{4,6},{5,7},{6,4},{7,5},{8,10},{9,11},{10,... | collective-permute-start | bytes 104456 | tf_op jit(solution)/shard_map/ppermute | solution.py:89
  42.5 0.0 collective-permute-done.5.refs_1_
  42.5 2.0 %collective-permute-done.6.refs_2_ = s16[264,128]{1,0:T(8,128)(2,1)S(1)} collective-permute-done((s16[264,128]{1,0:T(8,128)(2,1)S(1)}, s16[264,128]{1,0:T(8,128)(2,1)S(1)}, u32[]{:S(2)}, u32[]{:S(2)}) %collective-permute-start.6) | collective-permute-done | bytes 67616 | tf_op jit(solution)/shard_map/ppermute | solution.py:89
  44.4 0.9 %collective-permute-done.7.refs_3_ = s16[264,128]{1,0:T(8,128)(2,1)S(1)} collective-permute-done((s16[264,128]{1,0:T(8,128)(2,1)S(1)}, s16[264,128]{1,0:T(8,128)(2,1)S(1)}, u32[]{:S(2)}, u32[]{:S(2)}) %collective-permute-start.7) | collective-permute-done | bytes 67616 | tf_op jit(solution)/shard_map/ppermute | solution.py:89
  45.4 0.0 collective-permute-done.12.refs_4_
  45.4 0.0 collective-permute-done.13.refs_5_
  45.4 0.8 %last.1 = f32[32,1,2048]{2,1,0:T(1,128)} custom-call(f32[64,512]{1,0:T(8,128)S(1)} %get-tuple-element.37.refs_0_, s16[264,128]{1,0:T(8,128)(2,1)S(1)} %collective-permute-done.5.refs_1_, s16[264,128]{1,0:T(8,128)(2,1)S(1)} %collective-permute-done.6.refs_2_, s16[264,128]{1,0:T(8,128)(2,1)S(1)} %collective-permute-done.7.refs_3_, ...), custom_call_target="tpu_custom_call" | custom-call | tf_op jit(solution)/shard_map/last/pallas_call | solution.py:577
Async XLA Ops:
  1.0 10.4 %collective-permute-start = (bf16[512,256]{1,0:T(8,128)(2,1)S(1)}, bf16[512,256]{1,0:T(8,128)(2,1)S(1)}, u32[]{:S(2)}, u32[]{:S(2)}) collective-permute-start(bf16[512,256]{1,0:T(8,128)(2,1)S(1)} %cut.1), channel_id=1, source_target_pairs={{0,4},{4,8},{8,12},{12,16},{16,20},{20,24},{24,28},{1,5},{5,9},{9,... | collective-permute-start | bytes 786440 | tf_op jit(solution)/shard_map/ppermute | solution.py:42
  11.4 5.6 %collective-permute-start.1 = (bf16[512,256]{1,0:T(8,128)(2,1)S(1)}, bf16[512,256]{1,0:T(8,128)(2,1)S(1)}, u32[]{:S(2)}, u32[]{:S(2)}) collective-permute-start(bf16[512,256]{1,0:T(8,128)(2,1)S(1)} %collective-permute-done.refs_3_), channel_id=1, source_target_pairs={{0,1},{1,0},{2,3},{3,2},{4,5},{5,4},{6,7},{7,6},{8,9},{9,8},{10,11... | collective-permute-start | bytes 786440 | tf_op jit(solution)/shard_map/ppermute | solution.py:89
  18.3 9.8 %collective-permute-start.8 = (s16[1032,128]{1,0:T(8,128)(2,1)S(1)}, s16[1032,128]{1,0:T(8,128)(2,1)S(1)}, u32[]{:S(2)}, u32[]{:S(2)}) collective-permute-start(s16[1032,128]{1,0:T(8,128)(2,1)S(1)} %get-tuple-element.41), channel_id=1, source_target_pairs={{0,4},{1,5},{2,6},{3,7},{4,0},{5,1},{6,2},{7,3},{8,12},{9,13},{10,... | collective-permute-start | bytes 792584 | tf_op jit(solution)/shard_map/ppermute | solution.py:89
  22.6 11.3 %collective-permute-start.2 = (s16[520,128]{1,0:T(8,128)(2,1)S(1)}, s16[520,128]{1,0:T(8,128)(2,1)S(1)}, u32[]{:S(2)}, u32[]{:S(2)}) collective-permute-start(s16[520,128]{1,0:T(8,128)(2,1)S(1)} %get-tuple-element.33), channel_id=1, source_target_pairs={{0,5},{1,4},{2,7},{3,6},{4,1},{5,0},{6,3},{7,2},{8,13},{9,12},{10,... | collective-permute-start | bytes 399368 | tf_op jit(solution)/shard_map/ppermute | solution.py:89
  22.8 12.2 %collective-permute-start.3 = (s16[520,128]{1,0:T(8,128)(2,1)S(1)}, s16[520,128]{1,0:T(8,128)(2,1)S(1)}, u32[]{:S(2)}, u32[]{:S(2)}) collective-permute-start(s16[520,128]{1,0:T(8,128)(2,1)S(1)} %get-tuple-element.34), channel_id=1, source_target_pairs={{0,4},{1,5},{2,6},{3,7},{4,0},{5,1},{6,2},{7,3},{8,12},{9,13},{10,... | collective-permute-start | bytes 399368 | tf_op jit(solution)/shard_map/ppermute | solution.py:89
  24.5 10.5 %collective-permute-start.4 = (s16[520,128]{1,0:T(8,128)(2,1)S(1)}, s16[520,128]{1,0:T(8,128)(2,1)S(1)}, u32[]{:S(2)}, u32[]{:S(2)}) collective-permute-start(s16[520,128]{1,0:T(8,128)(2,1)S(1)} %get-tuple-element.35), channel_id=1, source_target_pairs={{0,1},{1,0},{2,3},{3,2},{4,5},{5,4},{6,7},{7,6},{8,9},{9,8},{10,11... | collective-permute-start | bytes 399368 | tf_op jit(solution)/shard_map/ppermute | solution.py:89
  28.2 10.9 %collective-permute-start.9 = (s16[264,128]{1,0:T(8,128)(2,1)S(1)}, s16[264,128]{1,0:T(8,128)(2,1)S(1)}, u32[]{:S(2)}, u32[]{:S(2)}) collective-permute-start(s16[264,128]{1,0:T(8,128)(2,1)S(1)} %get-tuple-element.44), channel_id=1, source_target_pairs={{0,8},{1,9},{2,10},{3,11},{4,12},{5,13},{6,14},{7,15},{8,0},{9,1},... | collective-permute-start | bytes 202760 | tf_op jit(solution)/shard_map/ppermute | solution.py:89
  31.3 8.4 %collective-permute-start.10 = (s16[264,128]{1,0:T(8,128)(2,1)S(1)}, s16[264,128]{1,0:T(8,128)(2,1)S(1)}, u32[]{:S(2)}, u32[]{:S(2)}) collective-permute-start(s16[264,128]{1,0:T(8,128)(2,1)S(1)} %get-tuple-element.45), channel_id=1, source_target_pairs={{0,16},{1,17},{2,18},{3,19},{4,20},{5,21},{6,22},{7,23},{8,24},{9,... | collective-permute-start | bytes 202760 | tf_op jit(solution)/shard_map/ppermute | solution.py:89
  33.9 6.8 %collective-permute-start.11 = (s16[264,128]{1,0:T(8,128)(2,1)S(1)}, s16[264,128]{1,0:T(8,128)(2,1)S(1)}, u32[]{:S(2)}, u32[]{:S(2)}) collective-permute-start(s16[264,128]{1,0:T(8,128)(2,1)S(1)} %get-tuple-element.46), channel_id=1, source_target_pairs={{0,24},{1,25},{2,26},{3,27},{4,28},{5,29},{6,30},{7,31},{8,16},{9,... | collective-permute-start | bytes 202760 | tf_op jit(solution)/shard_map/ppermute | solution.py:89
  35.2 7.3 %collective-permute-start.5 = (s16[264,128]{1,0:T(8,128)(2,1)S(1)}, s16[264,128]{1,0:T(8,128)(2,1)S(1)}, u32[]{:S(2)}, u32[]{:S(2)}) collective-permute-start(s16[264,128]{1,0:T(8,128)(2,1)S(1)} %get-tuple-element.38), channel_id=1, source_target_pairs={{0,8},{1,9},{2,10},{3,11},{4,12},{5,13},{6,14},{7,15},{8,0},{9,1},... | collective-permute-start | bytes 202760 | tf_op jit(solution)/shard_map/ppermute | solution.py:89
  36.6 7.9 %collective-permute-start.6 = (s16[264,128]{1,0:T(8,128)(2,1)S(1)}, s16[264,128]{1,0:T(8,128)(2,1)S(1)}, u32[]{:S(2)}, u32[]{:S(2)}) collective-permute-start(s16[264,128]{1,0:T(8,128)(2,1)S(1)} %get-tuple-element.39), channel_id=1, source_target_pairs={{0,16},{1,17},{2,18},{3,19},{4,20},{5,21},{6,22},{7,23},{8,24},{9,... | collective-permute-start | bytes 202760 | tf_op jit(solution)/shard_map/ppermute | solution.py:89
  39.2 6.2 %collective-permute-start.7 = (s16[264,128]{1,0:T(8,128)(2,1)S(1)}, s16[264,128]{1,0:T(8,128)(2,1)S(1)}, u32[]{:S(2)}, u32[]{:S(2)}) collective-permute-start(s16[264,128]{1,0:T(8,128)(2,1)S(1)} %get-tuple-element.40), channel_id=1, source_target_pairs={{0,24},{1,25},{2,26},{3,27},{4,28},{5,29},{6,30},{7,31},{8,16},{9,... | collective-permute-start | bytes 202760 | tf_op jit(solution)/shard_map/ppermute | solution.py:89
  40.8 4.6 %collective-permute-start.12 = (s16[136,128]{1,0:T(8,128)(2,1)S(1)}, s16[136,128]{1,0:T(8,128)(2,1)S(1)}, u32[]{:S(2)}, u32[]{:S(2)}) collective-permute-start(s16[136,128]{1,0:T(8,128)(2,1)S(1)} %get-tuple-element.47), channel_id=1, source_target_pairs={{0,3},{1,2},{2,1},{3,0},{4,7},{5,6},{6,5},{7,4},{8,11},{9,10},{10,... | collective-permute-start | bytes 104456 | tf_op jit(solution)/shard_map/ppermute | solution.py:89
  40.9 4.5 %collective-permute-start.13 = (s16[136,128]{1,0:T(8,128)(2,1)S(1)}, s16[136,128]{1,0:T(8,128)(2,1)S(1)}, u32[]{:S(2)}, u32[]{:S(2)}) collective-permute-start(s16[136,128]{1,0:T(8,128)(2,1)S(1)} %get-tuple-element.48), channel_id=1, source_target_pairs={{0,2},{1,3},{2,0},{3,1},{4,6},{5,7},{6,4},{7,5},{8,10},{9,11},{10,... | collective-permute-start | bytes 104456 | tf_op jit(solution)/shard_map/ppermute | solution.py:89

commit v6 on v5

--- a/solution.py
+++ b/solution.py
@@ -506,9 +506,9 @@
             name=name,
         )(*operands)
 
-    def far_exchange(sends):
+    def far_exchange(sends, masks):
         came = [None] * (far - 1)
-        for bits in range(far - 1, 0, -1):
+        for bits in masks:
             came[bits - 1] = exchange(sends[bits - 1], 2 * bits, 0)
         return came
 
@@ -561,7 +561,7 @@
     came_own = exchange(send_own, 1, 0)
     kept_one = exchange(kept_one, 0, 1)
     total_a, *sends_a = local("second_a", second_a, [wide(count)] + [payload(count, count)] * (far - 1), came_a, own_a)
-    far_a = far_exchange(sends_a)
+    far_a = far_exchange(sends_a, (2, 3, 1))
     total_b, *sends_b = local(
         "second_b",
         second_near_kernel,
@@ -571,7 +571,7 @@
         kept_one,
         own_b,
     )
-    far_b = far_exchange(sends_b)
+    far_b = far_exchange(sends_b, (3, 1, 2))
     outs = local("third_a", third_a, [payload(1, 1)] * count, total_a, *far_a)
     came = [exchange(out, 0, step) for step, out in zip(steps, outs)]
     return pl.pallas_call(

time: 46.3 us -> 46.3 us (level)
  no operation moved by 1% of the time
where the time goes in v6:
time: 46.3 us; the launch traced here: 46.2 us
  starting transfers between devices  22.2 us (48%)
  waiting for transfers between devices  13 us (28%)
  Pallas kernels  10.9 us (24%)
    ppermute x13, starting transfers between devices, exchange(): return lax.ppermute(value, ('seg', 'lag'), pairs)  17.3 us
    ppermute x13, waiting for transfers between devices, exchange(): return lax.ppermute(value, ('seg', 'lag'), pairs)  7.46 us
    pallas_call x1, Pallas kernels, per_device_staged(): pl.pallas_call(inner_kernel, in_specs=[hbm] * 4, out_specs=[vmem] * 5, ou...  5.63 us
    ppermute x1, waiting for transfers between devices, shifted_by(): lax.ppermute(value, axis, [(source, source + steps) for source in range(i...  5.53 us
    ppermute x1, starting transfers between devices, shifted_by(): lax.ppermute(value, axis, [(source, source + steps) for source in range(i...  4.89 us
    pallas_call x2, Pallas kernels, outer(): pl.pallas_call(body, in_specs=[vmem] * len(operands), out_specs=[vmem] *...  2.95 us
    pallas_call x1, Pallas kernels, per_device_staged(): pl.pallas_call(cut_kernel, in_specs=[hbm], out_specs=vmem, out_shape=jax....  0.96 us
  transfers between devices with their start and end apart: 14, of which 5 were waited for; matrix products, arithmetic and copies ran while one was open for 0% of the time, Pallas kernels for 17%

profile of v6, /device:TPU:0, one launch (start us, length us, event | category | flops | bytes accessed | tf_op | source)
XLA Modules:
  0.0 46.2 jit_solution(3635409498175813350)
XLA Ops:
  0.0 1.0 %cut.1 = bf16[512,256]{1,0:T(8,128)(2,1)S(1)} custom-call(bf16[3072,256]{1,0:T(8,128)(2,1)} %actuators_ref.3), custom_call_target="tpu_custom_call" | custom-call | tf_op jit(solution)/shard_map/cut/pallas_call | solution.py:439
  1.0 4.9 %collective-permute-start = (bf16[512,256]{1,0:T(8,128)(2,1)S(1)}, bf16[512,256]{1,0:T(8,128)(2,1)S(1)}, u32[]{:S(2)}, u32[]{:S(2)}) collective-permute-start(bf16[512,256]{1,0:T(8,128)(2,1)S(1)} %cut.1), channel_id=1, source_target_pairs={{0,4},{4,8},{8,12},{12,16},{16,20},{20,24},{24,28},{1,5},{5,9},{9,... | collective-permute-start | bytes 786440 | tf_op jit(solution)/shard_map/ppermute | solution.py:42
  5.9 5.5 %collective-permute-done.refs_3_ = bf16[512,256]{1,0:T(8,128)(2,1)S(1)} collective-permute-done((bf16[512,256]{1,0:T(8,128)(2,1)S(1)}, bf16[512,256]{1,0:T(8,128)(2,1)S(1)}, u32[]{:S(2)}, u32[]{:S(2)}) %collective-permute-start) | collective-permute-done | bytes 262176 | tf_op jit(solution)/shard_map/ppermute | solution.py:42
  11.4 0.0 collective-permute-start.1
  11.4 5.6 %inner.1 = (f32[1024,512]{1,0:T(8,128)S(1)}, bf16[256,2176]{1,0:T(8,128)(2,1)S(1)}, bf16[1024,512]{1,0:T(8,128)(2,1)S(1)}, s32[4]{0:T(128)S(1)}, s32[2]{0:T(128)S(1)}) custom-call(s32[4]{0:T(128)} %runs_ref.1, s32[2]{0:T(128)} %offsets_ref.1, bf16[3072,256]{1,0:T(8,128)(2,1)} %actuators_ref.3, bf16[3072,512]{1,0:T(8,128)(2,1)} %sensors_ref.1), custom_call_target="tpu_custom_call" | custom-call | flops 2147483648 | bytes 6291456 | tf_op jit(solution)/shard_map/inner/pallas_call | solution.py:452
  17.0 0.0 collective-permute-done.1.refs_4_
  17.0 1.2 %outer_a.1 = (bf16[256,2176]{1,0:T(8,128)(2,1)S(1)}, s16[1032,128]{1,0:T(8,128)(2,1)S(1)}) custom-call(bf16[256,2176]{1,0:T(8,128)(2,1)S(1)} %get-tuple-element.29.refs_0_, s32[4]{0:T(128)S(1)} %get-tuple-element.27.refs_1_.refs_0_, s32[2]{0:T(128)S(1)} %get-tuple-element.28.refs_2_.refs_1_, ...), custom_call_target="tpu_custom_call", output_to_operand_aliasing={{0}: (0, {})} | custom-call | flops 268435456 | bytes 4194304 | tf_op jit(solution)/shard_map/outer_a/pallas_call | solution.py:479
  18.3 2.5 %collective-permute-start.8 = (s16[1032,128]{1,0:T(8,128)(2,1)S(1)}, s16[1032,128]{1,0:T(8,128)(2,1)S(1)}, u32[]{:S(2)}, u32[]{:S(2)}) collective-permute-start(s16[1032,128]{1,0:T(8,128)(2,1)S(1)} %get-tuple-element.41), channel_id=1, source_target_pairs={{0,4},{1,5},{2,6},{3,7},{4,0},{5,1},{6,2},{7,3},{8,12},{9,13},{10,... | collective-permute-start | bytes 792584 | tf_op jit(solution)/shard_map/ppermute | solution.py:89
  20.8 1.7 %outer_b.1 = (f32[256,512]{1,0:T(8,128)S(1)}, s16[520,128]{1,0:T(8,128)(2,1)S(1)}, s16[520,128]{1,0:T(8,128)(2,1)S(1)}, s16[520,128]{1,0:T(8,128)(2,1)S(1)}, f32[128,512]{1,0:T(8,128)S(1)}) custom-call(s32[4]{0:T(128)S(1)} %get-tuple-element.27.refs_1_.refs_0_, s32[2]{0:T(128)S(1)} %get-tuple-element.28.refs_2_.refs_1_, ...), custom_call_target="tpu_custom_call" | custom-call | flops 805306368 | bytes 4194304 | tf_op jit(solution)/shard_map/outer_b/pallas_call | solution.py:479
  22.6 0.2 collective-permute-start.2
  22.8 1.7 %collective-permute-start.3 = (s16[520,128]{1,0:T(8,128)(2,1)S(1)}, s16[520,128]{1,0:T(8,128)(2,1)S(1)}, u32[]{:S(2)}, u32[]{:S(2)}) collective-permute-start(s16[520,128]{1,0:T(8,128)(2,1)S(1)} %get-tuple-element.34), channel_id=1, source_target_pairs={{0,4},{1,5},{2,6},{3,7},{4,0},{5,1},{6,2},{7,3},{8,12},{9,13},{10,... | collective-permute-start | bytes 399368 | tf_op jit(solution)/shard_map/ppermute | solution.py:89
  24.5 0.0 collective-permute-start.4
  24.5 3.5 %collective-permute-done.8.refs_0_ = s16[1032,128]{1,0:T(8,128)(2,1)S(1)} collective-permute-done((s16[1032,128]{1,0:T(8,128)(2,1)S(1)}, s16[1032,128]{1,0:T(8,128)(2,1)S(1)}, u32[]{:S(2)}, u32[]{:S(2)}) %collective-permute-start.8) | collective-permute-done | bytes 264224 | tf_op jit(solution)/shard_map/ppermute | solution.py:89
  28.0 0.2 second_a.1
  28.2 3.1 %collective-permute-start.9 = (s16[264,128]{1,0:T(8,128)(2,1)S(1)}, s16[264,128]{1,0:T(8,128)(2,1)S(1)}, u32[]{:S(2)}, u32[]{:S(2)}) collective-permute-start(s16[264,128]{1,0:T(8,128)(2,1)S(1)} %get-tuple-element.44), channel_id=1, source_target_pairs={{0,8},{1,9},{2,10},{3,11},{4,12},{5,13},{6,14},{7,15},{8,0},{9,1},... | collective-permute-start | bytes 202760 | tf_op jit(solution)/shard_map/ppermute | solution.py:89
  31.3 2.6 %collective-permute-start.10 = (s16[264,128]{1,0:T(8,128)(2,1)S(1)}, s16[264,128]{1,0:T(8,128)(2,1)S(1)}, u32[]{:S(2)}, u32[]{:S(2)}) collective-permute-start(s16[264,128]{1,0:T(8,128)(2,1)S(1)} %get-tuple-element.45), channel_id=1, source_target_pairs={{0,16},{1,17},{2,18},{3,19},{4,20},{5,21},{6,22},{7,23},{8,24},{9,... | collective-permute-start | bytes 202760 | tf_op jit(solution)/shard_map/ppermute | solution.py:89
  33.9 0.0 collective-permute-done.2.came_one_ref
  33.9 1.1 %collective-permute-start.11 = (s16[264,128]{1,0:T(8,128)(2,1)S(1)}, s16[264,128]{1,0:T(8,128)(2,1)S(1)}, u32[]{:S(2)}, u32[]{:S(2)}) collective-permute-start(s16[264,128]{1,0:T(8,128)(2,1)S(1)} %get-tuple-element.46), channel_id=1, source_target_pairs={{0,24},{1,25},{2,26},{3,27},{4,28},{5,29},{6,30},{7,31},{8,16},{9,... | collective-permute-start | bytes 202760 | tf_op jit(solution)/shard_map/ppermute | solution.py:89
  35.0 0.0 collective-permute-done.3.came_own_ref
  35.0 0.0 collective-permute-done.4.kept_one_ref
  35.0 0.2 second_b.1
  35.2 1.4 %collective-permute-start.5 = (s16[264,128]{1,0:T(8,128)(2,1)S(1)}, s16[264,128]{1,0:T(8,128)(2,1)S(1)}, u32[]{:S(2)}, u32[]{:S(2)}) collective-permute-start(s16[264,128]{1,0:T(8,128)(2,1)S(1)} %get-tuple-element.38), channel_id=1, source_target_pairs={{0,8},{1,9},{2,10},{3,11},{4,12},{5,13},{6,14},{7,15},{8,0},{9,1},... | collective-permute-start | bytes 202760 | tf_op jit(solution)/shard_map/ppermute | solution.py:89
  36.6 2.6 %collective-permute-start.6 = (s16[264,128]{1,0:T(8,128)(2,1)S(1)}, s16[264,128]{1,0:T(8,128)(2,1)S(1)}, u32[]{:S(2)}, u32[]{:S(2)}) collective-permute-start(s16[264,128]{1,0:T(8,128)(2,1)S(1)} %get-tuple-element.39), channel_id=1, source_target_pairs={{0,16},{1,17},{2,18},{3,19},{4,20},{5,21},{6,22},{7,23},{8,24},{9,... | collective-permute-start | bytes 202760 | tf_op jit(solution)/shard_map/ppermute | solution.py:89
  39.2 0.0 collective-permute-done.9.refs_1_
  39.2 0.5 %collective-permute-start.7 = (s16[264,128]{1,0:T(8,128)(2,1)S(1)}, s16[264,128]{1,0:T(8,128)(2,1)S(1)}, u32[]{:S(2)}, u32[]{:S(2)}) collective-permute-start(s16[264,128]{1,0:T(8,128)(2,1)S(1)} %get-tuple-element.40), channel_id=1, source_target_pairs={{0,24},{1,25},{2,26},{3,27},{4,28},{5,29},{6,30},{7,31},{8,16},{9,... | collective-permute-start | bytes 202760 | tf_op jit(solution)/shard_map/ppermute | solution.py:89
  39.7 0.0 collective-permute-done.10.refs_2_
  39.7 1.0 %collective-permute-done.11.refs_3_ = s16[264,128]{1,0:T(8,128)(2,1)S(1)} collective-permute-done((s16[264,128]{1,0:T(8,128)(2,1)S(1)}, s16[264,128]{1,0:T(8,128)(2,1)S(1)}, u32[]{:S(2)}, u32[]{:S(2)}) %collective-permute-start.11) | collective-permute-done | bytes 67616 | tf_op jit(solution)/shard_map/ppermute | solution.py:89
  40.7 0.1 third_a.1
  40.8 0.1 collective-permute-start.12
  40.9 1.6 %collective-permute-start.13 = (s16[136,128]{1,0:T(8,128)(2,1)S(1)}, s16[136,128]{1,0:T(8,128)(2,1)S(1)}, u32[]{:S(2)}, u32[]{:S(2)}) collective-permute-start(s16[136,128]{1,0:T(8,128)(2,1)S(1)} %get-tuple-element.48), channel_id=1, source_target_pairs={{0,2},{1,3},{2,0},{3,1},{4,6},{5,7},{6,4},{7,5},{8,10},{9,11},{10,... | collective-permute-start | bytes 104456 | tf_op jit(solution)/shard_map/ppermute | solution.py:89
  42.5 0.0 collective-permute-done.5.refs_1_
  42.5 2.0 %collective-permute-done.6.refs_2_ = s16[264,128]{1,0:T(8,128)(2,1)S(1)} collective-permute-done((s16[264,128]{1,0:T(8,128)(2,1)S(1)}, s16[264,128]{1,0:T(8,128)(2,1)S(1)}, u32[]{:S(2)}, u32[]{:S(2)}) %collective-permute-start.6) | collective-permute-done | bytes 67616 | tf_op jit(solution)/shard_map/ppermute | solution.py:89
  44.4 0.9 %collective-permute-done.7.refs_3_ = s16[264,128]{1,0:T(8,128)(2,1)S(1)} collective-permute-done((s16[264,128]{1,0:T(8,128)(2,1)S(1)}, s16[264,128]{1,0:T(8,128)(2,1)S(1)}, u32[]{:S(2)}, u32[]{:S(2)}) %collective-permute-start.7) | collective-permute-done | bytes 67616 | tf_op jit(solution)/shard_map/ppermute | solution.py:89
  45.4 0.0 collective-permute-done.12.refs_4_
  45.4 0.0 collective-permute-done.13.refs_5_
  45.4 0.8 %last.1 = f32[32,1,2048]{2,1,0:T(1,128)} custom-call(f32[64,512]{1,0:T(8,128)S(1)} %get-tuple-element.37.refs_0_, s16[264,128]{1,0:T(8,128)(2,1)S(1)} %collective-permute-done.5.refs_1_, s16[264,128]{1,0:T(8,128)(2,1)S(1)} %collective-permute-done.6.refs_2_, s16[264,128]{1,0:T(8,128)(2,1)S(1)} %collective-permute-done.7.refs_3_, ...), custom_call_target="tpu_custom_call" | custom-call | tf_op jit(solution)/shard_map/last/pallas_call | solution.py:577
Async XLA Ops:
  1.0 10.4 %collective-permute-start = (bf16[512,256]{1,0:T(8,128)(2,1)S(1)}, bf16[512,256]{1,0:T(8,128)(2,1)S(1)}, u32[]{:S(2)}, u32[]{:S(2)}) collective-permute-start(bf16[512,256]{1,0:T(8,128)(2,1)S(1)} %cut.1), channel_id=1, source_target_pairs={{0,4},{4,8},{8,12},{12,16},{16,20},{20,24},{24,28},{1,5},{5,9},{9,... | collective-permute-start | bytes 786440 | tf_op jit(solution)/shard_map/ppermute | solution.py:42
  11.4 5.6 %collective-permute-start.1 = (bf16[512,256]{1,0:T(8,128)(2,1)S(1)}, bf16[512,256]{1,0:T(8,128)(2,1)S(1)}, u32[]{:S(2)}, u32[]{:S(2)}) collective-permute-start(bf16[512,256]{1,0:T(8,128)(2,1)S(1)} %collective-permute-done.refs_3_), channel_id=1, source_target_pairs={{0,1},{1,0},{2,3},{3,2},{4,5},{5,4},{6,7},{7,6},{8,9},{9,8},{10,11... | collective-permute-start | bytes 786440 | tf_op jit(solution)/shard_map/ppermute | solution.py:89
  18.3 9.8 %collective-permute-start.8 = (s16[1032,128]{1,0:T(8,128)(2,1)S(1)}, s16[1032,128]{1,0:T(8,128)(2,1)S(1)}, u32[]{:S(2)}, u32[]{:S(2)}) collective-permute-start(s16[1032,128]{1,0:T(8,128)(2,1)S(1)} %get-tuple-element.41), channel_id=1, source_target_pairs={{0,4},{1,5},{2,6},{3,7},{4,0},{5,1},{6,2},{7,3},{8,12},{9,13},{10,... | collective-permute-start | bytes 792584 | tf_op jit(solution)/shard_map/ppermute | solution.py:89
  22.6 11.3 %collective-permute-start.2 = (s16[520,128]{1,0:T(8,128)(2,1)S(1)}, s16[520,128]{1,0:T(8,128)(2,1)S(1)}, u32[]{:S(2)}, u32[]{:S(2)}) collective-permute-start(s16[520,128]{1,0:T(8,128)(2,1)S(1)} %get-tuple-element.33), channel_id=1, source_target_pairs={{0,5},{1,4},{2,7},{3,6},{4,1},{5,0},{6,3},{7,2},{8,13},{9,12},{10,... | collective-permute-start | bytes 399368 | tf_op jit(solution)/shard_map/ppermute | solution.py:89
  22.8 12.2 %collective-permute-start.3 = (s16[520,128]{1,0:T(8,128)(2,1)S(1)}, s16[520,128]{1,0:T(8,128)(2,1)S(1)}, u32[]{:S(2)}, u32[]{:S(2)}) collective-permute-start(s16[520,128]{1,0:T(8,128)(2,1)S(1)} %get-tuple-element.34), channel_id=1, source_target_pairs={{0,4},{1,5},{2,6},{3,7},{4,0},{5,1},{6,2},{7,3},{8,12},{9,13},{10,... | collective-permute-start | bytes 399368 | tf_op jit(solution)/shard_map/ppermute | solution.py:89
  24.5 10.5 %collective-permute-start.4 = (s16[520,128]{1,0:T(8,128)(2,1)S(1)}, s16[520,128]{1,0:T(8,128)(2,1)S(1)}, u32[]{:S(2)}, u32[]{:S(2)}) collective-permute-start(s16[520,128]{1,0:T(8,128)(2,1)S(1)} %get-tuple-element.35), channel_id=1, source_target_pairs={{0,1},{1,0},{2,3},{3,2},{4,5},{5,4},{6,7},{7,6},{8,9},{9,8},{10,11... | collective-permute-start | bytes 399368 | tf_op jit(solution)/shard_map/ppermute | solution.py:89
  28.2 10.9 %collective-permute-start.9 = (s16[264,128]{1,0:T(8,128)(2,1)S(1)}, s16[264,128]{1,0:T(8,128)(2,1)S(1)}, u32[]{:S(2)}, u32[]{:S(2)}) collective-permute-start(s16[264,128]{1,0:T(8,128)(2,1)S(1)} %get-tuple-element.44), channel_id=1, source_target_pairs={{0,8},{1,9},{2,10},{3,11},{4,12},{5,13},{6,14},{7,15},{8,0},{9,1},... | collective-permute-start | bytes 202760 | tf_op jit(solution)/shard_map/ppermute | solution.py:89
  31.3 8.4 %collective-permute-start.10 = (s16[264,128]{1,0:T(8,128)(2,1)S(1)}, s16[264,128]{1,0:T(8,128)(2,1)S(1)}, u32[]{:S(2)}, u32[]{:S(2)}) collective-permute-start(s16[264,128]{1,0:T(8,128)(2,1)S(1)} %get-tuple-element.45), channel_id=1, source_target_pairs={{0,16},{1,17},{2,18},{3,19},{4,20},{5,21},{6,22},{7,23},{8,24},{9,... | collective-permute-start | bytes 202760 | tf_op jit(solution)/shard_map/ppermute | solution.py:89
  33.9 6.8 %collective-permute-start.11 = (s16[264,128]{1,0:T(8,128)(2,1)S(1)}, s16[264,128]{1,0:T(8,128)(2,1)S(1)}, u32[]{:S(2)}, u32[]{:S(2)}) collective-permute-start(s16[264,128]{1,0:T(8,128)(2,1)S(1)} %get-tuple-element.46), channel_id=1, source_target_pairs={{0,24},{1,25},{2,26},{3,27},{4,28},{5,29},{6,30},{7,31},{8,16},{9,... | collective-permute-start | bytes 202760 | tf_op jit(solution)/shard_map/ppermute | solution.py:89
  35.2 7.3 %collective-permute-start.5 = (s16[264,128]{1,0:T(8,128)(2,1)S(1)}, s16[264,128]{1,0:T(8,128)(2,1)S(1)}, u32[]{:S(2)}, u32[]{:S(2)}) collective-permute-start(s16[264,128]{1,0:T(8,128)(2,1)S(1)} %get-tuple-element.38), channel_id=1, source_target_pairs={{0,8},{1,9},{2,10},{3,11},{4,12},{5,13},{6,14},{7,15},{8,0},{9,1},... | collective-permute-start | bytes 202760 | tf_op jit(solution)/shard_map/ppermute | solution.py:89
  36.6 7.9 %collective-permute-start.6 = (s16[264,128]{1,0:T(8,128)(2,1)S(1)}, s16[264,128]{1,0:T(8,128)(2,1)S(1)}, u32[]{:S(2)}, u32[]{:S(2)}) collective-permute-start(s16[264,128]{1,0:T(8,128)(2,1)S(1)} %get-tuple-element.39), channel_id=1, source_target_pairs={{0,16},{1,17},{2,18},{3,19},{4,20},{5,21},{6,22},{7,23},{8,24},{9,... | collective-permute-start | bytes 202760 | tf_op jit(solution)/shard_map/ppermute | solution.py:89
  39.2 6.2 %collective-permute-start.7 = (s16[264,128]{1,0:T(8,128)(2,1)S(1)}, s16[264,128]{1,0:T(8,128)(2,1)S(1)}, u32[]{:S(2)}, u32[]{:S(2)}) collective-permute-start(s16[264,128]{1,0:T(8,128)(2,1)S(1)} %get-tuple-element.40), channel_id=1, source_target_pairs={{0,24},{1,25},{2,26},{3,27},{4,28},{5,29},{6,30},{7,31},{8,16},{9,... | collective-permute-start | bytes 202760 | tf_op jit(solution)/shard_map/ppermute | solution.py:89
  40.8 4.6 %collective-permute-start.12 = (s16[136,128]{1,0:T(8,128)(2,1)S(1)}, s16[136,128]{1,0:T(8,128)(2,1)S(1)}, u32[]{:S(2)}, u32[]{:S(2)}) collective-permute-start(s16[136,128]{1,0:T(8,128)(2,1)S(1)} %get-tuple-element.47), channel_id=1, source_target_pairs={{0,3},{1,2},{2,1},{3,0},{4,7},{5,6},{6,5},{7,4},{8,11},{9,10},{10,... | collective-permute-start | bytes 104456 | tf_op jit(solution)/shard_map/ppermute | solution.py:89
  40.9 4.5 %collective-permute-start.13 = (s16[136,128]{1,0:T(8,128)(2,1)S(1)}, s16[136,128]{1,0:T(8,128)(2,1)S(1)}, u32[]{:S(2)}, u32[]{:S(2)}) collective-permute-start(s16[136,128]{1,0:T(8,128)(2,1)S(1)} %get-tuple-element.48), channel_id=1, source_target_pairs={{0,2},{1,3},{2,0},{3,1},{4,6},{5,7},{6,4},{7,5},{8,10},{9,11},{10,... | collective-permute-start | bytes 104456 | tf_op jit(solution)/shard_map/ppermute | solution.py:89
